TPU v7x, 512 devices: a whole 4x4x16 slice. The times are simulated.
512 devices in a mesh: shard: 128 (over y, z, core), rep: 4 (over x).
Axes of the slice: x: 4, y: 4, z: 16, core: 2. Of those that a mesh axis runs over, the one named last changes fastest.
Arguments:
- feature_table: bfloat16 [32768, 1024], P('shard'), may hold values from -8 to 8
- projection: bfloat16 [1024, 1024], replicated, may hold values from -0.1875 to 0.1875
- slot_owner: int32 [16384, 16, 1], P(('shard', 'rep')), may hold values from 0 to 127; in each aligned block of 512 rows (0 to 511, 512 to 1023, ..., all dimensions but the last counted through in order) at most 8 rows name the same one
- slot_row: int32 [16384, 16], P(('shard', 'rep')), may hold values from 0 to 255
- visits: int32 [16384, 13], P(('shard', 'rep')), may hold values from 1 to 32
- neg_row: int32 [512], P('shard'), may hold values from 0 to 255
Outputs:
- table_grad: float32 [32768, 1024], P('shard')
Inputs may be any that keep to these rules, and one draw needn't show every extreme that they name: `slot_owner`: within the slots of one device's 32 queries (aligned blocks of 512 slots in order), no shard index is named more than 8 times, a bound that some block reaches. `neg_row`: negative j lies in the rows of shard index j // 4.
All inputs are finite; a program needn't handle non-finite values.
Results may differ from a plain program's by a relative error of at most 0.006.
Values may be sent and summed in bfloat16 or wider, within the bound.
No kernel may reach another device: no remote copies, remote signals or barrier semaphores. Data moves between devices by JAX's collectives and lax.ppermute only.
A program may use at most 64 MiB of HBM per device.

v0:
```python
import jax
import jax.numpy as jnp
from jax import lax
from jax.sharding import PartitionSpec as P

score_scale = 8.0
margin_value = 0.1
epsilon = 1e-06


def unit_rows(values):
    norms = jnp.sqrt(jnp.sum(values * values, axis=-1, keepdims=True) + epsilon)
    return (values / norms, norms)


def unit_back(grads, unit, norms):
    return (grads - unit * jnp.sum(unit * grads, axis=-1, keepdims=True)) / norms


def silu_slope(preact):
    gate_value = jax.nn.sigmoid(preact)
    return gate_value * (1.0 + preact * (1.0 - gate_value))


def times_back(left, projection):
    return jnp.einsum("re,fe->rf", left, projection, preferred_element_type=jnp.float32)


def on_device(feature_table, projection, slot_owner, slot_row, visits, neg_row):
    shard_count = lax.axis_size("shard")
    query_count, slot_count = slot_row.shape
    row_count = query_count * slot_count
    capacity = 2 * row_count // shard_count
    feat_width = projection.shape[0]
    embed_width = projection.shape[1]
    owners = slot_owner.reshape(row_count)
    one_hot = (owners[:, None] == jnp.arange(shard_count, dtype=jnp.int32)[None, :]).astype(
        jnp.int32
    )
    earlier = jnp.cumsum(one_hot, axis=0) - one_hot
    slot_rank = jnp.sum(earlier * one_hot, axis=1)
    position = owners * capacity + slot_rank
    send_ids = (
        jnp.zeros((shard_count * capacity,), jnp.int32)
        .at[position]
        .set(slot_row.reshape(row_count))
    )
    send_ids = send_ids.reshape(shard_count, capacity)
    asked = lax.all_to_all(send_ids, "shard", split_axis=0, concat_axis=0, tiled=True)
    picked = feature_table[asked]
    fetched = lax.all_to_all(picked, "shard", split_axis=0, concat_axis=0, tiled=True)
    gathered = fetched.reshape(shard_count * capacity, feat_width)[position]
    neg_pre = jnp.dot(feature_table[neg_row], projection, preferred_element_type=jnp.float32)
    neg_unit, neg_norms = unit_rows(jax.nn.silu(neg_pre))
    neg_embed = lax.all_gather(neg_unit.astype(jnp.bfloat16), "shard", axis=0, tiled=True)
    visit_float = visits.astype(jnp.float32)
    coefs = visit_float / jnp.sum(visit_float, axis=1, keepdims=True)
    preact = jnp.dot(gathered, projection, preferred_element_type=jnp.float32).reshape(
        query_count, slot_count, embed_width
    )
    active = jax.nn.silu(preact)
    hood = active[:, 0] + jnp.einsum("bk,bke->be", coefs, active[:, 3:])
    query_unit, query_norms = unit_rows(hood)
    query_embed = query_unit.astype(jnp.bfloat16)
    item_unit, item_norms = unit_rows(active[:, 1:3])
    item_embed = item_unit.astype(jnp.bfloat16)
    query_float = query_embed.astype(jnp.float32)
    item_float = item_embed.astype(jnp.float32)
    neg_scores = jnp.einsum("be,ne->bn", query_embed, neg_embed, preferred_element_type=jnp.float32)
    pair_scores = jnp.sum(query_float[:, None, :] * item_float, axis=2)
    positive = pair_scores[:, 0:1]
    neg_weight = (
        score_scale * jax.nn.sigmoid(score_scale * (neg_scores - positive + margin_value))
    ).astype(jnp.bfloat16)
    hard_weight = (
        score_scale * jax.nn.sigmoid(score_scale * (pair_scores[:, 1:2] - positive + margin_value))
    ).astype(jnp.bfloat16)
    hard_float = hard_weight.astype(jnp.float32)
    total_weight = jnp.sum(neg_weight.astype(jnp.float32), axis=1, keepdims=True) + hard_float
    query_grad = (
        jnp.dot(neg_weight, neg_embed, preferred_element_type=jnp.float32)
        + hard_float * item_float[:, 1]
        - total_weight * item_float[:, 0]
    )
    item_grad = jnp.stack([-total_weight * query_float, hard_float * query_float], axis=1)
    neg_partial = jnp.einsum(
        "bn,be->ne", neg_weight, query_embed, preferred_element_type=jnp.float32
    )
    hood_grad = unit_back(query_grad, query_unit, query_norms)
    item_back = unit_back(item_grad, item_unit, item_norms)
    active_grad = jnp.concatenate(
        [hood_grad[:, None], item_back, coefs[:, :, None] * hood_grad[:, None]], axis=1
    )
    preact_grad = (
        (active_grad * silu_slope(preact)).astype(jnp.bfloat16).reshape(row_count, embed_width)
    )
    neg_count = neg_row.shape[0]
    row_grads = times_back(preact_grad, projection)
    outgoing = (
        jnp.zeros((shard_count * capacity, feat_width), jnp.float32).at[position].set(row_grads)
    )
    incoming, neg_pieces = (
        lax.all_to_all(
            outgoing.reshape(shard_count, capacity, feat_width),
            "shard",
            split_axis=0,
            concat_axis=0,
            tiled=True,
        ),
        lax.all_to_all(
            neg_partial.reshape(shard_count, neg_count, embed_width),
            "shard",
            split_axis=0,
            concat_axis=0,
            tiled=True,
        ),
    )
    contrib = incoming.reshape(shard_count * capacity, feat_width)
    neg_sum = jnp.sum(neg_pieces, axis=0)
    grad_local = (
        jnp.zeros((feature_table.shape[0], feat_width), jnp.float32)
        .at[asked.reshape(-1)]
        .add(contrib)
    )
    grad_local, neg_total = lax.psum((grad_local, neg_sum), "rep")
    neg_back = unit_back(neg_total, neg_unit, neg_norms)
    neg_pre_grad = (neg_back * silu_slope(neg_pre)).astype(jnp.bfloat16)
    neg_rows = times_back(neg_pre_grad, projection)
    return grad_local.at[neg_row].add(neg_rows)


def solution(mesh):
    return jax.shard_map(
        on_device,
        mesh=mesh,
        in_specs=(
            P("shard", None),
            P(),
            P(("shard", "rep"), None, None),
            P(("shard", "rep"), None),
            P(("shard", "rep"), None),
            P("shard"),
        ),
        out_specs=P("shard", None),
        check_vma=False,
    )
```

profile of v0, /device:TPU:40, one launch (start us, length us, event | category | flops | bytes accessed | tf_op | source)
XLA Modules:
  0.0 565.5 jit_solution(18394827955306807878)
XLA Ops:
  6.5 0.9 broadcast_multiply_fusion.1
  7.4 0.8 copy.24
  8.2 0.1 eq.29
  8.3 0.1 eq.25
  8.3 0.1 copy.23
  8.4 0.1 mul.161
  8.5 0.8 copy.28
  9.3 0.1 reshape.191
  9.4 0.1 copy.26
  9.5 0.2 fusion.23
  9.8 0.2 fusion.22
  10.0 2.4 scatter_custom_fusion
  12.5 0.1 all_to_all.17
  12.6 32.7 %all_to_all.27 = s32[128,1,8]{2,1,0:T(1,128)S(1)} all-to-all(s32[128,1,8]{2,1,0:T(1,128)S(1)} %bitcast.111), channel_id=1, replica_groups=mesh['shard'=128,'rep'=4] {'shard'}, dimensions={0} | all-to-all | bytes 8192 | tf_op jit(solution)/shard_map/all_to_all | solution.py:49
  45.3 0.1 reshape.165
  45.4 5.4 gather_fusion
  50.8 9.2 %all-to-all-start.1 = ((bf16[128,8,1024]{2,1,0:T(8,128)(2,1)}), bf16[128,8,1024]{2,1,0:T(8,128)(2,1)}, u32[]{:S(2)}, u32[]{:S(2)}) async-start(bf16[128,8,1024]{2,1,0:T(8,128)(2,1)} %bitcast.105), calls=%async_computation.1 | async-start | bytes 4194304 | tf_op jit(solution)/shard_map/all_to_all | solution.py:51
  60.0 0.2 all-gather.3.cloned.1.call-start
  60.3 0.6 gather_fusion.2
  60.9 0.5 multiply_reduce_fusion.6
  61.4 0.7 convert_bitcast_fusion
  62.1 0.0 all-gather.3.cloned.1.call-update
  62.2 0.1 copy.32
  62.3 0.1 copy.35
  62.4 139.4 %all-gather.3.cloned.1.call-done = bf16[128,4,1024]{2,1,0:T(4,128)(2,1)} async-done(((bf16[1,4,1024]{2,1,0:T(4,128)(2,1)}), bf16[128,4,1024]{2,1,0:T(4,128)(2,1)}) %all-gather.3.cloned.1.call-update) | async-done | bytes 1048592 | tf_op jit(solution)/shard_map/all_gather | solution.py:55
  201.8 1.3 reshape.223
  203.2 5.3 gather_fusion.1
  208.5 2.5 fusion.44
  211.0 1.4 divide_multiply_fusion
  212.3 0.1 multiply_reduce_fusion.1
  212.4 0.1 slice.44
  212.6 0.6 fusion.4
  213.2 0.1 multiply_reduce_fusion.4
  213.3 0.1 fusion.42
  213.4 0.2 convert_convert_fusion
  213.6 0.6 convert_reduce_fusion
  214.2 0.4 multiply_reduce_fusion.3
  214.6 0.1 subtract_divide_fusion
  214.7 0.1 copy.33
  214.9 0.1 multiply_bitcast_fusion.1
  215.0 0.2 fusion.10
  215.2 0.2 copy.34
  215.4 0.2 broadcast_multiply_fusion
  215.6 0.6 pad_maximum_fusion
  216.2 0.8 fusion.3
  216.9 2.6 fusion.45
  219.6 5.5 scatter_custom_fusion.1
  225.0 11.6 %all-to-all-start.2 = ((f32[128,8,1024]{2,1,0:T(8,128)}), f32[128,8,1024]{2,1,0:T(8,128)}, u32[]{:S(2)}, u32[]{:S(2)}) async-start(f32[128,8,1024]{2,1,0:T(8,128)} %bitcast.104), calls=%async_computation.2 | async-start | bytes 8388608 | tf_op jit(solution)/shard_map/all_to_all | solution.py:103
  236.6 1.7 fusion.46
  238.4 2.9 reshape.162
  241.3 184.3 %all-to-all-done.2 = f32[128,8,1024]{2,1,0:T(8,128)} async-done(((f32[128,8,1024]{2,1,0:T(8,128)}), f32[128,8,1024]{2,1,0:T(8,128)}, u32[]{:S(2)}, u32[]{:S(2)}) %all-to-all-start.2) | async-done | bytes 4194336 | tf_op jit(solution)/shard_map/all_to_all | solution.py:103
  425.6 8.8 %all-to-all-start.3 = ((f32[128,4,1024]{2,1,0:T(4,128)}), f32[128,4,1024]{2,1,0:T(4,128)}, u32[]{:S(2)}, u32[]{:S(2)}) async-start(f32[128,4,1024]{2,1,0:T(4,128)} %reshape.162), calls=%async_computation.3 | async-start | bytes 4194304 | tf_op jit(solution)/shard_map/all_to_all | solution.py:110
  434.4 0.0 all-reduce.2.cloned.1.call-start
  434.5 0.5 broadcast.171
  435.0 0.8 reduce.3
  435.8 0.1 reshape.157
  435.9 11.0 %scatter_custom_fusion.2 = f32[256,1024]{1,0:T(8,128)} fusion(s32[1024]{0:T(1024)S(1)} %bitcast.117, f32[128,8,1024]{2,1,0:T(8,128)} %all-to-all-done.2, f32[]{:T(128)} %constant.9.clone.1), kind=kCustom, calls=%fused_computation.8 | custom fusion | flops 1048576 | bytes 5242884 | tf_op jit(solution)/shard_map/scatter-add | solution.py:123
  447.0 86.9 %all-to-all-done.3 = f32[128,4,1024]{2,1,0:T(4,128)} async-done(((f32[128,4,1024]{2,1,0:T(4,128)}), f32[128,4,1024]{2,1,0:T(4,128)}, u32[]{:S(2)}, u32[]{:S(2)}) %all-to-all-start.3) | async-done | bytes 2097184 | tf_op jit(solution)/shard_map/all_to_all | solution.py:110
  533.9 1.9 reduce_sum.111
  535.9 16.9 %psum.15 = f32[4,1024]{1,0:T(4,128)S(1)} all-reduce(f32[4,1024]{1,0:T(4,128)S(1)} %reduce_sum.111), channel_id=1, replica_groups=mesh['shard'=128,'rep'=4] {'rep'}, use_global_device_ids=true, to_apply=%region_16.17 | all-reduce | flops 4096 | bytes 32768 | tf_op jit(solution)/shard_map/psum | solution.py:125
  552.7 0.2 multiply_reduce_fusion.5
  552.9 0.7 fusion.31
  553.6 2.8 scatter_fusion
  556.4 2.3 copy.49
  (34 shorter events, 0.3 us)
Async XLA Ops:
  6.5 54.4 %copy-start = (bf16[1024,1024]{1,0:T(8,128)(2,1)S(1)}, bf16[1024,1024]{1,0:T(8,128)(2,1)}, u32[]{:S(2)}) copy-start(bf16[1024,1024]{1,0:T(8,128)(2,1)} %param.7) | copy-start | bytes 6291460
  6.5 38.9 %copy-start.1 = (bf16[256,1024]{1,0:T(8,128)(2,1)S(1)}, bf16[256,1024]{1,0:T(8,128)(2,1)}, u32[]{:S(2)}) copy-start(bf16[256,1024]{1,0:T(8,128)(2,1)} %param.6) | copy-start | bytes 1572868
  50.8 9.5 %copy-start.3 = (s32[4]{0:T(128)S(1)}, s32[4]{0:T(128)}, u32[]{:S(2)}) copy-start(s32[4]{0:T(128)} %param.11) | copy-start | bytes 52
  50.8 152.3 %all-to-all-start.1 = ((bf16[128,8,1024]{2,1,0:T(8,128)(2,1)}), bf16[128,8,1024]{2,1,0:T(8,128)(2,1)}, u32[]{:S(2)}, u32[]{:S(2)}) async-start(bf16[128,8,1024]{2,1,0:T(8,128)(2,1)} %bitcast.105), calls=%async_computation.1 | async-start | bytes 4194304 | tf_op jit(solution)/shard_map/all_to_all | solution.py:51
  60.0 2.1 copy-start.2
  60.0 141.8 %all-gather.3.cloned.1.call-start = ((), (), s32[]{:S(2)}) async-start(), calls=%async_computation.5 | async-start | bytes 1056768 | tf_op jit(solution)/shard_map/all_gather | solution.py:55
  225.0 200.5 %all-to-all-start.2 = ((f32[128,8,1024]{2,1,0:T(8,128)}), f32[128,8,1024]{2,1,0:T(8,128)}, u32[]{:S(2)}, u32[]{:S(2)}) async-start(f32[128,8,1024]{2,1,0:T(8,128)} %bitcast.104), calls=%async_computation.2 | async-start | bytes 8388608 | tf_op jit(solution)/shard_map/all_to_all | solution.py:103
  425.6 108.3 %all-to-all-start.3 = ((f32[128,4,1024]{2,1,0:T(4,128)}), f32[128,4,1024]{2,1,0:T(4,128)}, u32[]{:S(2)}, u32[]{:S(2)}) async-start(f32[128,4,1024]{2,1,0:T(4,128)} %reshape.162), calls=%async_computation.3 | async-start | bytes 4194304 | tf_op jit(solution)/shard_map/all_to_all | solution.py:110
  434.4 119.1 %all-reduce.2.cloned.1.call-start = ((), (), s32[]{:S(2)}) async-start(), calls=%async_computation.4 | async-start | bytes 2097152 | tf_op jit(solution)/shard_map/psum | solution.py:125
Sparse Core Ops, SparseCore 0:
  63.8 137.9 all-gather.2
  447.1 62.4 all-reduce.1
where the time goes:
time: 566 us
  waiting for transfers between devices  411 us (73%)
  blocking collectives  49.6 us (9%)
  starting transfers between devices  29.9 us (5%)
  local copies, waits for them, and re-layouts  29.3 us (5%)
  other arithmetic  22.8 us (4%)
  between operations  13.7 us (2%)
  matrix products  9.57 us (2%)
    all_to_all x1, waiting for transfers between devices, on_device(): lax.all_to_all(outgoing.reshape(shard_count, capacity, feat_width), 'shar...  184 us
    all_gather x1, waiting for transfers between devices, on_device(): lax.all_gather(neg_unit.astype(jnp.bfloat16), 'shard', axis=0, tiled=True)  139 us
    all_to_all x1, waiting for transfers between devices, on_device(): lax.all_to_all(neg_partial.reshape(shard_count, neg_count, embed_width),...  86.9 us
    all_to_all x1, blocking collectives, on_device(): lax.all_to_all(send_ids, 'shard', split_axis=0, concat_axis=0, tiled=True)  32.7 us
    psum x1, blocking collectives, on_device(): grad_local, neg_total = lax.psum((grad_local, neg_sum), 'rep')  16.9 us
    all_to_all x1, starting transfers between devices, on_device(): lax.all_to_all(outgoing.reshape(shard_count, capacity, feat_width), 'shar...  11.6 us
  transfers between devices with their start and end apart: 5, of which 3 were waited for; matrix products, arithmetic and copies ran while one was open for 4% of the time, Pallas kernels for 0%

commit v1 on v0

v1 whole, which is shorter than its diff:
```python
import jax
import jax.numpy as jnp
from jax import lax
from jax.sharding import Mesh
from jax.sharding import PartitionSpec as P

score_scale = 8.0
margin_value = 0.1
epsilon = 1e-06

Y, Z, C, X = 4, 16, 2, 4
ROWS = 256
PART = ROWS // X
BLOCK = PART + 8
OWN = X * BLOCK
bf16 = jnp.bfloat16
f32 = jnp.float32


def unit_rows(values):
    norms = jnp.sqrt(jnp.sum(values * values, axis=-1, keepdims=True) + epsilon)
    return (values / norms, norms)


def unit_back(grads, unit, norms):
    return (grads - unit * jnp.sum(unit * grads, axis=-1, keepdims=True)) / norms


def silu_slope(preact):
    gate_value = jax.nn.sigmoid(preact)
    return gate_value * (1.0 + preact * (1.0 - gate_value))


def weigh(score, positive):
    return (score_scale * jax.nn.sigmoid(score_scale * (score - positive + margin_value))).astype(bf16)


def dot_f32(left, right, dims):
    return lax.dot_general(left, right, (dims, ((), ())), preferred_element_type=f32)


def decode(packed, z):
    owner = packed & 127
    row = (packed >> 7) & 255
    visits = (packed >> 15).astype(f32)
    coefs = visits / jnp.sum(visits, axis=1, keepdims=True)
    place = (row // PART) * BLOCK + row % PART
    here = ((owner // C) % Z) == z
    return owner // (C * Z), owner % C, place, here, coefs


def hot_rows(column, coefs, width):
    lanes = lax.broadcasted_iota(jnp.int32, (column.shape[0], width), 1)
    total = (column[:, 0:1] == lanes).astype(f32)
    for slot in range(3, column.shape[1]):
        total = total + jnp.where(column[:, slot : slot + 1] == lanes, coefs[:, slot : slot + 1], 0.0)
    first = (column[:, 1:2] == lanes).astype(bf16)
    second = (column[:, 2:3] == lanes).astype(bf16)
    return lax.optimization_barrier((total.astype(bf16), first, second))


def on_device(feature_table, projection, slot_owner, slot_row, visits, neg_row):
    y, z, c, x = (lax.axis_index(a) for a in ("y", "z", "c", "x"))
    query_count, slot_count = slot_row.shape
    feat_width, embed_width = projection.shape
    line_count = Z * query_count

    shifted = jnp.pad(visits, ((0, 0), (3, 0)))
    packed = slot_owner.reshape(query_count, slot_count) + slot_row * 128 + shifted * 32768

    rows = jnp.concatenate(
        [
            feature_table.reshape(X, PART, feat_width),
            feature_table[neg_row].reshape(X, 1, feat_width),
            jnp.zeros((X, BLOCK - PART - 1, feat_width), bf16),
        ],
        axis=1,
    ).reshape(OWN, feat_width)
    pre = jnp.dot(rows, projection, preferred_element_type=f32)
    act = jax.nn.silu(pre)
    act_norm = jnp.sqrt(jnp.sum(act * act, axis=1, keepdims=True) + epsilon)
    is_neg = (lax.broadcasted_iota(jnp.int32, (OWN, 1), 0) % BLOCK) == PART
    shared = (act / jnp.where(is_neg, act_norm, 1.0)).astype(bf16)
    plane = lax.all_gather(shared, ("y", "c"), axis=0, tiled=True)

    line = lax.all_gather(packed, "z", axis=0, tiled=True)
    line_sib = lax.ppermute(line, "c", [(0, 1), (1, 0)])
    ny, nc, place, here, coefs = decode(line, z)
    column = jnp.where(here, (ny * C + nc) * OWN + place, -1)
    hood_w, first, second = hot_rows(column, coefs, Y * C * OWN)

    def fold(v):
        return v.reshape(Z, query_count, v.shape[-1])

    spread = jnp.stack([fold(hood_w), fold(first), fold(second)], axis=1).reshape(3 * line_count, -1)
    part = jnp.dot(spread, plane, preferred_element_type=f32).astype(bf16)
    got = lax.psum_scatter(part, "z", scatter_dimension=0, tiled=True)

    plane_neg = plane.reshape(Y, C, X, BLOCK, embed_width)[:, :, :, PART]
    half_neg = lax.dynamic_index_in_dim(plane_neg, c, axis=1, keepdims=False).reshape(Y * X, embed_width)
    some_neg = lax.all_gather(half_neg, "z", axis=0, tiled=True)
    other_neg = lax.ppermute(some_neg, "c", [(0, 1), (1, 0)])
    neg_embed = jnp.concatenate([some_neg, other_neg], axis=0)

    got = got.astype(f32)
    hood = got[:query_count]
    items = jnp.stack([got[query_count : 2 * query_count], got[2 * query_count :]], axis=1)
    query_unit, query_norms = unit_rows(hood)
    query_embed = query_unit.astype(bf16)
    item_unit, item_norms = unit_rows(items)
    query_float = query_embed.astype(f32)
    item_float = item_unit.astype(bf16).astype(f32)
    neg_scores = dot_f32(query_embed, neg_embed, ((1,), (1,)))
    pair_scores = jnp.sum(query_float[:, None, :] * item_float, axis=2)
    positive = pair_scores[:, 0:1]
    neg_weight = weigh(neg_scores, positive)
    hard_float = weigh(pair_scores[:, 1:2], positive).astype(f32)
    total_weight = jnp.sum(neg_weight.astype(f32), axis=1, keepdims=True) + hard_float
    query_grad = (
        jnp.dot(neg_weight, neg_embed, preferred_element_type=f32)
        + hard_float * item_float[:, 1]
        - total_weight * item_float[:, 0]
    )
    hood_grad = unit_back(query_grad, query_unit, query_norms).astype(bf16)
    item_weight = jnp.concatenate([-total_weight, hard_float], axis=1)
    overlap = jnp.sum(query_float[:, None, :] * item_unit, axis=2)
    on_query = item_weight / item_norms[:, :, 0]
    on_act = -item_weight * overlap / (item_norms[:, :, 0] * item_norms[:, :, 0])
    scalars = jnp.concatenate([on_query, on_act, positive, jnp.zeros((query_count, 3), f32)], axis=1)

    vectors = lax.all_gather(jnp.concatenate([hood_grad, query_embed], axis=0), "z", axis=0, tiled=True)
    scal = lax.all_gather(scalars, "z", axis=0, tiled=True)
    scal_sib = lax.ppermute(scal, "c", [(0, 1), (1, 0)])
    vectors_sib = lax.ppermute(vectors, "c", [(0, 1), (1, 0)])

    core_plane = lax.dynamic_index_in_dim(plane.reshape(Y, C, OWN, embed_width), c, axis=1, keepdims=False)
    core_plane = core_plane.reshape(Y * OWN, embed_width)
    core_neg = half_neg
    width = Y * OWN
    neg_spot = (
        lax.broadcasted_iota(jnp.int32, (Y * X, width), 0) * BLOCK + PART
        == lax.broadcasted_iota(jnp.int32, (Y * X, width), 1)
    ).astype(bf16)

    def to_nodes(packed_line, vecs, scals):
        ly, lc, lplace, lhere, lcoefs = decode(packed_line, z)
        lcolumn = jnp.where(lhere & (lc == c), ly * OWN + lplace, -1)
        w_hood, w_first, w_second = hot_rows(lcolumn, lcoefs, width)
        scores = dot_f32(vecs, core_neg, ((1,), (1,))).reshape(Z, 2, query_count, Y * X)[:, 1]
        neg_w = weigh(scores.reshape(line_count, Y * X), scals[:, 4:5])
        w_query = (
            w_first.astype(f32) * scals[:, 0:1]
            + w_second.astype(f32) * scals[:, 1:2]
            + jnp.dot(neg_w, neg_spot, preferred_element_type=f32)
        ).astype(bf16)
        both = jnp.stack([fold(w_hood), fold(w_query)], axis=1).reshape(2 * line_count, width)
        grads = dot_f32(both, vecs, ((0,), (0,)))
        on_acts = dot_f32(w_first, scals[:, 2:3].astype(bf16), ((0,), (0,))) + dot_f32(
            w_second, scals[:, 3:4].astype(bf16), ((0,), (0,))
        )
        return grads, on_acts

    grads, on_acts = to_nodes(line, vectors, scal)
    grads_sib, on_acts_sib = to_nodes(line_sib, vectors_sib, scal_sib)
    node_grads = grads + grads_sib + (on_acts + on_acts_sib) * core_plane.astype(f32)

    pieces = lax.all_to_all(node_grads.astype(bf16), ("y", "x"), split_axis=0, concat_axis=0, tiled=True)
    mine = jnp.sum(pieces.reshape(Y * X, BLOCK, embed_width).astype(f32), axis=0)
    my_pre = lax.dynamic_slice_in_dim(pre, x * BLOCK, BLOCK, axis=0)
    my_unit, my_norms = unit_rows(jax.nn.silu(my_pre))
    row_is_neg = lax.broadcasted_iota(jnp.int32, (BLOCK, 1), 0) == PART
    mine = jnp.where(row_is_neg, unit_back(mine, my_unit, my_norms), mine)
    pre_grad = (mine * silu_slope(my_pre)).astype(bf16)
    all_pre_grad = lax.all_gather(pre_grad, "x", axis=0, tiled=True)
    out = dot_f32(all_pre_grad, projection, ((1,), (1,))).reshape(X, BLOCK, feat_width)
    result = out[:, :PART].reshape(ROWS, feat_width)
    row_ids = lax.broadcasted_iota(jnp.int32, (ROWS, 1), 0)
    for i in range(X):
        result = result + jnp.where(row_ids == neg_row[i], out[i, PART][None, :], 0.0)
    return result


def solution(mesh):
    grid = Mesh(mesh.devices.reshape(Y, Z, C, X), ("y", "z", "c", "x"))
    shard = ("y", "z", "c")
    every = ("y", "z", "c", "x")
    return jax.shard_map(
        on_device,
        mesh=grid,
        in_specs=(
            P(shard, None),
            P(),
            P(every, None, None),
            P(every, None),
            P(every, None),
            P(shard),
        ),
        out_specs=P(shard, None),
        check_vma=False,
    )
```

time: 566 us -> 321 us (0.57)
  the two profiles are of different devices: /device:TPU:40 before, /device:TPU:32 now
where the time goes in v1:
time: 321 us; the launch traced here: 320 us
  blocking collectives  109 us (34%)
  waiting for transfers between devices  91.5 us (29%)
  other arithmetic  41.7 us (13%)
  matrix products  37.5 us (12%)
  starting transfers between devices  14.9 us (5%)
  between operations  13.7 us (4%)
  local copies, waits for them, and re-layouts  12.1 us (4%)
    all_gather x1, blocking collectives, on_device(): some_neg = lax.all_gather(half_neg, 'z', axis=0, tiled=True)  34 us
    all_gather x1, blocking collectives, on_device(): line = lax.all_gather(packed, 'z', axis=0, tiled=True)  34 us
    all_to_all x1, waiting for transfers between devices, on_device(): lax.all_to_all(node_grads.astype(bf16), ('y', 'x'), split_axis=0, concat_...  33.9 us
    reduce_scatter x1, waiting for transfers between devices, on_device(): got = lax.psum_scatter(part, 'z', scatter_dimension=0, tiled=True)  28.2 us
    all_gather x1, blocking collectives, on_device(): scal = lax.all_gather(scalars, 'z', axis=0, tiled=True)  27.8 us
    all_gather x1, waiting for transfers between devices, on_device(): lax.all_gather(jnp.concatenate([hood_grad, query_embed], axis=0), 'z', ax...  27.6 us
    convert_element_type x3, other arithmetic, hot_rows(): return lax.optimization_barrier((total.astype(bf16), first, second))  20.6 us
    dot_general x8, matrix products, dot_f32(): lax.dot_general(left, right, (dims, ((), ())), preferred_element_type=f32)  15.6 us
  transfers between devices with their start and end apart: 8, of which 4 were waited for; matrix products, arithmetic and copies ran while one was open for 16% of the time, Pallas kernels for 0%

profile of v1, /device:TPU:32, one launch (start us, length us, event | category | flops | bytes accessed | tf_op | source)
XLA Modules:
  0.0 320.3 jit_solution(16707698653182494376)
XLA Ops:
  6.5 0.8 compare_select_fusion
  7.4 1.7 gather_fusion
  9.1 1.2 maximum_maximum_fusion
  10.4 1.0 multiply_reduce_fusion
  11.4 1.0 copy-done.6
  12.4 1.2 divide_convert_fusion
  13.8 34.0 %all-gather = s32[16,32,16]{1,2,0:T(8,128)S(1)} all-gather(s32[1,32,16]{1,2,0:T(8,128)S(1)} %add_bitcast_fusion), channel_id=1, replica_groups=mesh['y'=4,'z'=16,'c'=2,'x'=4] {'z'}, dimensions={0}, use_global_device_ids=true | all-gather | bytes 34816 | tf_op jit(solution)/shard_map/all_gather | solution.py:86
  47.8 0.1 reshape.175
  47.9 0.1 add_select_fusion.12
  48.1 0.8 fusion.2
  48.9 9.8 %add_convert_fusion = bf16[512,2304]{1,0:T(8,128)(2,1)S(1)} fusion(f32[512]{0:T(512)S(1)} %bitcast.216, s32[512]{0:T(512)S(1)} %bitcast.292, f32[512]{0:T(512)S(1)} %bitcast.218, s32[512]{0:T(512)S(1)} %bitcast.293, f32[512]{0:T(512)S(1)} %bitcast.220, s32[512]{0:T(512)S(1)} %bitcast.294, f32[512]{0:T(512)S(1)} %bitcast.222, s32[512]{0:T(512)S(1)} %bitcast.295, ...), kind=kLoop, calls=%fused_computation.8 | loop fusion | flops 49545216 | bytes 2414592 | tf_op jit(solution)/shard_map/convert_element_type | solution.py:59
  58.7 3.5 %pad_maximum_fusion = bf16[16,3,32,2304]{3,2,1,0:T(8,128)(2,1)} fusion(bf16[16,1,32,2304]{3,2,1,0:T(8,128)(2,1)S(1)} %bitcast.196, bf16[16,1,32,2304]{3,2,1,0:T(8,128)(2,1)S(1)} %bitcast.195, bf16[16,1,32,2304]{3,2,1,0:T(8,128)(2,1)S(1)} %bitcast.194), kind=kLoop, calls=%fused_computation.1 | loop fusion | flops 7077888 | bytes 14155776 | tf_op jit(solution)/shard_map/stack | solution.py:95
  62.2 12.2 %convolution_convert_fusion = bf16[1536,1024]{1,0:T(8,128)(2,1)} fusion(bf16[1536,2304]{1,0:T(8,128)(2,1)} %bitcast.197, bf16[2304,1024]{1,0:T(8,128)(2,1)} %all-gather.5.cloned.1.call-done), kind=kOutput, calls=%fused_computation.25 | convolution fusion | flops 7249330176 | bytes 14942208 | tf_op jit(solution)/shard_map/dot_general | solution.py:96
  74.4 1.9 collective-permute-start.1
  76.4 1.8 fusion.5
  78.3 5.4 %add_convert_fusion.3 = bf16[512,1152]{1,0:T(8,128)(2,1)} fusion(f32[512]{0:T(512)S(1)} %bitcast.217, s32[512]{0:T(512)S(1)} %bitcast.258, f32[512]{0:T(512)S(1)} %bitcast.219, s32[512]{0:T(512)S(1)} %bitcast.259, f32[512]{0:T(512)S(1)} %bitcast.221, s32[512]{0:T(512)S(1)} %bitcast.260, f32[512]{0:T(512)S(1)} %bitcast.223, s32[512]{0:T(512)S(1)} %bitcast.261, ...), kind=kLoop, calls=%fused_computation.50 | loop fusion | flops 24772608 | bytes 1234944 | tf_op jit(solution)/shard_map/convert_element_type | solution.py:59
  83.8 1.1 slice.477
  85.1 34.0 %all_gather.20 = bf16[256,1024]{1,0:T(8,128)(2,1)S(1)} all-gather(bf16[16,1024]{1,0:T(8,128)(2,1)S(1)} %reshape.154), channel_id=1, replica_groups=mesh['y'=4,'z'=16,'c'=2,'x'=4] {'z'}, dimensions={0}, use_global_device_ids=true | all-gather | bytes 557056 | tf_op jit(solution)/shard_map/all_gather | solution.py:101
  119.1 1.9 collective-permute-start
  121.2 1.7 collective-permute-done
  122.9 28.2 %reduce-scatter.2.cloned.1.call-done = bf16[96,1024]{1,0:T(8,128)(2,1)} async-done(((bf16[1536,1024]{1,0:T(8,128)(2,1)}), bf16[96,1024]{1,0:T(8,128)(2,1)}) %reduce-scatter.2.cloned.1.call-update) | async-done | bytes 196624 | tf_op jit(solution)/shard_map/reduce_scatter | solution.py:97
  151.1 1.0 convert_element_type.135
  152.0 0.1 multiply_reduce_fusion.7
  152.4 0.2 multiply_reduce_fusion.3
  152.6 0.6 convert_reduce_fusion.1
  153.2 0.4 multiply_reduce_fusion.6
  153.6 0.1 divide_convert_fusion.1
  153.7 0.7 pad_maximum_fusion.4
  154.5 1.8 fusion.7
  156.3 5.4 %add_convert_fusion.2 = bf16[512,1152]{1,0:T(8,128)(2,1)} fusion(f32[512]{0:T(512)S(1)} %bitcast.279, s32[512]{0:T(512)S(1)} %bitcast.244, f32[512]{0:T(512)S(1)} %bitcast.280, s32[512]{0:T(512)S(1)} %bitcast.245, f32[512]{0:T(512)S(1)} %bitcast.281, s32[512]{0:T(512)S(1)} %bitcast.246, f32[512]{0:T(512)S(1)} %bitcast.282, s32[512]{0:T(512)S(1)} %bitcast.247, ...), kind=kLoop, calls=%fused_computation.33 | loop fusion | flops 24772608 | bytes 1234944 | tf_op jit(solution)/shard_map/convert_element_type | solution.py:59
  161.7 3.4 %constant_dynamic-slice_fusion = bf16[4,1,288,1024]{3,2,1,0:T(8,128)(2,1)} fusion(bf16[4,2,288,1024]{3,2,1,0:T(8,128)(2,1)} %bitcast.206, s32[]{:T(128)S(6)} %select_n.271), kind=kLoop, calls=%fused_computation.229 | loop fusion | bytes 4718596 | tf_op jit(solution)/shard_map/jit(dynamic_index_in_dim)/dynamic_slice | solution.py:136
  165.2 27.8 %all-gather.1 = f32[16,32,8]{1,2,0:T(8,128)S(1)} all-gather(f32[1,32,8]{1,2,0:T(8,128)S(1)} %maximum_bitcast_fusion), channel_id=1, replica_groups=mesh['y'=4,'z'=16,'c'=2,'x'=4] {'z'}, dimensions={0}, use_global_device_ids=true | all-gather | bytes 17408 | tf_op jit(solution)/shard_map/all_gather | solution.py:132
  193.1 2.1 collective-permute-start.2
  195.2 1.5 convolution_reduce_fusion.2
  196.8 0.3 convolution_reduce_fusion.3
  197.1 0.3 convolution_reduce_fusion
  197.4 27.6 %all-gather.7.cloned.1.call-done = bf16[1024,1024]{1,0:T(8,128)(2,1)} async-done(((bf16[64,1024]{1,0:T(8,128)(2,1)}), bf16[1024,1024]{1,0:T(8,128)(2,1)}) %all-gather.7.cloned.1.call-update) | async-done | bytes 2097168 | tf_op jit(solution)/shard_map/all_gather | solution.py:131
  225.0 2.1 collective-permute-start.3
  227.1 1.5 convolution_reduce_fusion.1
  228.7 2.0 fusion.44
  230.8 0.1 reshape_squeeze.6
  230.9 2.0 fusion.4
  232.9 0.2 pad_maximum_fusion.1
  233.2 1.3 copy-done.9
  234.5 4.3 %fusion.95 = f32[1152,1024]{1,0:T(8,128)} fusion(bf16[1024,1152]{1,0:T(8,128)(2,1)S(1)} %bitcast.203, bf16[1024,1024]{1,0:T(8,128)(2,1)S(1)} %copy-done.9), kind=kOutput, calls=%fused_computation.258 | convolution fusion | flops 2415919104 | bytes 9175040 | tf_op jit(solution)/shard_map/dot_general | solution.py:39
  238.9 2.1 fusion.42
  241.0 0.1 reshape_squeeze.7
  241.2 2.1 add_convert_fusion.1
  243.3 0.2 pad_maximum_fusion.2
  243.5 0.7 copy-done.14
  244.2 1.0 copy-done.8
  245.2 6.3 %fusion.1 = bf16[1152,1024]{1,0:T(8,128)(2,1)} fusion(bf16[1152,1024]{1,0:T(8,128)(2,1)S(1)} %bitcast.200, f32[1152,1024]{1,0:T(8,128)S(1)} %copy-done.14, bf16[1024,1152]{1,0:T(8,128)(2,1)S(1)} %bitcast.202, bf16[1024,1024]{1,0:T(8,128)(2,1)} %collective-permute-done.3, f32[1152]{0:T(1024)S(1)} %add_add_fusion), kind=kOutput, calls=%fused_computation.4 | convolution fusion | flops 2421817344 | bytes 13898240 | tf_op jit(solution)/shard_map/dot_general | solution.py:39
  251.4 6.9 %all-to-all-start = ((bf16[16,72,1024]{2,1,0:T(8,128)(2,1)}), bf16[16,72,1024]{2,1,0:T(8,128)(2,1)}, u32[]{:S(2)}, u32[]{:S(2)}) async-start(bf16[16,72,1024]{2,1,0:T(8,128)(2,1)} %bitcast.201), calls=%async_computation.1 | async-start | bytes 4718592 | tf_op jit(solution)/shard_map/all_to_all | solution.py:167
  258.3 0.2 multiply_reduce_fusion.2
  258.6 0.6 fusion.94
  259.2 1.2 iota_compare_fusion.53
  260.4 1.3 iota_compare_fusion.55
  261.7 33.9 %all-to-all-done = bf16[16,72,1024]{2,1,0:T(8,128)(2,1)} async-done(((bf16[16,72,1024]{2,1,0:T(8,128)(2,1)}), bf16[16,72,1024]{2,1,0:T(8,128)(2,1)}, u32[]{:S(2)}, u32[]{:S(2)}) %all-to-all-start) | async-done | bytes 2359328 | tf_op jit(solution)/shard_map/all_to_all | solution.py:167
  295.7 2.2 convert_reduce_fusion
  297.9 0.2 multiply_reduce_fusion.1
  298.1 0.2 multiply_convert_fusion
  298.3 13.1 %all_gather.23 = bf16[288,1024]{1,0:T(8,128)(2,1)S(1)} all-gather(bf16[72,1024]{1,0:T(8,128)(2,1)S(1)} %multiply_convert_fusion), channel_id=1, replica_groups=mesh['y'=4,'z'=16,'c'=2,'x'=4] {'x'}, dimensions={0}, use_global_device_ids=true | all-gather | bytes 737280 | tf_op jit(solution)/shard_map/all_gather | solution.py:174
  311.4 0.8 fusion.96
  312.4 1.4 fusion.20
  (84 shorter events, 1.6 us)
Async XLA Ops:
  6.5 3.8 %copy-start = (bf16[1024,1024]{1,0:T(8,128)(2,1)S(1)}, bf16[1024,1024]{1,0:T(8,128)(2,1)}, u32[]{:S(2)}) copy-start(bf16[1024,1024]{1,0:T(8,128)(2,1)} %param.7) | copy-start | bytes 6291460
  6.5 55.6 %all-gather.5.cloned.1.call-start = ((), (), s32[]{:S(2)}) async-start(), calls=%async_computation.2 | async-start | bytes 5308416 | tf_op jit(solution)/shard_map/all_gather | solution.py:84
  11.4 1.1 copy-start.6
  11.4 2.3 copy-start.11
  11.4 2.3 copy-start.12
  11.4 2.3 copy-start.13
  13.7 137.4 %reduce-scatter.2.cloned.1.call-start = ((), (), s32[]{:S(2)}) async-start(), calls=%async_computation.3 | async-start | bytes 3342336 | tf_op jit(solution)/shard_map/reduce_scatter | solution.py:97
  74.4 150.6 %all-gather.7.cloned.1.call-start = ((), (), s32[]{:S(2)}) async-start(), calls=%async_computation.4 | async-start | bytes 2228224 | tf_op jit(solution)/shard_map/all_gather | solution.py:131
  74.4 9.3 %collective-permute-start.1 = (s32[512,16]{0,1:T(8,128)S(1)}, s32[512,16]{0,1:T(8,128)S(1)}, u32[]{:S(2)}, u32[]{:S(2)}) collective-permute-start(s32[512,16]{0,1:T(8,128)S(1)} %reshape.175), channel_id=1, source_target_pairs={{0,4},{4,0},{1,5},{5,1},{2,6},{6,2},{3,7},{7,3},{8,12},{12,8},{9,1... | collective-permute-start | bytes 98312 | tf_op jit(solution)/shard_map/ppermute | solution.py:87
  119.1 3.8 %collective-permute-start = (bf16[256,1024]{1,0:T(8,128)(2,1)S(1)}, bf16[256,1024]{1,0:T(8,128)(2,1)S(1)}, u32[]{:S(2)}, u32[]{:S(2)}) collective-permute-start(bf16[256,1024]{1,0:T(8,128)(2,1)S(1)} %all_gather.20), channel_id=1, source_target_pairs={{0,4},{4,0},{1,5},{5,1},{2,6},{6,2},{3,7},{7,3},{8,12},{12,8},{9,1... | collective-permute-start | bytes 1572872 | tf_op jit(solution)/shard_map/ppermute | solution.py:102
  161.7 35.0 %copy-start.1 = (bf16[512,1152]{1,0:T(8,128)(2,1)S(1)}, bf16[512,1152]{1,0:T(8,128)(2,1)}, u32[]{:S(2)}) copy-start(bf16[512,1152]{1,0:T(8,128)(2,1)} %get-tuple-element.15) | copy-start | bytes 3538948
  193.1 4.0 %copy-start.3 = (bf16[512,1152]{1,0:T(8,128)(2,1)S(1)}, bf16[512,1152]{1,0:T(8,128)(2,1)}, u32[]{:S(2)}) copy-start(bf16[512,1152]{1,0:T(8,128)(2,1)} %get-tuple-element.22) | copy-start | bytes 3538948
  193.1 3.9 %collective-permute-start.2 = (f32[512,8]{0,1:T(8,128)S(1)}, f32[512,8]{0,1:T(8,128)S(1)}, u32[]{:S(2)}, u32[]{:S(2)}) collective-permute-start(f32[512,8]{0,1:T(8,128)S(1)} %reshape.177), channel_id=1, source_target_pairs={{0,4},{4,0},{1,5},{5,1},{2,6},{6,2},{3,7},{7,3},{8,12},{12,8},{9,1... | collective-permute-start | bytes 49160 | tf_op jit(solution)/shard_map/ppermute | solution.py:133
  225.0 13.9 %collective-permute-start.3 = (bf16[1024,1024]{1,0:T(8,128)(2,1)}, bf16[1024,1024]{1,0:T(8,128)(2,1)}, u32[]{:S(2)}, u32[]{:S(2)}) collective-permute-start(bf16[1024,1024]{1,0:T(8,128)(2,1)} %all-gather.7.cloned.1.call-done), channel_id=1, source_target_pairs={{0,4},{4,0},{1,5},{5,1},{2,6},{6,2},{3,7},{7,3},{8,12},{12,8},{9,1... | collective-permute-start | bytes 6291464 | tf_op jit(solution)/shard_map/ppermute | solution.py:134
  230.9 2.1 copy-start.4
  232.9 1.6 copy-start.9
  238.8 2.3 copy-start.2
  241.1 2.1 copy-start.5
  241.1 3.0 copy-start.14
  243.3 1.9 copy-start.8
  251.4 6.9 %copy-start.7 = (f32[288,1024]{1,0:T(8,128)S(1)}, f32[288,1024]{1,0:T(8,128)}, u32[]{:S(2)}) copy-start(f32[288,1024]{1,0:T(8,128)} %copy-done.6) | copy-start | bytes 3538948
  251.4 7.1 %copy-start.10 = (s32[4]{0:T(128)S(1)}, s32[4]{0:T(128)}, u32[]{:S(2)}) copy-start(s32[4]{0:T(128)} %param.11) | copy-start | bytes 52
  251.4 44.3 %all-to-all-start = ((bf16[16,72,1024]{2,1,0:T(8,128)(2,1)}), bf16[16,72,1024]{2,1,0:T(8,128)(2,1)}, u32[]{:S(2)}, u32[]{:S(2)}) async-start(bf16[16,72,1024]{2,1,0:T(8,128)(2,1)} %bitcast.201), calls=%async_computation.1 | async-start | bytes 4718592 | tf_op jit(solution)/shard_map/all_to_all | solution.py:167
Sparse Core Ops, SparseCore 0:
  13.8 46.0 all-gather.4
  74.5 76.5 reduce-scatter.1
  154.5 70.4 all-gather.6

commit v2 on v1

--- a/solution.py
+++ b/solution.py
@@ -14,6 +14,7 @@
 BLOCK = PART + 8
 OWN = X * BLOCK
 bf16 = jnp.bfloat16
+f16 = jnp.float16
 f32 = jnp.float32
 
 
@@ -101,6 +102,24 @@
     some_neg = lax.all_gather(half_neg, "z", axis=0, tiled=True)
     other_neg = lax.ppermute(some_neg, "c", [(0, 1), (1, 0)])
     neg_embed = jnp.concatenate([some_neg, other_neg], axis=0)
+
+    width = Y * OWN
+    core_plane = lax.dynamic_index_in_dim(plane.reshape(Y, C, OWN, embed_width), c, axis=1, keepdims=False)
+    core_plane = core_plane.reshape(width, embed_width)
+    core_is_neg = (lax.broadcasted_iota(jnp.int32, (width, 1), 0) % BLOCK) == PART
+    neg_spot = (
+        lax.broadcasted_iota(jnp.int32, (Y * X, width), 0) * BLOCK + PART
+        == lax.broadcasted_iota(jnp.int32, (Y * X, width), 1)
+    ).astype(bf16)
+
+    def core_rows(packed_line):
+        ly, lc, lplace, lhere, lcoefs = decode(packed_line, z)
+        return hot_rows(jnp.where(lhere & (lc == c), ly * OWN + lplace, -1), lcoefs, width)
+
+    weights, weights_sib = core_rows(line), core_rows(line_sib)
+    got, weights, weights_sib, core_plane, neg_embed = lax.optimization_barrier(
+        (got, weights, weights_sib, core_plane, neg_embed)
+    )
 
     got = got.astype(f32)
     hood = got[:query_count]
@@ -121,56 +140,66 @@
         + hard_float * item_float[:, 1]
         - total_weight * item_float[:, 0]
     )
-    hood_grad = unit_back(query_grad, query_unit, query_norms).astype(bf16)
-    item_weight = jnp.concatenate([-total_weight, hard_float], axis=1)
-    overlap = jnp.sum(query_float[:, None, :] * item_unit, axis=2)
-    on_query = item_weight / item_norms[:, :, 0]
-    on_act = -item_weight * overlap / (item_norms[:, :, 0] * item_norms[:, :, 0])
-    scalars = jnp.concatenate([on_query, on_act, positive, jnp.zeros((query_count, 3), f32)], axis=1)
-
-    vectors = lax.all_gather(jnp.concatenate([hood_grad, query_embed], axis=0), "z", axis=0, tiled=True)
-    scal = lax.all_gather(scalars, "z", axis=0, tiled=True)
-    scal_sib = lax.ppermute(scal, "c", [(0, 1), (1, 0)])
+    query_grad = query_grad - query_unit * jnp.sum(query_unit * query_grad, axis=1, keepdims=True)
+    lead = positive.astype(f16)
+    scalars = jnp.concatenate(
+        [
+            -total_weight,
+            hard_float,
+            item_norms[:, :, 0],
+            query_norms * 0.25,
+            lead.astype(f32),
+            positive - lead.astype(f32),
+            jnp.zeros((query_count, 121), f32),
+        ],
+        axis=1,
+    )
+    payload = jnp.concatenate([query_grad, query_float, scalars], axis=1).astype(f16)
+    vectors = lax.all_gather(payload, "z", axis=0, tiled=True)
     vectors_sib = lax.ppermute(vectors, "c", [(0, 1), (1, 0)])
 
-    core_plane = lax.dynamic_index_in_dim(plane.reshape(Y, C, OWN, embed_width), c, axis=1, keepdims=False)
-    core_plane = core_plane.reshape(Y * OWN, embed_width)
-    core_neg = half_neg
-    width = Y * OWN
-    neg_spot = (
-        lax.broadcasted_iota(jnp.int32, (Y * X, width), 0) * BLOCK + PART
-        == lax.broadcasted_iota(jnp.int32, (Y * X, width), 1)
-    ).astype(bf16)
-
-    def to_nodes(packed_line, vecs, scals):
-        ly, lc, lplace, lhere, lcoefs = decode(packed_line, z)
-        lcolumn = jnp.where(lhere & (lc == c), ly * OWN + lplace, -1)
-        w_hood, w_first, w_second = hot_rows(lcolumn, lcoefs, width)
-        scores = dot_f32(vecs, core_neg, ((1,), (1,))).reshape(Z, 2, query_count, Y * X)[:, 1]
-        neg_w = weigh(scores.reshape(line_count, Y * X), scals[:, 4:5])
+    def unpack(vecs):
+        scals = vecs[:, 2 * embed_width :].astype(f32)
+        grads = (vecs[:, :embed_width].astype(f32) / (4.0 * scals[:, 4:5])).astype(bf16)
+        embeds = vecs[:, embed_width : 2 * embed_width].astype(bf16)
+        on_first = scals[:, 0:1] / scals[:, 2:3]
+        on_second = scals[:, 1:2] / scals[:, 3:4]
+        pos = scals[:, 5:6] + scals[:, 6:7]
+        return lax.optimization_barrier((grads, embeds, jnp.concatenate([on_first, on_second, pos], axis=1)))
+
+    def to_nodes(weights, received):
+        w_hood, w_first, w_second = weights
+        grads, embeds, scals = received
+        scores = dot_f32(embeds, half_neg, ((1,), (1,)))
+        neg_w = weigh(scores, scals[:, 2:3])
         w_query = (
             w_first.astype(f32) * scals[:, 0:1]
             + w_second.astype(f32) * scals[:, 1:2]
             + jnp.dot(neg_w, neg_spot, preferred_element_type=f32)
         ).astype(bf16)
-        both = jnp.stack([fold(w_hood), fold(w_query)], axis=1).reshape(2 * line_count, width)
-        grads = dot_f32(both, vecs, ((0,), (0,)))
-        on_acts = dot_f32(w_first, scals[:, 2:3].astype(bf16), ((0,), (0,))) + dot_f32(
-            w_second, scals[:, 3:4].astype(bf16), ((0,), (0,))
-        )
-        return grads, on_acts
-
-    grads, on_acts = to_nodes(line, vectors, scal)
-    grads_sib, on_acts_sib = to_nodes(line_sib, vectors_sib, scal_sib)
-    node_grads = grads + grads_sib + (on_acts + on_acts_sib) * core_plane.astype(f32)
-
-    pieces = lax.all_to_all(node_grads.astype(bf16), ("y", "x"), split_axis=0, concat_axis=0, tiled=True)
-    mine = jnp.sum(pieces.reshape(Y * X, BLOCK, embed_width).astype(f32), axis=0)
+        return dot_f32(w_hood, grads, ((0,), (0,))), dot_f32(w_query, embeds, ((0,), (0,)))
+
+    own = unpack(vectors)
+    hood_part, query_part = to_nodes(weights, own)
+    hood_sib, query_sib = to_nodes(weights_sib, unpack(vectors_sib))
+    query_part = query_part + query_sib
+    core_float = core_plane.astype(f32)
+    core_square = jnp.where(core_is_neg, 0.0, 1.0 / (jnp.sum(core_float * core_float, axis=1, keepdims=True) + epsilon))
+    query_part = query_part - core_float * (core_square * jnp.sum(core_float * query_part, axis=1, keepdims=True))
+    node_grads = (hood_part + hood_sib + query_part).astype(bf16)
+
     my_pre = lax.dynamic_slice_in_dim(pre, x * BLOCK, BLOCK, axis=0)
     my_unit, my_norms = unit_rows(jax.nn.silu(my_pre))
-    row_is_neg = lax.broadcasted_iota(jnp.int32, (BLOCK, 1), 0) == PART
+    my_slope = silu_slope(my_pre)
+    node_grads, my_unit, my_norms, my_slope, nowhere = lax.optimization_barrier(
+        (node_grads, my_unit, my_norms, my_slope, x * 0)
+    )
+    pieces = lax.all_to_all(node_grads, ("y", "x"), split_axis=0, concat_axis=0, tiled=True)
+    pieces, neg_row, nowhere = lax.optimization_barrier((pieces, neg_row, nowhere))
+    mine = jnp.sum(pieces.reshape(Y * X, BLOCK, embed_width).astype(f32), axis=0)
+    row_is_neg = lax.broadcasted_iota(jnp.int32, (BLOCK, 1), 0) == PART + nowhere
     mine = jnp.where(row_is_neg, unit_back(mine, my_unit, my_norms), mine)
-    pre_grad = (mine * silu_slope(my_pre)).astype(bf16)
+    pre_grad = (mine * my_slope).astype(bf16)
     all_pre_grad = lax.all_gather(pre_grad, "x", axis=0, tiled=True)
     out = dot_f32(all_pre_grad, projection, ((1,), (1,))).reshape(X, BLOCK, feat_width)
     result = out[:, :PART].reshape(ROWS, feat_width)

time: 321 us -> 336 us (1.047)
  the two profiles are of different devices: /device:TPU:32 before, /device:TPU:4 now
where the time goes in v2:
time: 336 us; the launch traced here: 334 us
  blocking collectives  166 us (49%)
  other arithmetic  64.5 us (19%)
  matrix products  41.8 us (12%)
  local copies, waits for them, and re-layouts  24.1 us (7%)
  waiting for transfers between devices  18.6 us (6%)
  between operations  13.9 us (4%)
  starting transfers between devices  5.96 us (2%)
    all_gather x1, blocking collectives, on_device(): vectors = lax.all_gather(payload, 'z', axis=0, tiled=True)  45.8 us
    all_to_all x1, blocking collectives, on_device(): lax.all_to_all(node_grads, ('y', 'x'), split_axis=0, concat_axis=0, tiled...  36.6 us
    all_gather x1, blocking collectives, on_device(): line = lax.all_gather(packed, 'z', axis=0, tiled=True)  36.1 us
    all_gather x1, blocking collectives, on_device(): some_neg = lax.all_gather(half_neg, 'z', axis=0, tiled=True)  33.2 us
    dot_general x8, matrix products, dot_f32(): lax.dot_general(left, right, (dims, ((), ())), preferred_element_type=f32)  26.4 us
    convert_element_type x3, other arithmetic, hot_rows(): return lax.optimization_barrier((total.astype(bf16), first, second))  20.5 us
    reduce_scatter x1, waiting for transfers between devices, on_device(): got = lax.psum_scatter(part, 'z', scatter_dimension=0, tiled=True)  18.6 us
    all_gather x1, blocking collectives, on_device(): all_pre_grad = lax.all_gather(pre_grad, 'x', axis=0, tiled=True)  13.8 us
  transfers between devices with their start and end apart: 5, of which 1 were waited for; matrix products, arithmetic and copies ran while one was open for 23% of the time, Pallas kernels for 0%

profile of v2, /device:TPU:4, one launch (start us, length us, event | category | flops | bytes accessed | tf_op | source)
XLA Modules:
  0.0 334.5 jit_solution(5913449341195444287)
XLA Ops:
  6.5 0.8 compare_select_fusion
  7.4 1.7 gather_fusion
  9.1 1.2 maximum_maximum_fusion
  10.4 1.0 multiply_reduce_fusion
  11.4 1.2 divide_convert_fusion.2
  12.7 36.1 %all-gather = s32[16,32,16]{1,2,0:T(8,128)S(1)} all-gather(s32[1,32,16]{1,2,0:T(8,128)S(1)} %add_bitcast_fusion), channel_id=1, replica_groups=mesh['y'=4,'z'=16,'c'=2,'x'=4] {'z'}, dimensions={0}, use_global_device_ids=true | all-gather | bytes 34816 | tf_op jit(solution)/shard_map/all_gather | solution.py:87
  49.0 1.9 collective-permute-start
  51.1 3.0 fusion.5
  54.1 10.5 %add_convert_fusion = bf16[512,2304]{1,0:T(8,128)(2,1)} fusion(f32[512]{0:T(512)S(1)} %bitcast.186, s32[512]{0:T(512)S(1)} %bitcast.266, f32[512]{0:T(512)S(1)} %bitcast.188, s32[512]{0:T(512)S(1)} %bitcast.267, f32[512]{0:T(512)S(1)} %bitcast.190, s32[512]{0:T(512)S(1)} %bitcast.268, f32[512]{0:T(512)S(1)} %bitcast.192, s32[512]{0:T(512)S(1)} %bitcast.269, ...), kind=kLoop, calls=%fused_computation.15 | loop fusion | flops 49545216 | bytes 2414592 | tf_op jit(solution)/shard_map/convert_element_type | solution.py:60
  64.8 6.4 %pad_maximum_fusion = bf16[16,3,32,2304]{3,2,1,0:T(8,128)(2,1)} fusion(bf16[16,1,32,2304]{3,2,1,0:T(8,128)(2,1)} %bitcast.175, bf16[16,1,32,2304]{3,2,1,0:T(8,128)(2,1)} %bitcast.174, bf16[16,1,32,2304]{3,2,1,0:T(8,128)(2,1)} %bitcast.173), kind=kLoop, calls=%fused_computation.1 | loop fusion | flops 7077888 | bytes 14155776 | tf_op jit(solution)/shard_map/stack | solution.py:96
  71.2 12.2 %convolution_convert_fusion = bf16[1536,1024]{1,0:T(8,128)(2,1)} fusion(bf16[1536,2304]{1,0:T(8,128)(2,1)} %bitcast.176, bf16[2304,1024]{1,0:T(8,128)(2,1)} %all-gather.4.cloned.1.call-done), kind=kOutput, calls=%fused_computation.32 | convolution fusion | flops 7249330176 | bytes 14942208 | tf_op jit(solution)/shard_map/dot_general | solution.py:97
  84.0 0.9 add_multiply_fusion
  85.0 1.9 fusion.9
  86.8 4.5 %add_convert_fusion.2 = bf16[512,1152]{1,0:T(8,128)(2,1)S(1)} fusion(f32[512]{0:T(512)S(1)} %bitcast.187, s32[512]{0:T(512)S(1)} %bitcast.216, f32[512]{0:T(512)S(1)} %bitcast.189, s32[512]{0:T(512)S(1)} %bitcast.217, f32[512]{0:T(512)S(1)} %bitcast.191, s32[512]{0:T(512)S(1)} %bitcast.218, f32[512]{0:T(512)S(1)} %bitcast.193, s32[512]{0:T(512)S(1)} %bitcast.219, ...), kind=kLoop, calls=%fused_computation.56 | loop fusion | flops 24772608 | bytes 1234944 | tf_op jit(solution)/shard_map/convert_element_type | solution.py:60
  92.1 5.5 %add_convert_fusion.1 = bf16[512,1152]{1,0:T(8,128)(2,1)} fusion(f32[512]{0:T(512)S(1)} %bitcast.253, s32[512]{0:T(512)S(1)} %bitcast.230, f32[512]{0:T(512)S(1)} %bitcast.254, s32[512]{0:T(512)S(1)} %bitcast.231, f32[512]{0:T(512)S(1)} %bitcast.255, s32[512]{0:T(512)S(1)} %bitcast.232, f32[512]{0:T(512)S(1)} %bitcast.256, s32[512]{0:T(512)S(1)} %bitcast.233, ...), kind=kLoop, calls=%fused_computation.39 | loop fusion | flops 24772608 | bytes 1234944 | tf_op jit(solution)/shard_map/convert_element_type | solution.py:60
  97.6 1.1 slice.557
  98.9 33.2 %all_gather.17 = bf16[256,1024]{1,0:T(8,128)(2,1)S(1)} all-gather(bf16[16,1024]{1,0:T(8,128)(2,1)S(1)} %reshape.183), channel_id=1, replica_groups=mesh['y'=4,'z'=16,'c'=2,'x'=4] {'z'}, dimensions={0}, use_global_device_ids=true | all-gather | bytes 557056 | tf_op jit(solution)/shard_map/all_gather | solution.py:102
  132.1 1.9 collective-permute-start.1
  134.1 1.9 fusion.11
  135.9 3.3 constant_dynamic-slice_fusion
  139.2 1.0 pad_maximum_fusion.1
  140.2 18.6 %reduce-scatter.2.cloned.1.call-done = bf16[96,1024]{1,0:T(8,128)(2,1)} async-done(((bf16[1536,1024]{1,0:T(8,128)(2,1)}), bf16[96,1024]{1,0:T(8,128)(2,1)}) %reduce-scatter.2.cloned.1.call-update) | async-done | bytes 196624 | tf_op jit(solution)/shard_map/reduce_scatter | solution.py:98
  158.8 1.0 convert_element_type.164
  163.4 1.2 convert_reduce_fusion.1
  165.2 0.8 copy.51
  166.0 1.3 copy.52
  167.3 1.4 copy.48
  168.7 1.3 copy.49
  170.0 1.4 copy.50
  171.4 2.2 convert_convert_fusion
  173.6 1.0 subtract_convert_fusion
  174.6 1.0 concatenate.18
  175.6 45.8 %all-gather.5 = f16[512,2176]{1,0:T(8,128)(2,1)} all-gather(f16[32,2176]{1,0:T(8,128)(2,1)S(1)} %concatenate.18), channel_id=1, replica_groups=mesh['y'=4,'z'=16,'c'=2,'x'=4] {'z'}, dimensions={0}, use_global_device_ids=true | all-gather | bytes 2367488 | tf_op jit(solution)/shard_map/all_gather | solution.py:158
  221.4 2.1 collective-permute-start.2
  223.5 0.9 slice_convert_fusion.3
  224.4 1.5 fusion.95
  225.9 1.1 copy.53
  227.0 1.1 copy.54
  228.1 1.1 copy.55
  229.1 1.7 copy.56
  230.8 1.6 copy.57
  232.4 0.7 copy.58
  233.1 0.7 div.223
  233.8 0.7 add.456
  234.5 1.5 slice_convert_fusion.1
  236.0 2.0 divide_convert_fusion.1
  238.4 3.6 %fusion.104 = f32[1152,1024]{1,0:T(8,128)} fusion(bf16[512,1152]{1,0:T(8,128)(2,1)S(1)} %add_convert_fusion.2, bf16[512,1024]{1,0:T(8,128)(2,1)S(1)} %divide_convert_fusion.1), kind=kOutput, calls=%fused_computation.278 | convolution fusion | flops 1207959552 | bytes 6946816 | tf_op jit(solution)/shard_map/dot_general | solution.py:40
  242.0 5.9 %fusion.13 = f32[1152,1024]{1,0:T(8,128)} fusion(bf16[512,1024]{1,0:T(8,128)(2,1)} %copy-done.2, bf16[512,16]{0,1:T(8,128)(2,1)S(1)} %fusion.39, bf16[512,1152]{1,0:T(8,128)(2,1)} %get-tuple-element.54, bf16[512,1152]{1,0:T(8,128)(2,1)} %get-tuple-element.52, f32[512]{0:T(512)S(1)} %bitcast.281, f32[512]{0:T(512)S(1)} %bitcast.280, s32[16]{0:T(128)S(1)} %copy-done.13), kind=kOutput, calls=%fused_computation.77 | convolution fusion | flops 1230981120 | bytes 8147008 | tf_op jit(solution)/shard_map/dot_general | solution.py:40
  247.9 0.9 slice_convert_fusion.2
  248.8 1.2 fusion.94
  250.0 1.1 copy.59
  251.8 1.5 slice_convert_fusion
  253.2 2.6 divide_convert_fusion
  256.2 7.3 %fusion = (f32[1152]{0:T(1024)S(1)}, f32[1152]{0:T(1024)S(1)}, f32[1152,1024]{1,0:T(8,128)}) fusion(bf16[1152,1024]{1,0:T(8,128)(2,1)} %bitcast.170, f32[1152,1024]{1,0:T(8,128)} %fusion.13, bf16[512,1024]{1,0:T(8,128)(2,1)S(1)} %slice_convert_fusion, bf16[512,16]{0,1:T(8,128)(2,1)S(1)} %fusion.40, bf16[512,1152]{1,0:T(8,128)(2,1)} %get-tuple-element.58, ...), kind=kOutput, calls=%fused_computation.7 | convolution fusion | flops 1238056704 | bytes 15234112 | tf_op jit(solution)/shard_map/dot_general | solution.py:40
  263.6 6.9 %fusion.4 = bf16[1152,1024]{1,0:T(8,128)(2,1)S(1)} fusion(f32[1152,1024]{1,0:T(8,128)} %get-tuple-element.202, bf16[1152,1024]{1,0:T(8,128)(2,1)} %bitcast.171, f32[1152,1024]{1,0:T(8,128)} %fusion.104, bf16[512,1152]{1,0:T(8,128)(2,1)} %add_convert_fusion.1, bf16[512,1024]{1,0:T(8,128)(2,1)} %divide_convert_fusion, f32[1152]{0:T(1024)S(1)} %select_multiply_fusion), kind=kOutput, calls=%fused_computation.11 | convolution fusion | flops 1215037440 | bytes 16388608 | tf_op jit(solution)/shard_map/dot_general | solution.py:40
  270.4 36.6 %all_to_all.12 = bf16[16,72,1024]{2,1,0:T(8,128)(2,1)S(1)} all-to-all(bf16[16,72,1024]{2,1,0:T(8,128)(2,1)S(1)} %bitcast.172), channel_id=1, replica_groups=mesh['y'=4,'z'=16,'c'=2,'x'=4] {'y','x'}, dimensions={0} | all-to-all | bytes 4718592 | tf_op jit(solution)/shard_map/all_to_all | solution.py:197
  308.3 13.8 %all_gather.19 = bf16[288,1024]{1,0:T(8,128)(2,1)S(1)} all-gather(bf16[72,1024]{1,0:T(8,128)(2,1)S(1)} %multiply_convert_fusion), channel_id=1, replica_groups=mesh['y'=4,'z'=16,'c'=2,'x'=4] {'x'}, dimensions={0}, use_global_device_ids=true | all-gather | bytes 737280 | tf_op jit(solution)/shard_map/all_gather | solution.py:203
  322.1 0.8 fusion.105
  323.0 0.7 fusion.103
  323.7 0.6 iota_compare_fusion.53
  324.3 0.6 iota_compare_fusion.54
  325.0 0.6 iota_compare_fusion.55
  325.6 0.7 iota_compare_fusion.56
  326.3 1.4 fusion.43
  (96 shorter events, 9.2 us)
Async XLA Ops:
  6.5 3.8 %copy-start = (bf16[1024,1024]{1,0:T(8,128)(2,1)S(1)}, bf16[1024,1024]{1,0:T(8,128)(2,1)}, u32[]{:S(2)}) copy-start(bf16[1024,1024]{1,0:T(8,128)(2,1)} %param.7) | copy-start | bytes 6291460
  6.5 64.7 %all-gather.4.cloned.1.call-start = ((), (), s32[]{:S(2)}) async-start(), calls=%async_computation.2 | async-start | bytes 5308416 | tf_op jit(solution)/shard_map/all_gather | solution.py:85
  11.4 1.3 copy-start.9
  11.4 1.3 copy-start.10
  11.4 1.3 copy-start.11
  12.6 146.2 %reduce-scatter.2.cloned.1.call-start = ((), (), s32[]{:S(2)}) async-start(), calls=%async_computation.3 | async-start | bytes 3342336 | tf_op jit(solution)/shard_map/reduce_scatter | solution.py:98
  49.0 42.9 %collective-permute-start = (s32[512,16]{0,1:T(8,128)S(1)}, s32[512,16]{0,1:T(8,128)S(1)}, u32[]{:S(2)}, u32[]{:S(2)}) collective-permute-start(s32[512,16]{0,1:T(8,128)S(1)} %reshape.197), channel_id=1, source_target_pairs={{0,4},{4,0},{1,5},{5,1},{2,6},{6,2},{3,7},{7,3},{8,12},{12,8},{9,1... | collective-permute-start | bytes 98312 | tf_op jit(solution)/shard_map/ppermute | solution.py:88
  98.9 40.3 %copy-start.6 = (bf16[16,1024]{1,0:T(8,128)(2,1)}, bf16[16,1024]{1,0:T(8,128)(2,1)S(1)}, u32[]{:S(2)}) copy-start(bf16[16,1024]{1,0:T(8,128)(2,1)S(1)} %reshape.183) | copy-start | bytes 98308
  132.1 7.0 %collective-permute-start.1 = (bf16[256,1024]{1,0:T(8,128)(2,1)S(1)}, bf16[256,1024]{1,0:T(8,128)(2,1)S(1)}, u32[]{:S(2)}, u32[]{:S(2)}) collective-permute-start(bf16[256,1024]{1,0:T(8,128)(2,1)S(1)} %all_gather.17), channel_id=1, source_target_pairs={{0,4},{4,0},{1,5},{5,1},{2,6},{6,2},{3,7},{7,3},{8,12},{12,8},{9,1... | collective-permute-start | bytes 1572872 | tf_op jit(solution)/shard_map/ppermute | solution.py:103
  158.8 4.5 %copy-start.1 = (bf16[512,1024]{1,0:T(8,128)(2,1)S(1)}, bf16[512,1024]{1,0:T(8,128)(2,1)}, u32[]{:S(2)}) copy-start(bf16[512,1024]{1,0:T(8,128)(2,1)} %pad_maximum_fusion.1) | copy-start | bytes 3145732
  159.9 4.7 %copy-start.3 = (f32[96,1024]{1,0:T(8,128)}, f32[96,1024]{1,0:T(8,128)S(1)}, u32[]{:S(2)}) copy-start(f32[96,1024]{1,0:T(8,128)S(1)} %convert_element_type.164) | copy-start | bytes 1179652
  160.6 4.5 %copy-start.12 = (f32[32]{0:T(128)}, f32[32]{0:T(128)S(1)}, u32[]{:S(2)}) copy-start(f32[32]{0:T(128)S(1)} %get-tuple-element.196) | copy-start | bytes 388
  221.4 26.5 %collective-permute-start.2 = (f16[512,2176]{1,0:T(8,128)(2,1)}, f16[512,2176]{1,0:T(8,128)(2,1)}, u32[]{:S(2)}, u32[]{:S(2)}) collective-permute-start(f16[512,2176]{1,0:T(8,128)(2,1)} %all-gather.5), channel_id=1, source_target_pairs={{0,4},{4,0},{1,5},{5,1},{2,6},{6,2},{3,7},{7,3},{8,12},{12,8},{9,1... | collective-permute-start | bytes 6684680 | tf_op jit(solution)/shard_map/ppermute | solution.py:159
  233.1 4.9 %copy-start.7 = (bf16[16,1024]{1,0:T(8,128)(2,1)S(1)}, bf16[16,1024]{1,0:T(8,128)(2,1)}, u32[]{:S(2)}) copy-start(bf16[16,1024]{1,0:T(8,128)(2,1)} %copy-done.6) | copy-start | bytes 98308
  236.0 6.0 %copy-start.2 = (bf16[512,1024]{1,0:T(8,128)(2,1)}, bf16[512,1024]{1,0:T(8,128)(2,1)S(1)}, u32[]{:S(2)}) copy-start(bf16[512,1024]{1,0:T(8,128)(2,1)S(1)} %slice_convert_fusion.1) | copy-start | bytes 3145732
  238.4 3.6 %copy-start.13 = (s32[16]{0:T(128)S(1)}, s32[16]{0:T(128)}, u32[]{:S(2)}) copy-start(s32[16]{0:T(128)} %multiply_add_fusion) | copy-start | bytes 196
  307.1 1.0 copy-start.4
  307.1 1.1 copy-start.5
  307.1 1.1 copy-start.14
  322.1 0.9 copy-start.8
Sparse Core Ops, SparseCore 0:
  12.8 46.3 all-gather.3
  83.6 75.1 reduce-scatter.1

commit v3 on v1

v3 whole, which is shorter than its diff:
```python
import jax
import jax.numpy as jnp
from jax import lax
from jax.experimental import pallas as pl
from jax.experimental.pallas import tpu as pltpu
from jax.sharding import Mesh
from jax.sharding import PartitionSpec as P

score_scale = 8.0
margin_value = 0.1
epsilon = 1e-06
log_two = 0.6931471805599453

Y, Z, C, X = 4, 16, 2, 4
ROWS = 256
PART = ROWS // X
BLOCK = PART + 8
OWN = X * BLOCK
WIDE = Y * C * OWN
NARROW = Y * OWN
bf16 = jnp.bfloat16
f16 = jnp.float16
f32 = jnp.float32
SIBLING = [(0, 1), (1, 0)]


def silu_slope(preact):
    gate_value = jax.nn.sigmoid(preact)
    return gate_value * (1.0 + preact * (1.0 - gate_value))


def row_sum(values):
    return jnp.sum(values, axis=1, keepdims=True)


def row_norm(values):
    return jnp.sqrt(row_sum(values * values) + epsilon)


def weigh(score, positive):
    return (score_scale * jax.nn.sigmoid(score_scale * (score - positive + margin_value))).astype(bf16)


def dot_nn(left, right):
    return lax.dot_general(left, right, (((1,), (0,)), ((), ())), preferred_element_type=f32)


def dot_nt(left, right):
    return lax.dot_general(left, right, (((1,), (1,)), ((), ())), preferred_element_type=f32)


def decode(packed, axis):
    owner = packed & 127
    row = (packed >> 7) & 255
    visits = (packed >> 15).astype(f32)
    coefs = visits / jnp.sum(visits, axis=axis, keepdims=True)
    return owner >> 5, owner & 1, (owner >> 1) & 15, row >> 6, row & 63, coefs


def spread_kernel(where_ref, line_ref, out_ref):
    ny, nc, nz, part, rest, coefs = decode(line_ref[...], 1)
    column = jnp.where(nz == where_ref[0], (ny * C + nc) * OWN + part * BLOCK + rest, -1)
    rows, slots = column.shape
    chunk = WIDE // 3
    for k in range(3):
        lanes = lax.broadcasted_iota(jnp.int32, (rows, chunk), 1) + k * chunk
        total = jnp.where(lanes == column[:, 0:1], 1.0, 0.0)
        for slot in range(3, slots):
            total = total + jnp.where(lanes == column[:, slot : slot + 1], coefs[:, slot : slot + 1], 0.0)
        span = pl.ds(k * chunk, chunk)
        out_ref[0, 0, :, span] = total.astype(bf16)
        out_ref[0, 1, :, span] = jnp.where(lanes == column[:, 1:2], 1.0, 0.0).astype(bf16)
        out_ref[0, 2, :, span] = jnp.where(lanes == column[:, 2:3], 1.0, 0.0).astype(bf16)


def node_weights_kernel(where_ref, line_ref, out_ref):
    ny, nc, nz, part, rest, coefs = decode(line_ref[...], 0)
    here = (nz == where_ref[0]) & (nc == where_ref[1])
    column = jnp.where(here, part * (Y * BLOCK) + ny * BLOCK + rest, -1)
    slots, count = column.shape
    base = pl.program_id(0) * OWN
    chunk = 32
    for k in range(OWN // chunk):
        nodes = lax.broadcasted_iota(jnp.int32, (chunk, count), 0) + (base + k * chunk)
        total = jnp.where(nodes == column[0:1], 1.0, 0.0)
        for slot in range(3, slots):
            total = total + jnp.where(nodes == column[slot : slot + 1], coefs[slot : slot + 1], 0.0)
        span = pl.ds(k * chunk, chunk)
        out_ref[0, span, :] = total.astype(bf16)
        out_ref[1, span, :] = jnp.where(nodes == column[1:2], 1.0, 0.0).astype(bf16)
        out_ref[2, span, :] = jnp.where(nodes == column[2:3], 1.0, 0.0).astype(bf16)


def query_kernel(got_ref, neg_a_ref, neg_b_ref, out_ref):
    count = got_ref.shape[0] // 3
    width = got_ref.shape[1]
    hood = got_ref[0:count].astype(f32)
    query_norm = row_norm(hood)
    query_unit = hood / query_norm
    query_embed = query_unit.astype(bf16)
    query_float = query_embed.astype(f32)
    first = got_ref[count : 2 * count].astype(f32)
    second = got_ref[2 * count :].astype(f32)
    first_norm, second_norm = row_norm(first), row_norm(second)
    first_embed = (first / first_norm).astype(bf16).astype(f32)
    second_embed = (second / second_norm).astype(bf16).astype(f32)
    positive = row_sum(query_float * first_embed)
    hard = weigh(row_sum(query_float * second_embed), positive).astype(f32)
    weight_a = weigh(dot_nt(query_embed, neg_a_ref[...]), positive)
    weight_b = weigh(dot_nt(query_embed, neg_b_ref[...]), positive)
    total = row_sum(weight_a.astype(f32)) + row_sum(weight_b.astype(f32)) + hard
    grad = dot_nn(weight_a, neg_a_ref[...]) + dot_nn(weight_b, neg_b_ref[...]) + hard * second_embed - total * first_embed
    grad = grad - query_unit * row_sum(query_unit * grad)
    power = jnp.exp(jnp.ceil(jnp.log(query_norm) * (1.0 / log_two)) * log_two).astype(bf16).astype(f32)
    inverse = (16.0 / power).astype(bf16).astype(f32)
    out_ref[:, 0:width] = grad * (power / query_norm)
    out_ref[:, width : 2 * width] = query_float
    lanes = lax.broadcasted_iota(jnp.int32, (count, 128), 1)
    scalars = jnp.where(lanes == 0, inverse, 0.0)
    for place, value in ((1, total), (3, hard), (5, first_norm), (7, second_norm), (9, positive)):
        high = value.astype(bf16).astype(f32)
        scalars = jnp.where(lanes == place, high, scalars)
        scalars = jnp.where(lanes == place + 1, value - high, scalars)
    out_ref[:, 2 * width :] = scalars


def node_grad_kernel(own_w_ref, sib_w_ref, own_ref, sib_ref, plane_ref, neg_ref, out_ref, row_ref, neg_w_ref):
    step = pl.program_id(0)
    width = plane_ref.shape[1]
    received = (own_ref, sib_ref)

    @pl.when(step == 0)
    def _():
        for side, ref in enumerate(received):
            scalars = ref[:, 2 * width :].astype(f32).T
            total = scalars[1:2] + scalars[2:3]
            hard = scalars[3:4] + scalars[4:5]
            row_ref[side, 0:1] = scalars[0:1] * 0.0625
            row_ref[side, 1:2] = -total / (scalars[5:6] + scalars[6:7])
            row_ref[side, 2:3] = hard / (scalars[7:8] + scalars[8:9])
            scores = dot_nt(neg_ref[...], ref[:, width : 2 * width])
            neg_w_ref[side] = weigh(scores, scalars[9:10] + scalars[10:11])

    negs = neg_ref.shape[0]
    rows = lax.broadcasted_iota(jnp.int32, (OWN, negs), 0) + step * OWN
    spot = jnp.where(rows == lax.broadcasted_iota(jnp.int32, (OWN, negs), 1) * BLOCK + PART, 1.0, 0.0).astype(bf16)
    hood_part = jnp.zeros((OWN, width), f32)
    query_part = jnp.zeros((OWN, width), f32)
    for side, (w_ref, ref) in enumerate(((own_w_ref, own_ref), (sib_w_ref, sib_ref))):
        w_hood = (w_ref[0].astype(f32) * row_ref[side, 0:1]).astype(bf16)
        hood_part = hood_part + dot_nn(w_hood, ref[:, 0:width])
        w_query = w_ref[1].astype(f32) * row_ref[side, 1:2] + w_ref[2].astype(f32) * row_ref[side, 2:3]
        w_query = (w_query + dot_nn(spot, neg_w_ref[side])).astype(bf16)
        query_part = query_part + dot_nn(w_query, ref[:, width : 2 * width])
    plane = plane_ref[...].astype(f32)
    place = lax.broadcasted_iota(jnp.int32, (OWN, 1), 0) % BLOCK
    inverse = jnp.where(place == PART, 0.0, 1.0 / (row_sum(plane * plane) + epsilon))
    query_part = query_part - plane * (inverse * row_sum(plane * query_part))
    out_ref[...] = (hood_part + query_part).astype(bf16)


def owner_kernel(pieces_ref, pre_ref, out_ref):
    total = pieces_ref[0].astype(f32)
    for k in range(1, pieces_ref.shape[0]):
        total = total + pieces_ref[k].astype(f32)
    pre = pre_ref[...]
    act = pre * jax.nn.sigmoid(pre)
    norm = row_norm(act)
    unit = act / norm
    place = lax.broadcasted_iota(jnp.int32, (BLOCK, 1), 0)
    back = (total - unit * row_sum(unit * total)) / norm
    total = jnp.where(place == PART, back, total)
    out_ref[...] = (total * silu_slope(pre)).astype(bf16)


def table_kernel(neg_row_ref, grad_ref, projection_ref, out_ref):
    out = dot_nt(grad_ref[...], projection_ref[...])
    rows = lax.broadcasted_iota(jnp.int32, (PART, 1), 0)
    for k in range(X):
        block = out[k * BLOCK : k * BLOCK + PART]
        for i in range(X):
            hit = rows + k * PART == neg_row_ref[i]
            block = block + jnp.where(hit, out[i * BLOCK + PART : i * BLOCK + PART + 1], 0.0)
        out_ref[k * PART : (k + 1) * PART] = block


def call(kernel, out_shape, flops, moved, **rest):
    return pl.pallas_call(
        kernel,
        out_shape=out_shape,
        cost_estimate=pl.CostEstimate(flops=flops, bytes_accessed=moved, transcendentals=0),
        compiler_params=pltpu.CompilerParams(vmem_limit_bytes=56 << 20),
        **rest,
    )


VMEM = pl.BlockSpec(memory_space=pltpu.VMEM)
SMEM = pl.BlockSpec(memory_space=pltpu.SMEM)


def on_device(feature_table, projection, slot_owner, slot_row, visits, neg_row):
    z, c, x = (lax.axis_index(a) for a in ("z", "c", "x"))
    here = jnp.stack([z, c]).astype(jnp.int32)
    query_count, slot_count = slot_row.shape
    feat_width, embed_width = projection.shape
    line_count = Z * query_count

    shifted = jnp.pad(visits, ((0, 0), (3, 0)))
    packed = slot_owner.reshape(query_count, slot_count) + slot_row * 128 + shifted * 32768

    rows = jnp.concatenate(
        [
            feature_table.reshape(X, PART, feat_width),
            feature_table[neg_row].reshape(X, 1, feat_width),
            jnp.zeros((X, BLOCK - PART - 1, feat_width), bf16),
        ],
        axis=1,
    ).reshape(OWN, feat_width)
    pre = jnp.dot(rows, projection, preferred_element_type=f32)
    act = jax.nn.silu(pre)
    is_neg = (lax.broadcasted_iota(jnp.int32, (OWN, 1), 0) % BLOCK) == PART
    shared = (act / jnp.where(is_neg, row_norm(act), 1.0)).astype(bf16)
    plane = lax.all_gather(shared, ("y", "c"), axis=0, tiled=True)
    my_pre = lax.dynamic_slice_in_dim(pre, x * BLOCK, BLOCK, axis=0)

    line = lax.all_gather(packed, "z", axis=0, tiled=True)
    spread = call(
        spread_kernel,
        jax.ShapeDtypeStruct((Z, 3, query_count, WIDE), bf16),
        line_count * WIDE * 48,
        line_count * WIDE * 6,
        grid=(Z,),
        in_specs=[SMEM, pl.BlockSpec((query_count, slot_count), lambda i: (i, 0))],
        out_specs=pl.BlockSpec((1, 3, query_count, WIDE), lambda i: (i, 0, 0, 0)),
    )(here, line)
    part = dot_nn(spread.reshape(3 * line_count, WIDE), plane).astype(bf16)
    part, plane, line = lax.optimization_barrier((part, plane, line))
    got = lax.psum_scatter(part, "z", scatter_dimension=0, tiled=True)

    core_plane = lax.dynamic_index_in_dim(plane.reshape(Y, C, X, BLOCK, embed_width), c, axis=1, keepdims=False)
    core_plane = core_plane.transpose(1, 0, 2, 3)
    core_neg = core_plane[:, :, PART].reshape(X * Y, embed_width)
    core_plane = core_plane.reshape(NARROW, embed_width)
    some_neg = lax.all_gather(core_neg, "z", axis=0, tiled=True)
    other_neg = lax.ppermute(some_neg, "c", SIBLING)
    line_sib = lax.ppermute(line, "c", SIBLING)

    def node_weights(some_line):
        return call(
            node_weights_kernel,
            jax.ShapeDtypeStruct((3, NARROW, line_count), bf16),
            line_count * NARROW * 48,
            line_count * NARROW * 6,
            grid=(X,),
            in_specs=[SMEM, pl.BlockSpec((slot_count, line_count), lambda i: (0, 0))],
            out_specs=pl.BlockSpec((3, OWN, line_count), lambda i: (0, i, 0)),
        )(here, some_line.T)

    own_w, sib_w = node_weights(line), node_weights(line_sib)
    got, own_w, sib_w, core_plane, some_neg, other_neg = lax.optimization_barrier(
        (got, own_w, sib_w, core_plane, some_neg, other_neg)
    )

    payload_width = 2 * embed_width + 128
    payload = call(
        query_kernel,
        jax.ShapeDtypeStruct((query_count, payload_width), f32),
        4 * query_count * 512 * embed_width,
        1 << 20,
        in_specs=[VMEM] * 3,
        out_specs=VMEM,
    )(got, some_neg, other_neg)
    own = lax.all_gather(payload.astype(f16), "z", axis=0, tiled=True).astype(bf16)
    sib = lax.ppermute(own, "c", SIBLING)

    node_grads = call(
        node_grad_kernel,
        jax.ShapeDtypeStruct((NARROW, embed_width), bf16),
        8 * line_count * NARROW * embed_width,
        16 << 20,
        grid=(X,),
        in_specs=[
            pl.BlockSpec((3, OWN, line_count), lambda i: (0, i, 0)),
            pl.BlockSpec((3, OWN, line_count), lambda i: (0, i, 0)),
            pl.BlockSpec((line_count, payload_width), lambda i: (0, 0)),
            pl.BlockSpec((line_count, payload_width), lambda i: (0, 0)),
            pl.BlockSpec((OWN, embed_width), lambda i: (i, 0)),
            pl.BlockSpec((X * Y, embed_width), lambda i: (0, 0)),
        ],
        out_specs=pl.BlockSpec((OWN, embed_width), lambda i: (i, 0)),
        scratch_shapes=[pltpu.VMEM((2, 8, line_count), f32), pltpu.VMEM((2, X * Y, line_count), bf16)],
    )(own_w, sib_w, own, sib, core_plane, core_neg)

    pieces = lax.all_to_all(node_grads, ("x", "y"), split_axis=0, concat_axis=0, tiled=True)
    pre_grad = call(
        owner_kernel,
        jax.ShapeDtypeStruct((BLOCK, embed_width), bf16),
        1 << 22,
        3 << 20,
        in_specs=[VMEM] * 2,
        out_specs=VMEM,
    )(pieces.reshape(X * Y, BLOCK, embed_width), my_pre)
    all_pre_grad = lax.all_gather(pre_grad, "x", axis=0, tiled=True)
    return call(
        table_kernel,
        jax.ShapeDtypeStruct((ROWS, feat_width), f32),
        2 * OWN * embed_width * feat_width,
        4 << 20,
        in_specs=[SMEM, VMEM, VMEM],
        out_specs=VMEM,
    )(neg_row, all_pre_grad, projection)


def solution(mesh):
    grid = Mesh(mesh.devices.reshape(Y, Z, C, X), ("y", "z", "c", "x"))
    shard = ("y", "z", "c")
    every = ("y", "z", "c", "x")
    return jax.shard_map(
        on_device,
        mesh=grid,
        in_specs=(
            P(shard, None),
            P(),
            P(every, None, None),
            P(every, None),
            P(every, None),
            P(shard),
        ),
        out_specs=P(shard, None),
        check_vma=False,
    )
```

time: 321 us -> 291 us (0.907)
  the two profiles are of different devices: /device:TPU:32 before, /device:TPU:8 now
where the time goes in v3:
time: 291 us; the launch traced here: 289 us
  blocking collectives  125 us (43%)
  waiting for transfers between devices  55.2 us (19%)
  Pallas kernels  46 us (16%)
  local copies, waits for them, and re-layouts  15.4 us (5%)
  matrix products  14.8 us (5%)
  starting transfers between devices  14 us (5%)
  between operations  13.6 us (5%)
  other arithmetic  4.96 us (2%)
    all_gather x1, blocking collectives, on_device(): lax.all_gather(payload.astype(f16), 'z', axis=0, tiled=True).astype(bf16)  42.3 us
    all_gather x1, blocking collectives, on_device(): line = lax.all_gather(packed, 'z', axis=0, tiled=True)  36.1 us
    all_gather x1, blocking collectives, on_device(): some_neg = lax.all_gather(core_neg, 'z', axis=0, tiled=True)  32 us
    all_to_all x1, waiting for transfers between devices, on_device(): lax.all_to_all(node_grads, ('x', 'y'), split_axis=0, concat_axis=0, tiled...  30.8 us
    reduce_scatter x1, waiting for transfers between devices, on_device(): got = lax.psum_scatter(part, 'z', scatter_dimension=0, tiled=True)  20 us
    all_gather x1, blocking collectives, on_device(): all_pre_grad = lax.all_gather(pre_grad, 'x', axis=0, tiled=True)  14.6 us
    pallas_call x1, Pallas kernels, on_device(): call(spread_kernel, jax.ShapeDtypeStruct((Z, 3, query_count, WIDE), bf16)...  13.1 us
    dot_general x1, matrix products, dot_nn(): lax.dot_general(left, right, (((1,), (0,)), ((), ())), preferred_element_...  12.2 us
  transfers between devices with their start and end apart: 6, of which 3 were waited for; matrix products, arithmetic and copies ran while one was open for 3% of the time, Pallas kernels for 8%

profile of v3, /device:TPU:8, one launch (start us, length us, event | category | flops | bytes accessed | tf_op | source)
XLA Modules:
  0.0 288.9 jit_solution(9140015582494526866)
XLA Ops:
  6.5 0.0 all-gather.4.cloned.1.call-start
  6.5 0.7 compare_select_fusion
  7.2 1.7 gather_fusion
  8.9 0.1 pad.7.clone
  9.0 1.2 maximum_maximum_fusion
  10.2 2.6 multiply_reduce_fusion
  12.8 0.0 copy-start.3
  12.8 0.0 copy-start.8
  12.8 0.0 copy-start.9
  12.8 0.0 copy-start.10
  12.9 1.0 copy-done.3
  13.8 1.2 divide_convert_fusion
  15.0 0.0 all-gather.4.cloned.1.call-update
  15.1 0.0 reduce-scatter.2.cloned.1.call-start
  15.1 0.0 copy-done.8
  15.1 0.0 copy-done.9
  15.1 0.0 copy-done.10
  15.2 36.1 %all-gather = s32[16,32,16]{1,2,0:T(8,128)S(1)} all-gather(s32[1,32,16]{1,2,0:T(8,128)S(1)} %add_bitcast_fusion), channel_id=1, replica_groups=mesh['y'=4,'z'=16,'c'=2,'x'=4] {'z'}, dimensions={0}, use_global_device_ids=true | all-gather | bytes 34816 | tf_op jit(solution)/shard_map/all_gather | solution.py:226
  51.3 0.1 reshape.67
  51.4 0.0 copy-start.5
  51.4 0.8 copy.13.line_ref
  52.2 0.6 pad_add_fusion.where_ref
  52.9 13.1 %shard_map.64 = bf16[16,3,32,2304]{3,2,1,0:T(8,128)(2,1)} custom-call(s32[2]{0:T(128)} %pad_add_fusion.where_ref, s32[512,16]{1,0:T(8,128)} %copy.13.line_ref), custom_call_target="tpu_custom_call" | custom-call | flops 56623104 | bytes 7077888 | tf_op jit(solution)/shard_map/pallas_call | solution.py:227
  66.0 0.0 all-gather.4.cloned.1.call-done
  66.0 12.2 %convolution_convert_fusion = bf16[1536,1024]{1,0:T(8,128)(2,1)} fusion(bf16[1536,2304]{1,0:T(8,128)(2,1)} %bitcast.29, bf16[2304,1024]{1,0:T(8,128)(2,1)} %all-gather.4.cloned.1.call-done), kind=kOutput, calls=%fused_computation.1 | convolution fusion | flops 7249330176 | bytes 14942208 | tf_op jit(solution)/shard_map/dot_general | solution.py:45
  78.2 0.0 reduce-scatter.2.cloned.1.call-update
  78.2 2.0 constant_dynamic-slice_fusion.1
  80.2 1.8 copy.18
  82.1 0.0 copy-start.6
  82.1 32.0 %all_gather.17.neg_a_ref = bf16[256,1024]{1,0:T(8,128)(2,1)S(1)} all-gather(bf16[16,1024]{1,0:T(8,128)(2,1)S(1)} %reshape_squeeze.3.neg_ref), channel_id=1, replica_groups=mesh['y'=4,'z'=16,'c'=2,'x'=4] {'z'}, dimensions={0}, use_global_device_ids=true | all-gather | bytes 557056 | tf_op jit(solution)/shard_map/all_gather | solution.py:244
  114.1 0.0 copy-start.2
  114.1 1.9 collective-permute-start.1
  116.0 0.0 copy-done.5
  116.0 2.4 collective-permute-start
  118.4 2.8 copy.16
  121.2 0.0 copy-done.6
  121.2 0.0 copy-done.2
  121.2 5.6 %shard_map.65.own_w_ref = bf16[3,1152,512]{2,1,0:T(8,128)(2,1)} custom-call(s32[2]{0:T(128)} %pad_add_fusion.where_ref, s32[16,512]{1,0:T(8,128)} %bitcast.35), custom_call_target="tpu_custom_call" | custom-call | flops 28311552 | bytes 3538944 | tf_op jit(solution)/shard_map/pallas_call | solution.py:249
  126.7 0.0 collective-permute-done
  126.8 0.0 copy-start.7
  126.8 0.6 copy-done.7
  127.3 5.6 %shard_map.66.sib_w_ref = bf16[3,1152,512]{2,1,0:T(8,128)(2,1)} custom-call(s32[2]{0:T(128)} %pad_add_fusion.where_ref, s32[16,512]{1,0:T(8,128)} %bitcast.36), custom_call_target="tpu_custom_call" | custom-call | flops 28311552 | bytes 3538944 | tf_op jit(solution)/shard_map/pallas_call | solution.py:249
  132.9 0.0 collective-permute-done.1.neg_b_ref
  132.9 0.0 copy-start.4
  132.9 20.0 %reduce-scatter.2.cloned.1.call-done.got_ref = bf16[96,1024]{1,0:T(8,128)(2,1)} async-done(((bf16[1536,1024]{1,0:T(8,128)(2,1)}), bf16[96,1024]{1,0:T(8,128)(2,1)}) %reduce-scatter.2.cloned.1.call-update) | async-done | bytes 196624 | tf_op jit(solution)/shard_map/reduce_scatter | solution.py:238
  152.9 0.0 copy-done.4
  152.9 2.8 shard_map.67
  155.7 1.0 convert_element_type.14
  156.7 42.3 %all-gather.5 = f16[512,2176]{1,0:T(8,128)(2,1)S(1)} all-gather(f16[32,2176]{1,0:T(8,128)(2,1)S(1)} %convert_element_type.14), channel_id=1, replica_groups=mesh['y'=4,'z'=16,'c'=2,'x'=4] {'z'}, dimensions={0}, use_global_device_ids=true | all-gather | bytes 2367488 | tf_op jit(solution)/shard_map/all_gather | solution.py:273
  198.9 0.3 convert_element_type.15.own_ref
  199.2 0.0 copy-start.1
  199.2 1.9 collective-permute-start.2
  201.1 4.3 %collective-permute-done.2.sib_ref = bf16[512,2176]{1,0:T(8,128)(2,1)S(1)} collective-permute-done((bf16[512,2176]{1,0:T(8,128)(2,1)S(1)}, bf16[512,2176]{1,0:T(8,128)(2,1)S(1)}, u32[]{:S(2)}, u32[]{:S(2)}) %collective-permute-start.2) | collective-permute-done | bytes 2228256 | tf_op jit(solution)/shard_map/ppermute | solution.py:274
  205.5 0.0 copy-done.1
  205.5 0.0 copy-start.11
  205.5 1.4 copy-done.11
  206.8 12.1 %shard_map.68 = bf16[1152,1024]{1,0:T(8,128)(2,1)} custom-call(bf16[3,1152,512]{2,1,0:T(8,128)(2,1)} %shard_map.65.own_w_ref, bf16[3,1152,512]{2,1,0:T(8,128)(2,1)} %shard_map.66.sib_w_ref, bf16[512,2176]{1,0:T(8,128)(2,1)} %copy-done.1, bf16[512,2176]{1,0:T(8,128)(2,1)} %copy-done.11, bf16[1152,1024]{1,0:T(8,128)(2,1)} %bitcast.30, bf16[16,1024]{1,0:T(8,128)(2,1)} %copy-done.6), custom_call_target="tpu_custom_call" | custom-call | flops 4831838208 | bytes 16777216 | tf_op jit(solution)/shard_map/pallas_call | solution.py:276
  218.9 7.7 %all-to-all-start = ((bf16[16,72,1024]{2,1,0:T(8,128)(2,1)}), bf16[16,72,1024]{2,1,0:T(8,128)(2,1)S(1)}, u32[]{:S(2)}, u32[]{:S(2)}) async-start(bf16[16,72,1024]{2,1,0:T(8,128)(2,1)} %bitcast.31), calls=%async_computation.1 | async-start | bytes 4718592 | tf_op jit(solution)/shard_map/all_to_all | solution.py:294
  226.7 1.7 constant_dynamic-slice_fusion.pre_ref
  228.4 30.8 %all-to-all-done.pieces_ref = bf16[16,72,1024]{2,1,0:T(8,128)(2,1)S(1)} async-done(((bf16[16,72,1024]{2,1,0:T(8,128)(2,1)}), bf16[16,72,1024]{2,1,0:T(8,128)(2,1)S(1)}, u32[]{:S(2)}, u32[]{:S(2)}) %all-to-all-start) | async-done | bytes 2359328 | tf_op jit(solution)/shard_map/all_to_all | solution.py:294
  259.2 1.4 copy-done
  260.6 2.9 shard_map.69
  263.5 14.6 %all_gather.19.grad_ref = bf16[288,1024]{1,0:T(8,128)(2,1)} all-gather(bf16[72,1024]{1,0:T(8,128)(2,1)} %shard_map.69), channel_id=1, replica_groups=mesh['y'=4,'z'=16,'c'=2,'x'=4] {'x'}, dimensions={0}, use_global_device_ids=true | all-gather | bytes 737280 | tf_op jit(solution)/shard_map/all_gather | solution.py:303
  278.1 4.0 %shard_map.70 = f32[256,1024]{1,0:T(8,128)} custom-call(s32[4]{0:T(128)} %neg_row_ref.1, bf16[288,1024]{1,0:T(8,128)(2,1)} %all_gather.19.grad_ref, bf16[1024,1024]{1,0:T(8,128)(2,1)} %projection_ref.1), custom_call_target="tpu_custom_call" | custom-call | flops 603979776 | bytes 4194304 | tf_op jit(solution)/shard_map/pallas_call | solution.py:304
  (9 shorter events, 0.1 us)
Async XLA Ops:
  6.5 59.5 %all-gather.4.cloned.1.call-start = ((), (), s32[]{:S(2)}) async-start(), calls=%async_computation.2 | async-start | bytes 5308416 | tf_op jit(solution)/shard_map/all_gather | solution.py:223
  12.8 1.0 copy-start.3
  12.8 2.3 copy-start.8
  12.8 2.3 copy-start.9
  12.8 2.3 copy-start.10
  15.1 137.8 %reduce-scatter.2.cloned.1.call-start = ((), (), s32[]{:S(2)}) async-start(), calls=%async_computation.3 | async-start | bytes 3342336 | tf_op jit(solution)/shard_map/reduce_scatter | solution.py:238
  51.4 64.6 %copy-start.5 = (s32[512,16]{0,1:T(8,128)}, s32[512,16]{0,1:T(8,128)S(1)}, u32[]{:S(2)}) copy-start(s32[512,16]{0,1:T(8,128)S(1)} %reshape.67) | copy-start | bytes 98308
  82.1 39.1 %copy-start.6 = (bf16[16,1024]{1,0:T(8,128)(2,1)}, bf16[16,1024]{1,0:T(8,128)(2,1)S(1)}, u32[]{:S(2)}) copy-start(bf16[16,1024]{1,0:T(8,128)(2,1)S(1)} %reshape_squeeze.3.neg_ref) | copy-start | bytes 98308
  114.1 7.1 %copy-start.2 = (bf16[256,1024]{1,0:T(8,128)(2,1)}, bf16[256,1024]{1,0:T(8,128)(2,1)S(1)}, u32[]{:S(2)}) copy-start(bf16[256,1024]{1,0:T(8,128)(2,1)S(1)} %all_gather.17.neg_a_ref) | copy-start | bytes 1572868
  114.1 18.9 %collective-permute-start.1 = (bf16[256,1024]{1,0:T(8,128)(2,1)S(1)}, bf16[256,1024]{1,0:T(8,128)(2,1)S(1)}, u32[]{:S(2)}, u32[]{:S(2)}) collective-permute-start(bf16[256,1024]{1,0:T(8,128)(2,1)S(1)} %all_gather.17.neg_a_ref), channel_id=1, source_target_pairs={{0,4},{4,0},{1,5},{5,1},{2,6},{6,2},{3,7},{7,3},{8,12},{12,8},{9,1... | collective-permute-start | bytes 1572872 | tf_op jit(solution)/shard_map/ppermute | solution.py:245
  116.0 10.8 %collective-permute-start = (s32[512,16]{0,1:T(8,128)S(1)}, s32[512,16]{0,1:T(8,128)S(1)}, u32[]{:S(2)}, u32[]{:S(2)}) collective-permute-start(s32[512,16]{0,1:T(8,128)S(1)} %reshape.67), channel_id=1, source_target_pairs={{0,4},{4,0},{1,5},{5,1},{2,6},{6,2},{3,7},{7,3},{8,12},{12,8},{9,1... | collective-permute-start | bytes 98312 | tf_op jit(solution)/shard_map/ppermute | solution.py:246
  126.8 0.6 copy-start.7
  132.9 20.0 %copy-start.4 = (bf16[256,1024]{1,0:T(8,128)(2,1)}, bf16[256,1024]{1,0:T(8,128)(2,1)S(1)}, u32[]{:S(2)}) copy-start(bf16[256,1024]{1,0:T(8,128)(2,1)S(1)} %collective-permute-done.1.neg_b_ref) | copy-start | bytes 1572868
  199.2 6.3 %copy-start.1 = (bf16[512,2176]{1,0:T(8,128)(2,1)}, bf16[512,2176]{1,0:T(8,128)(2,1)S(1)}, u32[]{:S(2)}) copy-start(bf16[512,2176]{1,0:T(8,128)(2,1)S(1)} %convert_element_type.15.own_ref) | copy-start | bytes 6684676
  199.2 6.2 %collective-permute-start.2 = (bf16[512,2176]{1,0:T(8,128)(2,1)S(1)}, bf16[512,2176]{1,0:T(8,128)(2,1)S(1)}, u32[]{:S(2)}, u32[]{:S(2)}) collective-permute-start(bf16[512,2176]{1,0:T(8,128)(2,1)S(1)} %convert_element_type.15.own_ref), channel_id=1, source_target_pairs={{0,4},{4,0},{1,5},{5,1},{2,6},{6,2},{3,7},{7,3},{8,12},{12,8},{9,1... | collective-permute-start | bytes 6684680 | tf_op jit(solution)/shard_map/ppermute | solution.py:274
  205.5 1.4 copy-start.11
  218.9 40.3 %all-to-all-start = ((bf16[16,72,1024]{2,1,0:T(8,128)(2,1)}), bf16[16,72,1024]{2,1,0:T(8,128)(2,1)S(1)}, u32[]{:S(2)}, u32[]{:S(2)}) async-start(bf16[16,72,1024]{2,1,0:T(8,128)(2,1)} %bitcast.31), calls=%async_computation.1 | async-start | bytes 4718592 | tf_op jit(solution)/shard_map/all_to_all | solution.py:294
  259.2 1.4 copy-start
Sparse Core Ops, SparseCore 0:
  15.2 45.3 all-gather.3
  78.3 74.4 reduce-scatter.1

commit v4 on v3

--- a/solution.py
+++ b/solution.py
@@ -55,6 +55,25 @@
     visits = (packed >> 15).astype(f32)
     coefs = visits / jnp.sum(visits, axis=axis, keepdims=True)
     return owner >> 5, owner & 1, (owner >> 1) & 15, row >> 6, row & 63, coefs
+
+
+def embed_kernel(neg_row_ref, table_ref, projection_ref, pre_ref, shared_ref):
+    picks = lax.broadcasted_iota(jnp.int32, (X * 8, ROWS), 0)
+    cols = lax.broadcasted_iota(jnp.int32, (X * 8, ROWS), 1)
+    hot = jnp.zeros((X * 8, ROWS), f32)
+    for i in range(X):
+        hot = hot + jnp.where((picks == 8 * i) & (cols == neg_row_ref[i]), 1.0, 0.0)
+    neg_rows = dot_nn(hot.astype(bf16), table_ref[...]).astype(bf16)
+    neg_pre = dot_nn(neg_rows, projection_ref[...])
+    neg_act = neg_pre * jax.nn.sigmoid(neg_pre)
+    neg_unit = (neg_act / row_norm(neg_act)).astype(bf16)
+    for i in range(X):
+        node_pre = dot_nn(table_ref[i * PART : (i + 1) * PART], projection_ref[...])
+        start = i * BLOCK
+        pre_ref[start : start + PART] = node_pre
+        pre_ref[start + PART : start + BLOCK] = neg_pre[8 * i : 8 * i + 8]
+        shared_ref[start : start + PART] = (node_pre * jax.nn.sigmoid(node_pre)).astype(bf16)
+        shared_ref[start + PART : start + BLOCK] = neg_unit[8 * i : 8 * i + 8]
 
 
 def spread_kernel(where_ref, line_ref, out_ref):
@@ -184,12 +203,12 @@
         out_ref[k * PART : (k + 1) * PART] = block
 
 
-def call(kernel, out_shape, flops, moved, **rest):
+def call(kernel, out_shape, flops, moved, room, **rest):
     return pl.pallas_call(
         kernel,
         out_shape=out_shape,
         cost_estimate=pl.CostEstimate(flops=flops, bytes_accessed=moved, transcendentals=0),
-        compiler_params=pltpu.CompilerParams(vmem_limit_bytes=56 << 20),
+        compiler_params=pltpu.CompilerParams(vmem_limit_bytes=room << 20),
         **rest,
     )
 
@@ -208,27 +227,26 @@
     shifted = jnp.pad(visits, ((0, 0), (3, 0)))
     packed = slot_owner.reshape(query_count, slot_count) + slot_row * 128 + shifted * 32768
 
-    rows = jnp.concatenate(
-        [
-            feature_table.reshape(X, PART, feat_width),
-            feature_table[neg_row].reshape(X, 1, feat_width),
-            jnp.zeros((X, BLOCK - PART - 1, feat_width), bf16),
-        ],
-        axis=1,
-    ).reshape(OWN, feat_width)
-    pre = jnp.dot(rows, projection, preferred_element_type=f32)
-    act = jax.nn.silu(pre)
-    is_neg = (lax.broadcasted_iota(jnp.int32, (OWN, 1), 0) % BLOCK) == PART
-    shared = (act / jnp.where(is_neg, row_norm(act), 1.0)).astype(bf16)
+    pre, shared = call(
+        embed_kernel,
+        (jax.ShapeDtypeStruct((OWN, embed_width), f32), jax.ShapeDtypeStruct((OWN, embed_width), bf16)),
+        2 * OWN * embed_width * feat_width,
+        5 << 20,
+        16,
+        in_specs=[SMEM, VMEM, VMEM],
+        out_specs=(VMEM, VMEM),
+    )(neg_row, feature_table, projection)
     plane = lax.all_gather(shared, ("y", "c"), axis=0, tiled=True)
     my_pre = lax.dynamic_slice_in_dim(pre, x * BLOCK, BLOCK, axis=0)
 
-    line = lax.all_gather(packed, "z", axis=0, tiled=True)
+    copies = jnp.broadcast_to(packed, (Z, query_count, slot_count))
+    line = lax.all_to_all(copies, "z", split_axis=0, concat_axis=0, tiled=True).reshape(line_count, slot_count)
     spread = call(
         spread_kernel,
         jax.ShapeDtypeStruct((Z, 3, query_count, WIDE), bf16),
         line_count * WIDE * 48,
         line_count * WIDE * 6,
+        16,
         grid=(Z,),
         in_specs=[SMEM, pl.BlockSpec((query_count, slot_count), lambda i: (i, 0))],
         out_specs=pl.BlockSpec((1, 3, query_count, WIDE), lambda i: (i, 0, 0, 0)),
@@ -251,14 +269,15 @@
             jax.ShapeDtypeStruct((3, NARROW, line_count), bf16),
             line_count * NARROW * 48,
             line_count * NARROW * 6,
+            12,
             grid=(X,),
             in_specs=[SMEM, pl.BlockSpec((slot_count, line_count), lambda i: (0, 0))],
             out_specs=pl.BlockSpec((3, OWN, line_count), lambda i: (0, i, 0)),
         )(here, some_line.T)
 
     own_w, sib_w = node_weights(line), node_weights(line_sib)
-    got, own_w, sib_w, core_plane, some_neg, other_neg = lax.optimization_barrier(
-        (got, own_w, sib_w, core_plane, some_neg, other_neg)
+    got, own_w, sib_w, core_plane, some_neg, other_neg, my_pre = lax.optimization_barrier(
+        (got, own_w, sib_w, core_plane, some_neg, other_neg, my_pre)
     )
 
     payload_width = 2 * embed_width + 128
@@ -267,6 +286,7 @@
         jax.ShapeDtypeStruct((query_count, payload_width), f32),
         4 * query_count * 512 * embed_width,
         1 << 20,
+        10,
         in_specs=[VMEM] * 3,
         out_specs=VMEM,
     )(got, some_neg, other_neg)
@@ -278,6 +298,7 @@
         jax.ShapeDtypeStruct((NARROW, embed_width), bf16),
         8 * line_count * NARROW * embed_width,
         16 << 20,
+        36,
         grid=(X,),
         in_specs=[
             pl.BlockSpec((3, OWN, line_count), lambda i: (0, i, 0)),
@@ -297,6 +318,7 @@
         jax.ShapeDtypeStruct((BLOCK, embed_width), bf16),
         1 << 22,
         3 << 20,
+        10,
         in_specs=[VMEM] * 2,
         out_specs=VMEM,
     )(pieces.reshape(X * Y, BLOCK, embed_width), my_pre)
@@ -306,6 +328,7 @@
         jax.ShapeDtypeStruct((ROWS, feat_width), f32),
         2 * OWN * embed_width * feat_width,
         4 << 20,
+        16,
         in_specs=[SMEM, VMEM, VMEM],
         out_specs=VMEM,
     )(neg_row, all_pre_grad, projection)

time: 291 us -> 273 us (0.938)
  waiting for transfers between devices: 55.2 us -> 31.4 us
  Pallas kernels: 46 us -> 37.9 us
  local copies, waits for them, and re-layouts: 15.4 us -> 23.1 us
  starting transfers between devices: 14 us -> 21.7 us
  blocking collectives: 125 us -> 131 us
  other arithmetic: 4.96 us -> 1.08 us
    all_to_all x0 -> x1, blocking collectives: none -> 36.6 us  [on_device(): lax.all_to_all(node_grads, ('x', 'y'), split_axis=0, concat_axis=0, tiled...]
    all_gather x1 -> x0, blocking collectives: 36.1 us -> none  [on_device(): line = lax.all_gather(packed, 'z', axis=0, tiled=True)]
    all_to_all x1, waiting for transfers between devices: 30.8 us -> 12.4 us  [on_device(): lax.all_to_all(copies, 'z', split_axis=0, concat_axis=0, tiled=True)]
    all_to_all x1, starting transfers between devices: 7.75 us -> 15.2 us  [on_device(): lax.all_to_all(copies, 'z', split_axis=0, concat_axis=0, tiled=True)]
    all_gather x1, blocking collectives: 32 us -> 38.6 us  [on_device(): some_neg = lax.all_gather(core_neg, 'z', axis=0, tiled=True)]
    reduce_scatter x1, waiting for transfers between devices: 20 us -> 14.7 us  [on_device(): got = lax.psum_scatter(part, 'z', scatter_dimension=0, tiled=True)]
    unnamed x25 -> x35, local copies, waits for them, and re-layouts: 5.24 us -> 9.71 us
    pallas_call x1, Pallas kernels: 12.1 us -> 8.63 us  [on_device(): call(node_grad_kernel, jax.ShapeDtypeStruct((NARROW, embed_width), bf16),...]
  transfers between devices with their start and end apart: 6 -> 6, of which waited for: 3 -> 3; matrix products, arithmetic and copies ran while one was open for 3% -> 6% of each run, Pallas kernels for 8% -> 8%
where the time goes in v4:
time: 273 us; the launch traced here: 272 us
  blocking collectives  131 us (48%)
  Pallas kernels  37.9 us (14%)
  waiting for transfers between devices  31.4 us (12%)
  local copies, waits for them, and re-layouts  23.1 us (8%)
  starting transfers between devices  21.7 us (8%)
  between operations  13.7 us (5%)
  matrix products  12.2 us (4%)
    all_gather x1, blocking collectives, on_device(): lax.all_gather(payload.astype(f16), 'z', axis=0, tiled=True).astype(bf16)  42.5 us
    all_gather x1, blocking collectives, on_device(): some_neg = lax.all_gather(core_neg, 'z', axis=0, tiled=True)  38.6 us
    all_to_all x1, blocking collectives, on_device(): lax.all_to_all(node_grads, ('x', 'y'), split_axis=0, concat_axis=0, tiled...  36.6 us
    all_to_all x1, starting transfers between devices, on_device(): lax.all_to_all(copies, 'z', split_axis=0, concat_axis=0, tiled=True)  15.2 us
    reduce_scatter x1, waiting for transfers between devices, on_device(): got = lax.psum_scatter(part, 'z', scatter_dimension=0, tiled=True)  14.7 us
    all_gather x1, blocking collectives, on_device(): all_pre_grad = lax.all_gather(pre_grad, 'x', axis=0, tiled=True)  13.6 us
    all_to_all x1, waiting for transfers between devices, on_device(): lax.all_to_all(copies, 'z', split_axis=0, concat_axis=0, tiled=True)  12.4 us
    dot_general x1, matrix products, dot_nn(): lax.dot_general(left, right, (((1,), (0,)), ((), ())), preferred_element_...  12.2 us
  transfers between devices with their start and end apart: 6, of which 3 were waited for; matrix products, arithmetic and copies ran while one was open for 6% of the time, Pallas kernels for 8%

profile of v4, /device:TPU:8, one launch (start us, length us, event | category | flops | bytes accessed | tf_op | source)
XLA Modules:
  0.0 272.5 jit_solution(12811733366928442942)
XLA Ops:
  6.5 0.0 all-gather.3.cloned.1.call-start
  6.5 1.6 copy-done
  8.1 1.0 copy-done.7
  9.2 0.7 copy-done.11
  9.8 3.4 %shard_map.65 = (f32[288,1024]{1,0:T(8,128)S(1)}, bf16[288,1024]{1,0:T(8,128)(2,1)}) custom-call(s32[4]{0:T(128)S(1)} %copy-done.11, bf16[256,1024]{1,0:T(8,128)(2,1)S(1)} %copy-done.7, bf16[1024,1024]{1,0:T(8,128)(2,1)S(1)} %copy-done), custom_call_target="tpu_custom_call" | custom-call | flops 603979776 | bytes 5242880 | tf_op jit(solution)/shard_map/pallas_call | solution.py:230
  13.3 0.0 all-gather.3.cloned.1.call-update
  13.3 0.0 copy-done.13
  13.3 0.0 copy-done.14
  13.3 0.0 copy-done.15
  13.3 0.7 reshape.24
  14.1 15.2 %all-to-all-start = ((s32[16,1,512]{2,1,0:T(1,128)}), s32[16,1,512]{2,1,0:T(1,128)S(1)}, u32[]{:S(2)}, u32[]{:S(2)}) async-start(s32[16,1,512]{2,1,0:T(1,128)} %reshape.24), calls=%async_computation | async-start | bytes 65536 | tf_op jit(solution)/shard_map/all_to_all | solution.py:243
  29.3 0.0 reduce-scatter.2.cloned.1.call-start
  29.3 0.1 pad_add_fusion.where_ref
  29.4 12.4 %all-to-all-done = s32[16,1,512]{2,1,0:T(1,128)S(1)} async-done(((s32[16,1,512]{2,1,0:T(1,128)}), s32[16,1,512]{2,1,0:T(1,128)S(1)}, u32[]{:S(2)}, u32[]{:S(2)}) %all-to-all-start) | async-done | bytes 32800 | tf_op jit(solution)/shard_map/all_to_all | solution.py:243
  41.8 0.6 broadcast.2
  42.4 0.7 reduce
  43.1 0.1 reshape.25
  43.3 0.7 reshape.20
  44.0 0.9 copy.11.line_ref
  44.9 11.2 %shard_map.64 = bf16[16,3,32,2304]{3,2,1,0:T(8,128)(2,1)S(1)} custom-call(s32[2]{0:T(128)S(1)} %pad_add_fusion.where_ref, s32[512,16]{1,0:T(8,128)S(1)} %copy.11.line_ref), custom_call_target="tpu_custom_call" | custom-call | flops 56623104 | bytes 7077888 | tf_op jit(solution)/shard_map/pallas_call | solution.py:244
  56.1 0.0 copy-start.2
  56.1 2.9 %copy-done.2 = bf16[16,3,32,2304]{3,2,1,0:T(8,128)(2,1)} copy-done((bf16[16,3,32,2304]{3,2,1,0:T(8,128)(2,1)}, bf16[16,3,32,2304]{3,2,1,0:T(8,128)(2,1)S(1)}, u32[]{:S(2)}) %copy-start.2) | copy-done | bytes 7077912
  59.0 12.2 %convolution_convert_fusion = bf16[1536,1024]{1,0:T(8,128)(2,1)} fusion(bf16[1536,2304]{1,0:T(8,128)(2,1)} %bitcast.23, bf16[2304,1024]{1,0:T(8,128)(2,1)} %all-gather.3.cloned.1.call-done), kind=kOutput, calls=%fused_computation | convolution fusion | flops 7249330176 | bytes 14942208 | tf_op jit(solution)/shard_map/dot_general | solution.py:45
  71.2 0.0 reduce-scatter.2.cloned.1.call-update
  71.2 2.0 constant_dynamic-slice_fusion.1
  73.2 3.3 %copy.15 = bf16[4,1,4,72,1024]{4,0,2,3,1:T(4,128)(2,1)} copy(bf16[4,1,4,72,1024]{4,3,2,1,0:T(8,128)(2,1)S(1)} %constant_dynamic-slice_fusion.1) | data formatting | bytes 4718592 | tf_op jit(solution)/shard_map/jit(dynamic_index_in_dim)/dynamic_slice | solution.py:258
  76.5 0.8 slice.4
  77.3 0.0 copy-start.9
  77.3 38.6 %all_gather.13.neg_a_ref = bf16[256,1024]{1,0:T(8,128)(2,1)} all-gather(bf16[16,1024]{1,0:T(8,128)(2,1)S(1)} %reshape_squeeze.3.neg_ref), channel_id=1, replica_groups=mesh['y'=4,'z'=16,'c'=2,'x'=4] {'z'}, dimensions={0}, use_global_device_ids=true | all-gather | bytes 557056 | tf_op jit(solution)/shard_map/all_gather | solution.py:262
  115.9 1.9 collective-permute-start.1
  117.8 2.6 collective-permute-start
  120.4 0.7 constant_dynamic-slice_fusion.pre_ref
  121.2 4.4 %copy.13 = bf16[4,4,72,1024]{3,2,1,0:T(8,128)(2,1)} copy(bf16[4,4,72,1024]{3,1,0,2:T(4,128)(2,1)} %bitcast.22) | data formatting | bytes 4718592 | tf_op jit(solution)/shard_map/transpose | solution.py:259
  125.5 0.0 copy-done.9
  125.5 4.8 %shard_map.66.own_w_ref = bf16[3,1152,512]{2,1,0:T(8,128)(2,1)S(1)} custom-call(s32[2]{0:T(128)S(1)} %pad_add_fusion.where_ref, s32[16,512]{1,0:T(8,128)} %bitcast.4.line_ref), custom_call_target="tpu_custom_call" | custom-call | flops 28311552 | bytes 3538944 | tf_op jit(solution)/shard_map/pallas_call | solution.py:267
  130.4 0.0 collective-permute-done
  130.4 4.6 %shard_map.67.sib_w_ref = bf16[3,1152,512]{2,1,0:T(8,128)(2,1)S(1)} custom-call(s32[2]{0:T(128)S(1)} %pad_add_fusion.where_ref, s32[16,512]{1,0:T(8,128)S(1)} %bitcast.26), custom_call_target="tpu_custom_call" | custom-call | flops 28311552 | bytes 3538944 | tf_op jit(solution)/shard_map/pallas_call | solution.py:267
  135.0 0.0 copy-start.3
  135.0 1.8 copy-done.3
  136.7 0.0 collective-permute-done.1.neg_b_ref
  136.8 14.7 %reduce-scatter.2.cloned.1.call-done.got_ref = bf16[96,1024]{1,0:T(8,128)(2,1)} async-done(((bf16[1536,1024]{1,0:T(8,128)(2,1)}), bf16[96,1024]{1,0:T(8,128)(2,1)}) %reduce-scatter.2.cloned.1.call-update) | async-done | bytes 196624 | tf_op jit(solution)/shard_map/reduce_scatter | solution.py:256
  151.4 0.9 copy-done.8
  152.3 2.0 shard_map.68
  154.4 0.0 copy-start.4
  154.4 0.0 copy-start.5
  154.4 0.0 copy-start.10
  154.4 42.5 %all-gather.4 = f16[512,2176]{1,0:T(8,128)(2,1)S(1)} all-gather(f16[32,2176]{1,0:T(8,128)(2,1)S(1)} %convert_element_type.10), channel_id=1, replica_groups=mesh['y'=4,'z'=16,'c'=2,'x'=4] {'z'}, dimensions={0}, use_global_device_ids=true | all-gather | bytes 2367488 | tf_op jit(solution)/shard_map/all_gather | solution.py:293
  196.9 0.3 convert_element_type.11.own_ref
  197.2 1.9 collective-permute-start.2
  199.1 4.3 %collective-permute-done.2.sib_ref = bf16[512,2176]{1,0:T(8,128)(2,1)S(1)} collective-permute-done((bf16[512,2176]{1,0:T(8,128)(2,1)S(1)}, bf16[512,2176]{1,0:T(8,128)(2,1)S(1)}, u32[]{:S(2)}, u32[]{:S(2)}) %collective-permute-start.2) | collective-permute-done | bytes 2228256 | tf_op jit(solution)/shard_map/ppermute | solution.py:294
  203.4 0.0 copy-done.4
  203.5 0.0 copy-done.5
  203.5 0.0 copy-done.10
  203.5 8.6 %shard_map.69 = bf16[1152,1024]{1,0:T(8,128)(2,1)S(1)} custom-call(bf16[3,1152,512]{2,1,0:T(8,128)(2,1)S(1)} %shard_map.66.own_w_ref, bf16[3,1152,512]{2,1,0:T(8,128)(2,1)S(1)} %copy-done.4, bf16[512,2176]{1,0:T(8,128)(2,1)S(1)} %convert_element_type.11.own_ref, bf16[512,2176]{1,0:T(8,128)(2,1)S(1)} %collective-permute-done.2.sib_ref, ...), custom_call_target="tpu_custom_call" | custom-call | flops 4831838208 | bytes 16777216 | tf_op jit(solution)/shard_map/pallas_call | solution.py:296
  212.1 0.0 copy-start.6
  212.1 0.0 copy-start.1
  212.1 0.0 copy-start.12
  212.1 36.6 %all_to_all.14.pieces_ref = bf16[16,72,1024]{2,1,0:T(8,128)(2,1)S(1)} all-to-all(bf16[16,72,1024]{2,1,0:T(8,128)(2,1)S(1)} %bitcast.25), channel_id=1, replica_groups=mesh['y'=4,'z'=16,'c'=2,'x'=4] {'x','y'}, dimensions={0} | all-to-all | bytes 4718592 | tf_op jit(solution)/shard_map/all_to_all | solution.py:315
  248.8 0.0 copy-done.6
  248.8 0.5 shard_map.70
  249.3 13.6 %all_gather.15.grad_ref = bf16[288,1024]{1,0:T(8,128)(2,1)S(1)} all-gather(bf16[72,1024]{1,0:T(8,128)(2,1)S(1)} %shard_map.70), channel_id=1, replica_groups=mesh['y'=4,'z'=16,'c'=2,'x'=4] {'x'}, dimensions={0}, use_global_device_ids=true | all-gather | bytes 737280 | tf_op jit(solution)/shard_map/all_gather | solution.py:325
  262.9 0.0 copy-done.1
  262.9 0.0 copy-done.12
  262.9 2.7 shard_map.71
  (13 shorter events, 0.1 us)
Async XLA Ops:
  6.5 52.4 %all-gather.3.cloned.1.call-start = ((), (), s32[]{:S(2)}) async-start(), calls=%async_computation.3 | async-start | bytes 5308416 | tf_op jit(solution)/shard_map/all_gather | solution.py:239
  6.5 1.6 copy-start
  8.1 1.0 copy-start.7
  9.2 0.7 copy-start.11
  9.8 3.5 %copy-start.13 = (s32[32,13]{0,1:T(8,128)S(1)}, s32[32,13]{0,1:T(8,128)}, u32[]{:S(2)}) copy-start(s32[32,13]{0,1:T(8,128)} %param.10) | copy-start | bytes 4996
  9.8 3.5 %copy-start.14 = (s32[32,16,1]{0,2,1:T(1,128)S(1)}, s32[32,16,1]{0,2,1:T(1,128)}, u32[]{:S(2)}) copy-start(s32[32,16,1]{0,2,1:T(1,128)} %param.8) | copy-start | bytes 6148
  9.8 3.5 %copy-start.15 = (s32[32,16]{0,1:T(8,128)S(1)}, s32[32,16]{0,1:T(8,128)}, u32[]{:S(2)}) copy-start(s32[32,16]{0,1:T(8,128)} %param.9) | copy-start | bytes 6148
  14.1 27.8 %all-to-all-start = ((s32[16,1,512]{2,1,0:T(1,128)}), s32[16,1,512]{2,1,0:T(1,128)S(1)}, u32[]{:S(2)}, u32[]{:S(2)}) async-start(s32[16,1,512]{2,1,0:T(1,128)} %reshape.24), calls=%async_computation | async-start | bytes 65536 | tf_op jit(solution)/shard_map/all_to_all | solution.py:243
  29.3 122.1 %reduce-scatter.2.cloned.1.call-start = ((), (), s32[]{:S(2)}) async-start(), calls=%async_computation.4 | async-start | bytes 3342336 | tf_op jit(solution)/shard_map/reduce_scatter | solution.py:256
  56.1 2.9 %copy-start.2 = (bf16[16,3,32,2304]{3,2,1,0:T(8,128)(2,1)}, bf16[16,3,32,2304]{3,2,1,0:T(8,128)(2,1)S(1)}, u32[]{:S(2)}) copy-start(bf16[16,3,32,2304]{3,2,1,0:T(8,128)(2,1)S(1)} %shard_map.64) | copy-start | bytes 21233668
  77.3 48.3 %copy-start.9 = (bf16[16,1024]{1,0:T(8,128)(2,1)}, bf16[16,1024]{1,0:T(8,128)(2,1)S(1)}, u32[]{:S(2)}) copy-start(bf16[16,1024]{1,0:T(8,128)(2,1)S(1)} %reshape_squeeze.3.neg_ref) | copy-start | bytes 98308
  115.9 20.8 %collective-permute-start.1 = (bf16[256,1024]{1,0:T(8,128)(2,1)}, bf16[256,1024]{1,0:T(8,128)(2,1)}, u32[]{:S(2)}, u32[]{:S(2)}) collective-permute-start(bf16[256,1024]{1,0:T(8,128)(2,1)} %all_gather.13.neg_a_ref), channel_id=1, source_target_pairs={{0,4},{4,0},{1,5},{5,1},{2,6},{6,2},{3,7},{7,3},{8,12},{12,8},{9,1... | collective-permute-start | bytes 1572872 | tf_op jit(solution)/shard_map/ppermute | solution.py:263
  117.8 12.5 %collective-permute-start = (s32[512,16]{0,1:T(8,128)}, s32[512,16]{0,1:T(8,128)S(1)}, u32[]{:S(2)}, u32[]{:S(2)}) collective-permute-start(s32[512,16]{0,1:T(8,128)} %reshape.20), channel_id=1, source_target_pairs={{0,4},{4,0},{1,5},{5,1},{2,6},{6,2},{3,7},{7,3},{8,12},{12,8},{9,1... | collective-permute-start | bytes 98312 | tf_op jit(solution)/shard_map/ppermute | solution.py:264
  135.0 1.8 copy-start.3
  151.4 0.9 copy-start.8
  154.4 49.0 %copy-start.4 = (bf16[3,1152,512]{2,1,0:T(8,128)(2,1)S(1)}, bf16[3,1152,512]{2,1,0:T(8,128)(2,1)}, u32[]{:S(2)}) copy-start(bf16[3,1152,512]{2,1,0:T(8,128)(2,1)} %copy-done.3) | copy-start | bytes 10616836
  154.4 49.0 %copy-start.5 = (bf16[4,4,72,1024]{3,2,1,0:T(8,128)(2,1)S(1)}, bf16[4,4,72,1024]{3,2,1,0:T(8,128)(2,1)}, u32[]{:S(2)}) copy-start(bf16[4,4,72,1024]{3,2,1,0:T(8,128)(2,1)} %copy.13) | copy-start | bytes 7077892
  154.4 49.0 %copy-start.10 = (bf16[16,1024]{1,0:T(8,128)(2,1)S(1)}, bf16[16,1024]{1,0:T(8,128)(2,1)}, u32[]{:S(2)}) copy-start(bf16[16,1024]{1,0:T(8,128)(2,1)} %copy-done.9) | copy-start | bytes 98308
  197.2 6.2 %collective-permute-start.2 = (bf16[512,2176]{1,0:T(8,128)(2,1)S(1)}, bf16[512,2176]{1,0:T(8,128)(2,1)S(1)}, u32[]{:S(2)}, u32[]{:S(2)}) collective-permute-start(bf16[512,2176]{1,0:T(8,128)(2,1)S(1)} %convert_element_type.11.own_ref), channel_id=1, source_target_pairs={{0,4},{4,0},{1,5},{5,1},{2,6},{6,2},{3,7},{7,3},{8,12},{12,8},{9,1... | collective-permute-start | bytes 6684680 | tf_op jit(solution)/shard_map/ppermute | solution.py:294
  212.1 36.7 %copy-start.6 = (f32[72,1024]{1,0:T(8,128)S(1)}, f32[72,1024]{1,0:T(8,128)}, u32[]{:S(2)}) copy-start(f32[72,1024]{1,0:T(8,128)} %constant_dynamic-slice_fusion.pre_ref) | copy-start | bytes 884740
  212.1 50.8 %copy-start.1 = (bf16[1024,1024]{1,0:T(8,128)(2,1)S(1)}, bf16[1024,1024]{1,0:T(8,128)(2,1)}, u32[]{:S(2)}) copy-start(bf16[1024,1024]{1,0:T(8,128)(2,1)} %projection_ref.3) | copy-start | bytes 6291460
  212.1 50.8 %copy-start.12 = (s32[4]{0:T(128)S(1)}, s32[4]{0:T(128)}, u32[]{:S(2)}) copy-start(s32[4]{0:T(128)} %neg_row_ref.3) | copy-start | bytes 52
Sparse Core Ops, SparseCore 0:
  13.4 45.3 all-gather.2
  71.3 80.0 reduce-scatter.1

commit v5 on v4

--- a/solution.py
+++ b/solution.py
@@ -87,9 +87,9 @@
         for slot in range(3, slots):
             total = total + jnp.where(lanes == column[:, slot : slot + 1], coefs[:, slot : slot + 1], 0.0)
         span = pl.ds(k * chunk, chunk)
-        out_ref[0, 0, :, span] = total.astype(bf16)
-        out_ref[0, 1, :, span] = jnp.where(lanes == column[:, 1:2], 1.0, 0.0).astype(bf16)
-        out_ref[0, 2, :, span] = jnp.where(lanes == column[:, 2:3], 1.0, 0.0).astype(bf16)
+        out_ref[0, :, span] = total.astype(bf16)
+        out_ref[1, :, span] = jnp.where(lanes == column[:, 1:2], 1.0, 0.0).astype(bf16)
+        out_ref[2, :, span] = jnp.where(lanes == column[:, 2:3], 1.0, 0.0).astype(bf16)
 
 
 def node_weights_kernel(where_ref, line_ref, out_ref):
@@ -110,16 +110,15 @@
         out_ref[2, span, :] = jnp.where(nodes == column[2:3], 1.0, 0.0).astype(bf16)
 
 
-def query_kernel(got_ref, neg_a_ref, neg_b_ref, out_ref):
-    count = got_ref.shape[0] // 3
-    width = got_ref.shape[1]
-    hood = got_ref[0:count].astype(f32)
+def query_kernel(where_ref, got_ref, neg_a_ref, neg_b_ref, out_ref):
+    count, width = got_ref.shape[1:]
+    hood = got_ref[0].astype(f32)
     query_norm = row_norm(hood)
     query_unit = hood / query_norm
     query_embed = query_unit.astype(bf16)
     query_float = query_embed.astype(f32)
-    first = got_ref[count : 2 * count].astype(f32)
-    second = got_ref[2 * count :].astype(f32)
+    first = got_ref[1].astype(f32)
+    second = got_ref[2].astype(f32)
     first_norm, second_norm = row_norm(first), row_norm(second)
     first_embed = (first / first_norm).astype(bf16).astype(f32)
     second_embed = (second / second_norm).astype(bf16).astype(f32)
@@ -132,32 +131,40 @@
     grad = grad - query_unit * row_sum(query_unit * grad)
     power = jnp.exp(jnp.ceil(jnp.log(query_norm) * (1.0 / log_two)) * log_two).astype(bf16).astype(f32)
     inverse = (16.0 / power).astype(bf16).astype(f32)
-    out_ref[:, 0:width] = grad * (power / query_norm)
-    out_ref[:, width : 2 * width] = query_float
+    out_ref[0:count] = grad * (power / query_norm)
+    out_ref[count : 2 * count] = query_float
     lanes = lax.broadcasted_iota(jnp.int32, (count, 128), 1)
     scalars = jnp.where(lanes == 0, inverse, 0.0)
     for place, value in ((1, total), (3, hard), (5, first_norm), (7, second_norm), (9, positive)):
         high = value.astype(bf16).astype(f32)
         scalars = jnp.where(lanes == place, high, scalars)
         scalars = jnp.where(lanes == place + 1, value - high, scalars)
-    out_ref[:, 2 * width :] = scalars
+    line_count = Z * count
+    spots = lax.broadcasted_iota(jnp.int32, (count, line_count), 0) + where_ref[0] * count
+    spots = jnp.where(spots == lax.broadcasted_iota(jnp.int32, (count, line_count), 1), 1.0, 0.0)
+    across = dot_nn(scalars.T[0:16].astype(bf16), spots.astype(bf16))
+    out_ref[2 * count : 2 * count + 8, 0:line_count] = across[0:8]
+    out_ref[2 * count : 2 * count + 8, line_count : 2 * line_count] = across[8:16]
 
 
 def node_grad_kernel(own_w_ref, sib_w_ref, own_ref, sib_ref, plane_ref, neg_ref, out_ref, row_ref, neg_w_ref):
     step = pl.program_id(0)
     width = plane_ref.shape[1]
+    count = (own_ref.shape[1] - 8) // 2
+    line_count = Z * count
     received = (own_ref, sib_ref)
 
     @pl.when(step == 0)
     def _():
         for side, ref in enumerate(received):
-            scalars = ref[:, 2 * width :].astype(f32).T
+            spread = jnp.sum(ref[:, 2 * count : 2 * count + 8].astype(f32), axis=0)
+            scalars = jnp.concatenate([spread[:, :line_count], spread[:, line_count:]], axis=0)
             total = scalars[1:2] + scalars[2:3]
             hard = scalars[3:4] + scalars[4:5]
             row_ref[side, 0:1] = scalars[0:1] * 0.0625
             row_ref[side, 1:2] = -total / (scalars[5:6] + scalars[6:7])
             row_ref[side, 2:3] = hard / (scalars[7:8] + scalars[8:9])
-            scores = dot_nt(neg_ref[...], ref[:, width : 2 * width])
+            scores = dot_nt(neg_ref[...], ref[:, count : 2 * count].reshape(line_count, width))
             neg_w_ref[side] = weigh(scores, scalars[9:10] + scalars[10:11])
 
     negs = neg_ref.shape[0]
@@ -167,10 +174,10 @@
     query_part = jnp.zeros((OWN, width), f32)
     for side, (w_ref, ref) in enumerate(((own_w_ref, own_ref), (sib_w_ref, sib_ref))):
         w_hood = (w_ref[0].astype(f32) * row_ref[side, 0:1]).astype(bf16)
-        hood_part = hood_part + dot_nn(w_hood, ref[:, 0:width])
+        hood_part = hood_part + dot_nn(w_hood, ref[:, 0:count].reshape(line_count, width))
         w_query = w_ref[1].astype(f32) * row_ref[side, 1:2] + w_ref[2].astype(f32) * row_ref[side, 2:3]
         w_query = (w_query + dot_nn(spot, neg_w_ref[side])).astype(bf16)
-        query_part = query_part + dot_nn(w_query, ref[:, width : 2 * width])
+        query_part = query_part + dot_nn(w_query, ref[:, count : 2 * count].reshape(line_count, width))
     plane = plane_ref[...].astype(f32)
     place = lax.broadcasted_iota(jnp.int32, (OWN, 1), 0) % BLOCK
     inverse = jnp.where(place == PART, 0.0, 1.0 / (row_sum(plane * plane) + epsilon))
@@ -243,17 +250,19 @@
     line = lax.all_to_all(copies, "z", split_axis=0, concat_axis=0, tiled=True).reshape(line_count, slot_count)
     spread = call(
         spread_kernel,
-        jax.ShapeDtypeStruct((Z, 3, query_count, WIDE), bf16),
+        jax.ShapeDtypeStruct((3, line_count, WIDE), bf16),
         line_count * WIDE * 48,
         line_count * WIDE * 6,
         16,
         grid=(Z,),
         in_specs=[SMEM, pl.BlockSpec((query_count, slot_count), lambda i: (i, 0))],
-        out_specs=pl.BlockSpec((1, 3, query_count, WIDE), lambda i: (i, 0, 0, 0)),
+        out_specs=pl.BlockSpec((3, query_count, WIDE), lambda i: (0, i, 0)),
     )(here, line)
     part = dot_nn(spread.reshape(3 * line_count, WIDE), plane).astype(bf16)
     part, plane, line = lax.optimization_barrier((part, plane, line))
-    got = lax.psum_scatter(part, "z", scatter_dimension=0, tiled=True)
+    got = lax.psum_scatter(
+        part.reshape(3, line_count, embed_width), "z", scatter_dimension=1, tiled=True
+    )
 
     core_plane = lax.dynamic_index_in_dim(plane.reshape(Y, C, X, BLOCK, embed_width), c, axis=1, keepdims=False)
     core_plane = core_plane.transpose(1, 0, 2, 3)
@@ -280,17 +289,18 @@
         (got, own_w, sib_w, core_plane, some_neg, other_neg, my_pre)
     )
 
-    payload_width = 2 * embed_width + 128
+    payload_rows = 2 * query_count + 8
     payload = call(
         query_kernel,
-        jax.ShapeDtypeStruct((query_count, payload_width), f32),
+        jax.ShapeDtypeStruct((payload_rows, embed_width), f32),
         4 * query_count * 512 * embed_width,
         1 << 20,
         10,
-        in_specs=[VMEM] * 3,
+        in_specs=[SMEM] + [VMEM] * 3,
         out_specs=VMEM,
-    )(got, some_neg, other_neg)
+    )(here, got, some_neg, other_neg)
     own = lax.all_gather(payload.astype(f16), "z", axis=0, tiled=True).astype(bf16)
+    own = own.reshape(Z, payload_rows, embed_width)
     sib = lax.ppermute(own, "c", SIBLING)
 
     node_grads = call(
@@ -303,8 +313,8 @@
         in_specs=[
             pl.BlockSpec((3, OWN, line_count), lambda i: (0, i, 0)),
             pl.BlockSpec((3, OWN, line_count), lambda i: (0, i, 0)),
-            pl.BlockSpec((line_count, payload_width), lambda i: (0, 0)),
-            pl.BlockSpec((line_count, payload_width), lambda i: (0, 0)),
+            pl.BlockSpec((Z, payload_rows, embed_width), lambda i: (0, 0, 0)),
+            pl.BlockSpec((Z, payload_rows, embed_width), lambda i: (0, 0, 0)),
             pl.BlockSpec((OWN, embed_width), lambda i: (i, 0)),
             pl.BlockSpec((X * Y, embed_width), lambda i: (0, 0)),
         ],

time: 273 us -> 276 us (1.011)
  transfers between devices with their start and end apart: 6 -> 6, of which waited for: 3 -> 3; matrix products, arithmetic and copies ran while one was open for 6% -> 5% of each run, Pallas kernels for 8% -> 8%
where the time goes in v5:
time: 276 us; the launch traced here: 275 us
  blocking collectives  133 us (48%)
  Pallas kernels  38.4 us (14%)
  waiting for transfers between devices  31.3 us (11%)
  local copies, waits for them, and re-layouts  23.1 us (8%)
  starting transfers between devices  21.7 us (8%)
  between operations  13.7 us (5%)
  matrix products  12.2 us (4%)
    all_gather x1, blocking collectives, on_device(): lax.all_gather(payload.astype(f16), 'z', axis=0, tiled=True).astype(bf16)  43.9 us
    all_gather x1, blocking collectives, on_device(): some_neg = lax.all_gather(core_neg, 'z', axis=0, tiled=True)  38.5 us
    all_to_all x1, blocking collectives, on_device(): lax.all_to_all(node_grads, ('x', 'y'), split_axis=0, concat_axis=0, tiled...  37.1 us
    all_to_all x1, starting transfers between devices, on_device(): lax.all_to_all(copies, 'z', split_axis=0, concat_axis=0, tiled=True)  15.2 us
    reduce_scatter x1, waiting for transfers between devices, on_device(): lax.psum_scatter(part.reshape(3, line_count, embed_width), 'z', scatter_d...  14.3 us
    all_gather x1, blocking collectives, on_device(): all_pre_grad = lax.all_gather(pre_grad, 'x', axis=0, tiled=True)  13.6 us
    all_to_all x1, waiting for transfers between devices, on_device(): lax.all_to_all(copies, 'z', split_axis=0, concat_axis=0, tiled=True)  12.4 us
    dot_general x1, matrix products, dot_nn(): lax.dot_general(left, right, (((1,), (0,)), ((), ())), preferred_element_...  12.2 us
  transfers between devices with their start and end apart: 6, of which 3 were waited for; matrix products, arithmetic and copies ran while one was open for 5% of the time, Pallas kernels for 8%

profile of v5, /device:TPU:8, one launch (start us, length us, event | category | flops | bytes accessed | tf_op | source)
XLA Modules:
  0.0 275.0 jit_solution(16268011014845957127)
XLA Ops:
  6.5 0.0 all-gather.3.cloned.1.call-start
  6.5 1.6 copy-done
  8.1 1.0 copy-done.7
  9.2 0.7 copy-done.11
  9.8 3.4 %shard_map.65 = (f32[288,1024]{1,0:T(8,128)S(1)}, bf16[288,1024]{1,0:T(8,128)(2,1)}) custom-call(s32[4]{0:T(128)S(1)} %copy-done.11, bf16[256,1024]{1,0:T(8,128)(2,1)S(1)} %copy-done.7, bf16[1024,1024]{1,0:T(8,128)(2,1)S(1)} %copy-done), custom_call_target="tpu_custom_call" | custom-call | flops 603979776 | bytes 5242880 | tf_op jit(solution)/shard_map/pallas_call | solution.py:237
  13.3 0.0 all-gather.3.cloned.1.call-update
  13.3 0.0 copy-done.13
  13.3 0.0 copy-done.14
  13.3 0.0 copy-done.15
  13.3 0.7 reshape.32
  14.1 15.2 %all-to-all-start = ((s32[16,1,512]{2,1,0:T(1,128)}), s32[16,1,512]{2,1,0:T(1,128)S(1)}, u32[]{:S(2)}, u32[]{:S(2)}) async-start(s32[16,1,512]{2,1,0:T(1,128)} %reshape.32), calls=%async_computation | async-start | bytes 65536 | tf_op jit(solution)/shard_map/all_to_all | solution.py:250
  29.3 0.0 reduce-scatter.2.cloned.1.call-start
  29.3 0.1 pad_add_fusion.where_ref
  29.4 12.4 %all-to-all-done = s32[16,1,512]{2,1,0:T(1,128)S(1)} async-done(((s32[16,1,512]{2,1,0:T(1,128)}), s32[16,1,512]{2,1,0:T(1,128)S(1)}, u32[]{:S(2)}, u32[]{:S(2)}) %all-to-all-start) | async-done | bytes 32800 | tf_op jit(solution)/shard_map/all_to_all | solution.py:250
  41.8 0.6 broadcast.2
  42.4 0.7 reduce
  43.1 0.1 reshape.33
  43.3 0.7 reshape.26
  44.0 0.9 copy.11.line_ref
  44.9 11.6 %shard_map.64 = bf16[3,512,2304]{2,1,0:T(8,128)(2,1)S(1)} custom-call(s32[2]{0:T(128)S(1)} %pad_add_fusion.where_ref, s32[512,16]{1,0:T(8,128)S(1)} %copy.11.line_ref), custom_call_target="tpu_custom_call" | custom-call | flops 56623104 | bytes 7077888 | tf_op jit(solution)/shard_map/pallas_call | solution.py:251
  56.5 0.0 copy-start.2
  56.5 2.9 %copy-done.2 = bf16[3,512,2304]{2,1,0:T(8,128)(2,1)} copy-done((bf16[3,512,2304]{2,1,0:T(8,128)(2,1)}, bf16[3,512,2304]{2,1,0:T(8,128)(2,1)S(1)}, u32[]{:S(2)}) %copy-start.2) | copy-done | bytes 7077912
  59.4 12.2 %convolution_convert_fusion = bf16[1536,1024]{1,0:T(8,128)(2,1)} fusion(bf16[1536,2304]{1,0:T(8,128)(2,1)} %bitcast.25, bf16[2304,1024]{1,0:T(8,128)(2,1)} %all-gather.3.cloned.1.call-done), kind=kOutput, calls=%fused_computation | convolution fusion | flops 7249330176 | bytes 14942208 | tf_op jit(solution)/shard_map/dot_general | solution.py:45
  71.6 0.0 reduce-scatter.2.cloned.1.call-update
  71.6 2.0 constant_dynamic-slice_fusion.1
  73.6 3.3 %copy.15 = bf16[4,1,4,72,1024]{4,0,2,3,1:T(4,128)(2,1)} copy(bf16[4,1,4,72,1024]{4,3,2,1,0:T(8,128)(2,1)S(1)} %constant_dynamic-slice_fusion.1) | data formatting | bytes 4718592 | tf_op jit(solution)/shard_map/jit(dynamic_index_in_dim)/dynamic_slice | solution.py:267
  76.9 0.8 slice.4
  77.7 0.0 copy-start.9
  77.7 38.5 %all_gather.13.neg_a_ref = bf16[256,1024]{1,0:T(8,128)(2,1)} all-gather(bf16[16,1024]{1,0:T(8,128)(2,1)S(1)} %reshape_squeeze.3.neg_ref), channel_id=1, replica_groups=mesh['y'=4,'z'=16,'c'=2,'x'=4] {'z'}, dimensions={0}, use_global_device_ids=true | all-gather | bytes 557056 | tf_op jit(solution)/shard_map/all_gather | solution.py:271
  116.2 1.9 collective-permute-start.1
  118.1 2.6 collective-permute-start
  120.7 0.7 constant_dynamic-slice_fusion.pre_ref
  121.4 4.4 %copy.13 = bf16[4,4,72,1024]{3,2,1,0:T(8,128)(2,1)} copy(bf16[4,4,72,1024]{3,1,0,2:T(4,128)(2,1)} %bitcast.24) | data formatting | bytes 4718592 | tf_op jit(solution)/shard_map/transpose | solution.py:268
  125.8 0.0 copy-done.9
  125.8 4.8 %shard_map.66.own_w_ref = bf16[3,1152,512]{2,1,0:T(8,128)(2,1)S(1)} custom-call(s32[2]{0:T(128)S(1)} %pad_add_fusion.where_ref, s32[16,512]{1,0:T(8,128)} %bitcast.5.line_ref), custom_call_target="tpu_custom_call" | custom-call | flops 28311552 | bytes 3538944 | tf_op jit(solution)/shard_map/pallas_call | solution.py:276
  130.6 0.0 collective-permute-done
  130.6 4.6 %shard_map.67.sib_w_ref = bf16[3,1152,512]{2,1,0:T(8,128)(2,1)S(1)} custom-call(s32[2]{0:T(128)S(1)} %pad_add_fusion.where_ref, s32[16,512]{1,0:T(8,128)S(1)} %bitcast.30), custom_call_target="tpu_custom_call" | custom-call | flops 28311552 | bytes 3538944 | tf_op jit(solution)/shard_map/pallas_call | solution.py:276
  135.3 0.0 copy-start.3
  135.3 1.8 copy-done.3
  137.0 0.0 collective-permute-done.1.neg_b_ref
  137.0 14.3 %reduce-scatter.2.cloned.1.call-done.got_ref = bf16[3,32,1024]{2,1,0:T(8,128)(2,1)} async-done(((bf16[3,512,1024]{2,1,0:T(8,128)(2,1)}), bf16[3,32,1024]{2,1,0:T(8,128)(2,1)}) %reduce-scatter.2.cloned.1.call-update) | async-done | bytes 196624 | tf_op jit(solution)/shard_map/reduce_scatter | solution.py:263
  151.4 0.9 copy-done.8
  152.3 2.0 shard_map.68
  154.4 0.0 copy-start.4
  154.4 0.0 copy-start.5
  154.4 0.0 copy-start.10
  154.4 43.9 %all-gather.4 = f16[1152,1024]{1,0:T(8,128)(2,1)S(1)} all-gather(f16[72,1024]{1,0:T(8,128)(2,1)S(1)} %convert_element_type.10), channel_id=1, replica_groups=mesh['y'=4,'z'=16,'c'=2,'x'=4] {'z'}, dimensions={0}, use_global_device_ids=true | all-gather | bytes 2506752 | tf_op jit(solution)/shard_map/all_gather | solution.py:302
  198.3 0.6 convert_element_type.11
  199.0 1.9 collective-permute-start.2
  200.9 4.5 %collective-permute-done.2.sib_ref = bf16[16,72,1024]{2,1,0:T(8,128)(2,1)S(1)} collective-permute-done((bf16[16,72,1024]{2,1,0:T(8,128)(2,1)S(1)}, bf16[16,72,1024]{2,1,0:T(8,128)(2,1)S(1)}, u32[]{:S(2)}, u32[]{:S(2)}) %collective-permute-start.2) | collective-permute-done | bytes 2359328 | tf_op jit(solution)/shard_map/ppermute | solution.py:304
  205.4 0.0 copy-done.4
  205.4 0.0 copy-done.5
  205.4 0.0 copy-done.10
  205.4 8.7 %shard_map.69 = bf16[1152,1024]{1,0:T(8,128)(2,1)S(1)} custom-call(bf16[3,1152,512]{2,1,0:T(8,128)(2,1)S(1)} %shard_map.66.own_w_ref, bf16[3,1152,512]{2,1,0:T(8,128)(2,1)S(1)} %copy-done.4, bf16[16,72,1024]{2,1,0:T(8,128)(2,1)S(1)} %bitcast.28, bf16[16,72,1024]{2,1,0:T(8,128)(2,1)S(1)} %collective-permute-done.2.sib_ref, bf16[1152,1024]{1,0:T(8,128)(2,1)S(1)} %bitcast.26, ...), custom_call_target="tpu_custom_call" | custom-call | flops 4831838208 | bytes 16777216 | tf_op jit(solution)/shard_map/pallas_call | solution.py:306
  214.1 0.0 copy-start.6
  214.1 0.0 copy-start.1
  214.2 0.0 copy-start.12
  214.2 37.1 %all_to_all.14.pieces_ref = bf16[16,72,1024]{2,1,0:T(8,128)(2,1)S(1)} all-to-all(bf16[16,72,1024]{2,1,0:T(8,128)(2,1)S(1)} %bitcast.29), channel_id=1, replica_groups=mesh['y'=4,'z'=16,'c'=2,'x'=4] {'x','y'}, dimensions={0} | all-to-all | bytes 4718592 | tf_op jit(solution)/shard_map/all_to_all | solution.py:325
  251.3 0.0 copy-done.6
  251.3 0.5 shard_map.70
  251.8 13.6 %all_gather.15.grad_ref = bf16[288,1024]{1,0:T(8,128)(2,1)S(1)} all-gather(bf16[72,1024]{1,0:T(8,128)(2,1)S(1)} %shard_map.70), channel_id=1, replica_groups=mesh['y'=4,'z'=16,'c'=2,'x'=4] {'x'}, dimensions={0}, use_global_device_ids=true | all-gather | bytes 737280 | tf_op jit(solution)/shard_map/all_gather | solution.py:335
  265.4 0.0 copy-done.1
  265.4 0.0 copy-done.12
  265.4 2.7 shard_map.71
  (13 shorter events, 0.1 us)
Async XLA Ops:
  6.5 52.8 %all-gather.3.cloned.1.call-start = ((), (), s32[]{:S(2)}) async-start(), calls=%async_computation.3 | async-start | bytes 5308416 | tf_op jit(solution)/shard_map/all_gather | solution.py:246
  6.5 1.6 copy-start
  8.1 1.0 copy-start.7
  9.2 0.7 copy-start.11
  9.8 3.5 %copy-start.13 = (s32[32,13]{0,1:T(8,128)S(1)}, s32[32,13]{0,1:T(8,128)}, u32[]{:S(2)}) copy-start(s32[32,13]{0,1:T(8,128)} %param.10) | copy-start | bytes 4996
  9.8 3.5 %copy-start.14 = (s32[32,16,1]{0,2,1:T(1,128)S(1)}, s32[32,16,1]{0,2,1:T(1,128)}, u32[]{:S(2)}) copy-start(s32[32,16,1]{0,2,1:T(1,128)} %param.8) | copy-start | bytes 6148
  9.8 3.5 %copy-start.15 = (s32[32,16]{0,1:T(8,128)S(1)}, s32[32,16]{0,1:T(8,128)}, u32[]{:S(2)}) copy-start(s32[32,16]{0,1:T(8,128)} %param.9) | copy-start | bytes 6148
  14.1 27.8 %all-to-all-start = ((s32[16,1,512]{2,1,0:T(1,128)}), s32[16,1,512]{2,1,0:T(1,128)S(1)}, u32[]{:S(2)}, u32[]{:S(2)}) async-start(s32[16,1,512]{2,1,0:T(1,128)} %reshape.32), calls=%async_computation | async-start | bytes 65536 | tf_op jit(solution)/shard_map/all_to_all | solution.py:250
  29.3 122.1 %reduce-scatter.2.cloned.1.call-start = ((), (), s32[]{:S(2)}) async-start(), calls=%async_computation.4 | async-start | bytes 3342336 | tf_op jit(solution)/shard_map/reduce_scatter | solution.py:263
  56.5 2.9 %copy-start.2 = (bf16[3,512,2304]{2,1,0:T(8,128)(2,1)}, bf16[3,512,2304]{2,1,0:T(8,128)(2,1)S(1)}, u32[]{:S(2)}) copy-start(bf16[3,512,2304]{2,1,0:T(8,128)(2,1)S(1)} %shard_map.64) | copy-start | bytes 21233668
  77.7 48.2 %copy-start.9 = (bf16[16,1024]{1,0:T(8,128)(2,1)}, bf16[16,1024]{1,0:T(8,128)(2,1)S(1)}, u32[]{:S(2)}) copy-start(bf16[16,1024]{1,0:T(8,128)(2,1)S(1)} %reshape_squeeze.3.neg_ref) | copy-start | bytes 98308
  116.2 20.8 %collective-permute-start.1 = (bf16[256,1024]{1,0:T(8,128)(2,1)}, bf16[256,1024]{1,0:T(8,128)(2,1)}, u32[]{:S(2)}, u32[]{:S(2)}) collective-permute-start(bf16[256,1024]{1,0:T(8,128)(2,1)} %all_gather.13.neg_a_ref), channel_id=1, source_target_pairs={{0,4},{4,0},{1,5},{5,1},{2,6},{6,2},{3,7},{7,3},{8,12},{12,8},{9,1... | collective-permute-start | bytes 1572872 | tf_op jit(solution)/shard_map/ppermute | solution.py:272
  118.1 12.5 %collective-permute-start = (s32[512,16]{0,1:T(8,128)}, s32[512,16]{0,1:T(8,128)S(1)}, u32[]{:S(2)}, u32[]{:S(2)}) collective-permute-start(s32[512,16]{0,1:T(8,128)} %reshape.26), channel_id=1, source_target_pairs={{0,4},{4,0},{1,5},{5,1},{2,6},{6,2},{3,7},{7,3},{8,12},{12,8},{9,1... | collective-permute-start | bytes 98312 | tf_op jit(solution)/shard_map/ppermute | solution.py:273
  135.3 1.8 copy-start.3
  151.4 0.9 copy-start.8
  154.4 51.0 %copy-start.4 = (bf16[3,1152,512]{2,1,0:T(8,128)(2,1)S(1)}, bf16[3,1152,512]{2,1,0:T(8,128)(2,1)}, u32[]{:S(2)}) copy-start(bf16[3,1152,512]{2,1,0:T(8,128)(2,1)} %copy-done.3) | copy-start | bytes 10616836
  154.4 51.0 %copy-start.5 = (bf16[4,4,72,1024]{3,2,1,0:T(8,128)(2,1)S(1)}, bf16[4,4,72,1024]{3,2,1,0:T(8,128)(2,1)}, u32[]{:S(2)}) copy-start(bf16[4,4,72,1024]{3,2,1,0:T(8,128)(2,1)} %copy.13) | copy-start | bytes 7077892
  154.4 51.0 %copy-start.10 = (bf16[16,1024]{1,0:T(8,128)(2,1)S(1)}, bf16[16,1024]{1,0:T(8,128)(2,1)}, u32[]{:S(2)}) copy-start(bf16[16,1024]{1,0:T(8,128)(2,1)} %copy-done.9) | copy-start | bytes 98308
  199.0 6.4 %collective-permute-start.2 = (bf16[16,72,1024]{2,1,0:T(8,128)(2,1)S(1)}, bf16[16,72,1024]{2,1,0:T(8,128)(2,1)S(1)}, u32[]{:S(2)}, u32[]{:S(2)}) collective-permute-start(bf16[16,72,1024]{2,1,0:T(8,128)(2,1)S(1)} %bitcast.27), channel_id=1, source_target_pairs={{0,4},{4,0},{1,5},{5,1},{2,6},{6,2},{3,7},{7,3},{8,12},{12,8},{9,1... | collective-permute-start | bytes 7077896 | tf_op jit(solution)/shard_map/ppermute | solution.py:304
  214.1 37.1 %copy-start.6 = (f32[72,1024]{1,0:T(8,128)S(1)}, f32[72,1024]{1,0:T(8,128)}, u32[]{:S(2)}) copy-start(f32[72,1024]{1,0:T(8,128)} %constant_dynamic-slice_fusion.pre_ref) | copy-start | bytes 884740
  214.1 51.3 %copy-start.1 = (bf16[1024,1024]{1,0:T(8,128)(2,1)S(1)}, bf16[1024,1024]{1,0:T(8,128)(2,1)}, u32[]{:S(2)}) copy-start(bf16[1024,1024]{1,0:T(8,128)(2,1)} %projection_ref.3) | copy-start | bytes 6291460
  214.2 51.3 %copy-start.12 = (s32[4]{0:T(128)S(1)}, s32[4]{0:T(128)}, u32[]{:S(2)}) copy-start(s32[4]{0:T(128)} %neg_row_ref.3) | copy-start | bytes 52
Sparse Core Ops, SparseCore 0:
  13.4 45.3 all-gather.2
  71.7 79.5 reduce-scatter.1

commit v6 on v5

--- a/solution.py
+++ b/solution.py
@@ -57,7 +57,7 @@
     return owner >> 5, owner & 1, (owner >> 1) & 15, row >> 6, row & 63, coefs
 
 
-def embed_kernel(neg_row_ref, table_ref, projection_ref, pre_ref, shared_ref):
+def embed_kernel(neg_row_ref, table_ref, projection_ref, pre_ref, shared_ref, negs_ref):
     picks = lax.broadcasted_iota(jnp.int32, (X * 8, ROWS), 0)
     cols = lax.broadcasted_iota(jnp.int32, (X * 8, ROWS), 1)
     hot = jnp.zeros((X * 8, ROWS), f32)
@@ -67,6 +67,9 @@
     neg_pre = dot_nn(neg_rows, projection_ref[...])
     neg_act = neg_pre * jax.nn.sigmoid(neg_pre)
     neg_unit = (neg_act / row_norm(neg_act)).astype(bf16)
+    source = lax.broadcasted_iota(jnp.int32, (8, X * 8), 0) * 8
+    pick = jnp.where(source == lax.broadcasted_iota(jnp.int32, (8, X * 8), 1), 1.0, 0.0)
+    negs_ref[...] = dot_nn(pick.astype(bf16), neg_unit).astype(bf16)
     for i in range(X):
         node_pre = dot_nn(table_ref[i * PART : (i + 1) * PART], projection_ref[...])
         start = i * BLOCK
@@ -76,20 +79,30 @@
         shared_ref[start + PART : start + BLOCK] = neg_unit[8 * i : 8 * i + 8]
 
 
-def spread_kernel(where_ref, line_ref, out_ref):
-    ny, nc, nz, part, rest, coefs = decode(line_ref[...], 1)
+def spread_kernel(where_ref, received_ref, out_ref, line_ref):
+    rows, slots = line_ref.shape
+    tiles = [received_ref[0, X:8, t * 128 : (t + 1) * 128].astype(f32) for t in range(8)]
+    fields = jnp.concatenate(tiles, axis=0)
+    packed = fields[:, 0:slots] + fields[:, slots : 2 * slots] * 128.0 + fields[:, 2 * slots : 3 * slots] * 32768.0
+    packed = packed.astype(jnp.int32)
+    line_ref[...] = packed
+    ny, nc, nz, part, rest, coefs = decode(packed, 1)
     column = jnp.where(nz == where_ref[0], (ny * C + nc) * OWN + part * BLOCK + rest, -1)
-    rows, slots = column.shape
-    chunk = WIDE // 3
-    for k in range(3):
-        lanes = lax.broadcasted_iota(jnp.int32, (rows, chunk), 1) + k * chunk
-        total = jnp.where(lanes == column[:, 0:1], 1.0, 0.0)
-        for slot in range(3, slots):
-            total = total + jnp.where(lanes == column[:, slot : slot + 1], coefs[:, slot : slot + 1], 0.0)
-        span = pl.ds(k * chunk, chunk)
-        out_ref[0, :, span] = total.astype(bf16)
-        out_ref[1, :, span] = jnp.where(lanes == column[:, 1:2], 1.0, 0.0).astype(bf16)
-        out_ref[2, :, span] = jnp.where(lanes == column[:, 2:3], 1.0, 0.0).astype(bf16)
+    high, low = column >> 8, column & 255
+    lanes = lax.broadcasted_iota(jnp.int32, (rows, 256), 1)
+    chunks = WIDE // 256
+    totals = [jnp.zeros((rows, 256), bf16) for _ in range(chunks)]
+    for slot in range(slots):
+        hot = jnp.where(lanes == low[:, slot : slot + 1], 1.0, 0.0).astype(bf16)
+        weight = coefs[:, slot : slot + 1] if slot > 2 else 1.0
+        for k in range(chunks):
+            term = hot * jnp.where(high[:, slot : slot + 1] == k, weight, 0.0).astype(bf16)
+            if slot == 1 or slot == 2:
+                out_ref[slot, :, k * 256 : (k + 1) * 256] = term
+            else:
+                totals[k] = totals[k] + term
+    for k in range(chunks):
+        out_ref[0, :, k * 256 : (k + 1) * 256] = totals[k]
 
 
 def node_weights_kernel(where_ref, line_ref, out_ref):
@@ -231,35 +244,48 @@
     feat_width, embed_width = projection.shape
     line_count = Z * query_count
 
-    shifted = jnp.pad(visits, ((0, 0), (3, 0)))
-    packed = slot_owner.reshape(query_count, slot_count) + slot_row * 128 + shifted * 32768
-
-    pre, shared = call(
+    pre, shared, negs = call(
         embed_kernel,
-        (jax.ShapeDtypeStruct((OWN, embed_width), f32), jax.ShapeDtypeStruct((OWN, embed_width), bf16)),
+        (
+            jax.ShapeDtypeStruct((OWN, embed_width), f32),
+            jax.ShapeDtypeStruct((OWN, embed_width), bf16),
+            jax.ShapeDtypeStruct((8, embed_width), bf16),
+        ),
         2 * OWN * embed_width * feat_width,
         5 << 20,
         16,
         in_specs=[SMEM, VMEM, VMEM],
-        out_specs=(VMEM, VMEM),
+        out_specs=(VMEM, VMEM, VMEM),
     )(neg_row, feature_table, projection)
     plane = lax.all_gather(shared, ("y", "c"), axis=0, tiled=True)
     my_pre = lax.dynamic_slice_in_dim(pre, x * BLOCK, BLOCK, axis=0)
 
-    copies = jnp.broadcast_to(packed, (Z, query_count, slot_count))
-    line = lax.all_to_all(copies, "z", split_axis=0, concat_axis=0, tiled=True).reshape(line_count, slot_count)
-    spread = call(
+    shifted = jnp.pad(visits, ((0, 0), (3, 0)))
+    fields = jnp.concatenate([slot_owner.reshape(query_count, slot_count), slot_row, shifted], axis=1)
+    fields = jnp.pad(fields.astype(bf16), ((0, 0), (0, 128 - 3 * slot_count)))
+    fields = fields.reshape(8, 4, 128).transpose(1, 0, 2).reshape(4, embed_width)
+    block = jnp.concatenate([negs[0:X], fields], axis=0)
+    copies = jnp.broadcast_to(block, (Z, 8, embed_width))
+    received = lax.all_to_all(copies, "z", split_axis=0, concat_axis=0, tiled=True)
+    line_neg = received[:, 0:X].reshape(Z * X, embed_width)
+    spread, line = call(
         spread_kernel,
-        jax.ShapeDtypeStruct((3, line_count, WIDE), bf16),
+        (
+            jax.ShapeDtypeStruct((3, line_count, WIDE), bf16),
+            jax.ShapeDtypeStruct((line_count, slot_count), jnp.int32),
+        ),
         line_count * WIDE * 48,
         line_count * WIDE * 6,
-        16,
+        56,
         grid=(Z,),
-        in_specs=[SMEM, pl.BlockSpec((query_count, slot_count), lambda i: (i, 0))],
-        out_specs=pl.BlockSpec((3, query_count, WIDE), lambda i: (0, i, 0)),
-    )(here, line)
+        in_specs=[SMEM, pl.BlockSpec((1, 8, embed_width), lambda i: (i, 0, 0))],
+        out_specs=(
+            pl.BlockSpec((3, query_count, WIDE), lambda i: (0, i, 0)),
+            pl.BlockSpec((query_count, slot_count), lambda i: (i, 0)),
+        ),
+    )(here, received)
     part = dot_nn(spread.reshape(3 * line_count, WIDE), plane).astype(bf16)
-    part, plane, line = lax.optimization_barrier((part, plane, line))
+    part, plane, line, line_neg = lax.optimization_barrier((part, plane, line, line_neg))
     got = lax.psum_scatter(
         part.reshape(3, line_count, embed_width), "z", scatter_dimension=1, tiled=True
     )
@@ -268,7 +294,7 @@
     core_plane = core_plane.transpose(1, 0, 2, 3)
     core_neg = core_plane[:, :, PART].reshape(X * Y, embed_width)
     core_plane = core_plane.reshape(NARROW, embed_width)
-    some_neg = lax.all_gather(core_neg, "z", axis=0, tiled=True)
+    some_neg = lax.all_gather(line_neg, "y", axis=0, tiled=True)
     other_neg = lax.ppermute(some_neg, "c", SIBLING)
     line_sib = lax.ppermute(line, "c", SIBLING)
 

time: 276 us -> 284 us (1.029)
  waiting for transfers between devices: 31.3 us -> 58.4 us
  blocking collectives: 133 us -> 109 us
  Pallas kernels: 38.4 us -> 42 us
    all_gather x1, blocking collectives: 38.5 us -> 13.9 us  [on_device(): some_neg = lax.all_gather(line_neg, 'y', axis=0, tiled=True)]
    reduce_scatter x1, waiting for transfers between devices: 14.3 us -> 38.5 us  [on_device(): lax.psum_scatter(part.reshape(3, line_count, embed_width), 'z', scatter_d...]
    all_to_all x1, waiting for transfers between devices: 12.4 us -> 17.8 us  [on_device(): lax.all_to_all(copies, 'z', split_axis=0, concat_axis=0, tiled=True)]
    unnamed x35 -> x37, local copies, waits for them, and re-layouts: 9.71 us -> 11.1 us
  transfers between devices with their start and end apart: 6 -> 6, of which waited for: 3 -> 3; matrix products, arithmetic and copies ran while one was open for 5% -> 4% of each run, Pallas kernels for 8% -> 8%
where the time goes in v6:
time: 284 us; the launch traced here: 282 us
  blocking collectives  109 us (38%)
  waiting for transfers between devices  58.4 us (21%)
  Pallas kernels  42 us (15%)
  local copies, waits for them, and re-layouts  22.7 us (8%)
  starting transfers between devices  21.5 us (8%)
  between operations  13.7 us (5%)
  matrix products  12.2 us (4%)
    all_gather x1, blocking collectives, on_device(): lax.all_gather(payload.astype(f16), 'z', axis=0, tiled=True).astype(bf16)  44.3 us
    reduce_scatter x1, waiting for transfers between devices, on_device(): lax.psum_scatter(part.reshape(3, line_count, embed_width), 'z', scatter_d...  38.5 us
    all_to_all x1, blocking collectives, on_device(): lax.all_to_all(node_grads, ('x', 'y'), split_axis=0, concat_axis=0, tiled...  36.7 us
    all_to_all x1, waiting for transfers between devices, on_device(): lax.all_to_all(copies, 'z', split_axis=0, concat_axis=0, tiled=True)  17.8 us
    all_to_all x1, starting transfers between devices, on_device(): lax.all_to_all(copies, 'z', split_axis=0, concat_axis=0, tiled=True)  15.2 us
    all_gather x1, blocking collectives, on_device(): some_neg = lax.all_gather(line_neg, 'y', axis=0, tiled=True)  13.9 us
    all_gather x1, blocking collectives, on_device(): all_pre_grad = lax.all_gather(pre_grad, 'x', axis=0, tiled=True)  13.6 us
    pallas_call x1, Pallas kernels, on_device(): call(spread_kernel, (jax.ShapeDtypeStruct((3, line_count, WIDE), bf16), j...  12.7 us
  transfers between devices with their start and end apart: 6, of which 3 were waited for; matrix products, arithmetic and copies ran while one was open for 4% of the time, Pallas kernels for 8%

profile of v6, /device:TPU:8, one launch (start us, length us, event | category | flops | bytes accessed | tf_op | source)
XLA Modules:
  0.0 281.6 jit_solution(9096806794053189327)
XLA Ops:
  6.5 0.0 all-gather.3.cloned.1.call-start
  6.5 0.0 copy-start
  6.5 1.6 copy-done
  8.1 0.0 copy-start.6
  8.1 1.0 copy-done.6
  9.2 0.0 copy-start.10
  9.2 0.7 copy-done.10
  9.8 3.7 %shard_map.64 = (f32[288,1024]{1,0:T(8,128)S(1)}, bf16[288,1024]{1,0:T(8,128)(2,1)}, bf16[8,1024]{1,0:T(8,128)(2,1)S(1)}) custom-call(s32[4]{0:T(128)S(1)} %copy-done.10, bf16[256,1024]{1,0:T(8,128)(2,1)S(1)} %copy-done.6, bf16[1024,1024]{1,0:T(8,128)(2,1)S(1)} %copy-done), custom_call_target="tpu_custom_call" | custom-call | flops 603979776 | bytes 5242880 | tf_op jit(solution)/shard_map/pallas_call | solution.py:247
  13.5 0.0 all-gather.3.cloned.1.call-update
  13.5 0.0 copy-done.15
  13.6 0.0 copy-done.16
  13.6 0.0 copy-done.17
  13.6 0.1 copy.26
  13.7 0.7 broadcast_in_dim.3
  14.5 15.2 %all-to-all-start = ((bf16[16,8,1024]{2,1,0:T(8,128)(2,1)}), bf16[16,8,1024]{2,1,0:T(8,128)(2,1)S(1)}, u32[]{:S(2)}, u32[]{:S(2)}) async-start(bf16[16,8,1024]{2,1,0:T(8,128)(2,1)} %broadcast_in_dim.3), calls=%async_computation | async-start | bytes 524288 | tf_op jit(solution)/shard_map/all_to_all | solution.py:269
  29.7 0.0 reduce-scatter.2.cloned.1.call-start
  29.7 0.6 pad_add_fusion.where_ref
  30.3 17.8 %all-to-all-done.received_ref = bf16[16,8,1024]{2,1,0:T(8,128)(2,1)S(1)} async-done(((bf16[16,8,1024]{2,1,0:T(8,128)(2,1)}), bf16[16,8,1024]{2,1,0:T(8,128)(2,1)S(1)}, u32[]{:S(2)}, u32[]{:S(2)}) %all-to-all-start) | async-done | bytes 262176 | tf_op jit(solution)/shard_map/all_to_all | solution.py:269
  48.1 0.6 copy-done.13
  48.8 12.7 %shard_map.65 = (bf16[3,512,2304]{2,1,0:T(8,128)(2,1)}, s32[512,16]{1,0:T(8,128)}) custom-call(s32[2]{0:T(128)} %pad_add_fusion.where_ref, bf16[16,8,1024]{2,1,0:T(8,128)(2,1)} %copy-done.13), custom_call_target="tpu_custom_call" | custom-call | flops 56623104 | bytes 7077888 | tf_op jit(solution)/shard_map/pallas_call | solution.py:271
  61.5 12.2 %convolution_convert_fusion = bf16[1536,1024]{1,0:T(8,128)(2,1)} fusion(bf16[1536,2304]{1,0:T(8,128)(2,1)} %bitcast.36, bf16[2304,1024]{1,0:T(8,128)(2,1)} %all-gather.3.cloned.1.call-done), kind=kOutput, calls=%fused_computation | convolution fusion | flops 7249330176 | bytes 14942208 | tf_op jit(solution)/shard_map/dot_general | solution.py:45
  73.7 0.0 reduce-scatter.2.cloned.1.call-update
  73.7 13.9 %all_gather.13.neg_a_ref = bf16[256,1024]{1,0:T(8,128)(2,1)} all-gather(bf16[64,1024]{1,0:T(8,128)(2,1)S(1)} %reshape.36), channel_id=1, replica_groups=mesh['y'=4,'z'=16,'c'=2,'x'=4] {'y'}, dimensions={0}, use_global_device_ids=true | all-gather | bytes 655360 | tf_op jit(solution)/shard_map/all_gather | solution.py:297
  87.6 1.9 collective-permute-start.1
  89.5 0.7 constant_dynamic-slice_fusion.pre_ref
  90.3 0.0 copy-done.14
  90.3 0.7 copy.22
  91.0 2.4 collective-permute-start
  93.4 2.0 constant_dynamic-slice_fusion.1
  95.4 1.8 copy.28
  97.2 0.0 copy-start.12
  97.2 0.0 copy-start.9
  97.2 2.7 copy.25
  99.9 0.0 copy-done.9
  99.9 4.8 %shard_map.66.own_w_ref = bf16[3,1152,512]{2,1,0:T(8,128)(2,1)S(1)} custom-call(s32[2]{0:T(128)S(1)} %copy-done.9, s32[16,512]{1,0:T(8,128)} %bitcast.9.line_ref), custom_call_target="tpu_custom_call" | custom-call | flops 28311552 | bytes 3538944 | tf_op jit(solution)/shard_map/pallas_call | solution.py:302
  104.7 0.0 copy-done.12
  104.8 0.0 collective-permute-done
  104.8 4.6 %shard_map.67.sib_w_ref = bf16[3,1152,512]{2,1,0:T(8,128)(2,1)S(1)} custom-call(s32[2]{0:T(128)S(1)} %copy-done.9, s32[16,512]{1,0:T(8,128)S(1)} %bitcast.29), custom_call_target="tpu_custom_call" | custom-call | flops 28311552 | bytes 3538944 | tf_op jit(solution)/shard_map/pallas_call | solution.py:302
  109.4 0.0 copy-start.2
  109.4 1.7 copy-done.2
  111.1 0.0 collective-permute-done.1.neg_b_ref
  111.1 38.5 %reduce-scatter.2.cloned.1.call-done.got_ref = bf16[3,32,1024]{2,1,0:T(8,128)(2,1)} async-done(((bf16[3,512,1024]{2,1,0:T(8,128)(2,1)}), bf16[3,32,1024]{2,1,0:T(8,128)(2,1)}) %reduce-scatter.2.cloned.1.call-update) | async-done | bytes 196624 | tf_op jit(solution)/shard_map/reduce_scatter | solution.py:289
  149.6 0.9 copy-done.7
  150.5 2.0 shard_map.68
  152.6 44.3 %all-gather.4 = f16[1152,1024]{1,0:T(8,128)(2,1)S(1)} all-gather(f16[72,1024]{1,0:T(8,128)(2,1)S(1)} %convert_element_type.13), channel_id=1, replica_groups=mesh['y'=4,'z'=16,'c'=2,'x'=4] {'z'}, dimensions={0}, use_global_device_ids=true | all-gather | bytes 2506752 | tf_op jit(solution)/shard_map/all_gather | solution.py:328
  196.9 2.1 convert_element_type.14
  199.0 1.9 collective-permute-start.2
  201.0 1.4 slice.13
  202.3 1.4 reshape_squeeze.3.neg_ref
  203.7 2.1 collective-permute-done.2.sib_ref
  205.8 2.0 copy-done.3
  207.8 1.7 copy-done.4
  209.5 0.8 copy-done.8
  210.2 10.9 %shard_map.69 = bf16[1152,1024]{1,0:T(8,128)(2,1)S(1)} custom-call(bf16[3,1152,512]{2,1,0:T(8,128)(2,1)S(1)} %shard_map.66.own_w_ref, bf16[3,1152,512]{2,1,0:T(8,128)(2,1)S(1)} %copy-done.3, bf16[16,72,1024]{2,1,0:T(8,128)(2,1)} %bitcast.15.own_ref, bf16[16,72,1024]{2,1,0:T(8,128)(2,1)} %collective-permute-done.2.sib_ref, bf16[1152,1024]{1,0:T(8,128)(2,1)S(1)} %bitcast.27, ...), custom_call_target="tpu_custom_call" | custom-call | flops 4831838208 | bytes 16777216 | tf_op jit(solution)/shard_map/pallas_call | solution.py:332
  221.2 0.0 copy-start.5
  221.2 0.0 copy-start.1
  221.2 0.0 copy-start.11
  221.2 36.7 %all_to_all.14.pieces_ref = bf16[16,72,1024]{2,1,0:T(8,128)(2,1)S(1)} all-to-all(bf16[16,72,1024]{2,1,0:T(8,128)(2,1)S(1)} %bitcast.28), channel_id=1, replica_groups=mesh['y'=4,'z'=16,'c'=2,'x'=4] {'x','y'}, dimensions={0} | all-to-all | bytes 4718592 | tf_op jit(solution)/shard_map/all_to_all | solution.py:351
  257.9 0.0 copy-done.5
  257.9 0.5 shard_map.70
  258.5 13.6 %all_gather.15.grad_ref = bf16[288,1024]{1,0:T(8,128)(2,1)S(1)} all-gather(bf16[72,1024]{1,0:T(8,128)(2,1)S(1)} %shard_map.70), channel_id=1, replica_groups=mesh['y'=4,'z'=16,'c'=2,'x'=4] {'x'}, dimensions={0}, use_global_device_ids=true | all-gather | bytes 737280 | tf_op jit(solution)/shard_map/all_gather | solution.py:361
  272.1 0.0 copy-done.1
  272.1 0.0 copy-done.11
  272.1 2.7 shard_map.71
  (20 shorter events, 0.2 us)
Async XLA Ops:
  6.5 55.0 %all-gather.3.cloned.1.call-start = ((), (), s32[]{:S(2)}) async-start(), calls=%async_computation.3 | async-start | bytes 5308416 | tf_op jit(solution)/shard_map/all_gather | solution.py:260
  6.5 1.6 copy-start
  8.1 1.0 copy-start.6
  9.2 0.7 copy-start.10
  9.8 3.7 %copy-start.15 = (s32[32,16]{0,1:T(8,128)S(1)}, s32[32,16]{0,1:T(8,128)}, u32[]{:S(2)}) copy-start(s32[32,16]{0,1:T(8,128)} %param.9) | copy-start | bytes 6148
  9.8 3.7 %copy-start.16 = (s32[32,13]{0,1:T(8,128)S(1)}, s32[32,13]{0,1:T(8,128)}, u32[]{:S(2)}) copy-start(s32[32,13]{0,1:T(8,128)} %param.10) | copy-start | bytes 4996
  9.8 3.7 %copy-start.17 = (s32[32,16,1]{0,2,1:T(1,128)S(1)}, s32[32,16,1]{0,2,1:T(1,128)}, u32[]{:S(2)}) copy-start(s32[32,16,1]{0,2,1:T(1,128)} %param.8) | copy-start | bytes 6148
  14.5 33.6 %all-to-all-start = ((bf16[16,8,1024]{2,1,0:T(8,128)(2,1)}), bf16[16,8,1024]{2,1,0:T(8,128)(2,1)S(1)}, u32[]{:S(2)}, u32[]{:S(2)}) async-start(bf16[16,8,1024]{2,1,0:T(8,128)(2,1)} %broadcast_in_dim.3), calls=%async_computation | async-start | bytes 524288 | tf_op jit(solution)/shard_map/all_to_all | solution.py:269
  29.7 119.9 %reduce-scatter.2.cloned.1.call-start = ((), (), s32[]{:S(2)}) async-start(), calls=%async_computation.4 | async-start | bytes 3342336 | tf_op jit(solution)/shard_map/reduce_scatter | solution.py:289
  48.1 0.7 copy-start.13
  73.7 16.5 %copy-start.14 = (s32[512,16]{1,0:T(8,128)S(1)}, s32[512,16]{1,0:T(8,128)}, u32[]{:S(2)}) copy-start(s32[512,16]{1,0:T(8,128)} %get-tuple-element.26) | copy-start | bytes 98308
  87.6 23.5 %collective-permute-start.1 = (bf16[256,1024]{1,0:T(8,128)(2,1)}, bf16[256,1024]{1,0:T(8,128)(2,1)}, u32[]{:S(2)}, u32[]{:S(2)}) collective-permute-start(bf16[256,1024]{1,0:T(8,128)(2,1)} %all_gather.13.neg_a_ref), channel_id=1, source_target_pairs={{0,4},{4,0},{1,5},{5,1},{2,6},{6,2},{3,7},{7,3},{8,12},{12,8},{9,1... | collective-permute-start | bytes 1572872 | tf_op jit(solution)/shard_map/ppermute | solution.py:298
  91.0 13.8 %collective-permute-start = (s32[512,16]{0,1:T(8,128)}, s32[512,16]{0,1:T(8,128)S(1)}, u32[]{:S(2)}, u32[]{:S(2)}) collective-permute-start(s32[512,16]{0,1:T(8,128)} %copy.22), channel_id=1, source_target_pairs={{0,4},{4,0},{1,5},{5,1},{2,6},{6,2},{3,7},{7,3},{8,12},{12,8},{9,1... | collective-permute-start | bytes 98312 | tf_op jit(solution)/shard_map/ppermute | solution.py:299
  97.2 7.5 %copy-start.12 = (bf16[4,1,4,72,1024]{4,0,2,3,1:T(4,128)(2,1)}, bf16[4,1,4,72,1024]{4,0,2,3,1:T(4,128)(2,1)S(1)}, u32[]{:S(2)}) copy-start(bf16[4,1,4,72,1024]{4,0,2,3,1:T(4,128)(2,1)S(1)} %copy.28) | copy-start | bytes 7077892
  97.2 2.7 copy-start.9
  109.4 1.7 copy-start.2
  149.6 0.9 copy-start.7
  199.0 6.8 %collective-permute-start.2 = (bf16[16,72,1024]{2,1,0:T(8,128)(2,1)}, bf16[16,72,1024]{2,1,0:T(8,128)(2,1)}, u32[]{:S(2)}, u32[]{:S(2)}) collective-permute-start(bf16[16,72,1024]{2,1,0:T(8,128)(2,1)} %bitcast.15.own_ref), channel_id=1, source_target_pairs={{0,4},{4,0},{1,5},{5,1},{2,6},{6,2},{3,7},{7,3},{8,12},{12,8},{9,1... | collective-permute-start | bytes 7077896 | tf_op jit(solution)/shard_map/ppermute | solution.py:330
  205.8 2.0 copy-start.3
  207.8 1.7 copy-start.4
  209.5 0.8 copy-start.8
  221.2 36.8 %copy-start.5 = (f32[72,1024]{1,0:T(8,128)S(1)}, f32[72,1024]{1,0:T(8,128)}, u32[]{:S(2)}) copy-start(f32[72,1024]{1,0:T(8,128)} %constant_dynamic-slice_fusion.pre_ref) | copy-start | bytes 884740
  221.2 50.9 %copy-start.1 = (bf16[1024,1024]{1,0:T(8,128)(2,1)S(1)}, bf16[1024,1024]{1,0:T(8,128)(2,1)}, u32[]{:S(2)}) copy-start(bf16[1024,1024]{1,0:T(8,128)(2,1)} %projection_ref.3) | copy-start | bytes 6291460
  221.2 50.9 %copy-start.11 = (s32[4]{0:T(128)S(1)}, s32[4]{0:T(128)}, u32[]{:S(2)}) copy-start(s32[4]{0:T(128)} %neg_row_ref.3) | copy-start | bytes 52
Sparse Core Ops, SparseCore 0:
  13.6 45.3 all-gather.2
  73.9 75.6 reduce-scatter.1

commit v7 on v6

--- a/solution.py
+++ b/solution.py
@@ -92,11 +92,13 @@
     lanes = lax.broadcasted_iota(jnp.int32, (rows, 256), 1)
     chunks = WIDE // 256
     totals = [jnp.zeros((rows, 256), bf16) for _ in range(chunks)]
+    nothing = jnp.zeros((rows, 256), bf16)
     for slot in range(slots):
-        hot = jnp.where(lanes == low[:, slot : slot + 1], 1.0, 0.0).astype(bf16)
         weight = coefs[:, slot : slot + 1] if slot > 2 else 1.0
+        hot = jnp.where(lanes == low[:, slot : slot + 1], weight, 0.0).astype(bf16)
+        level = jnp.broadcast_to(high[:, slot : slot + 1].astype(f32), (rows, 256)).astype(bf16)
         for k in range(chunks):
-            term = hot * jnp.where(high[:, slot : slot + 1] == k, weight, 0.0).astype(bf16)
+            term = jnp.where(level == k, hot, nothing)
             if slot == 1 or slot == 2:
                 out_ref[slot, :, k * 256 : (k + 1) * 256] = term
             else:
@@ -311,8 +313,8 @@
         )(here, some_line.T)
 
     own_w, sib_w = node_weights(line), node_weights(line_sib)
-    got, own_w, sib_w, core_plane, some_neg, other_neg, my_pre = lax.optimization_barrier(
-        (got, own_w, sib_w, core_plane, some_neg, other_neg, my_pre)
+    got, own_w, sib_w, core_plane, core_neg, some_neg, other_neg, my_pre = lax.optimization_barrier(
+        (got, own_w, sib_w, core_plane, core_neg, some_neg, other_neg, my_pre)
     )
 
     payload_rows = 2 * query_count + 8

time: 284 us -> 275 us (0.968)
  local copies, waits for them, and re-layouts: 22.7 us -> 16.1 us
    unnamed x37 -> x35, local copies, waits for them, and re-layouts: 11.1 us -> 6.7 us
where the time goes in v7:
time: 275 us; the launch traced here: 273 us
  blocking collectives  109 us (40%)
  waiting for transfers between devices  59.9 us (22%)
  Pallas kernels  39.5 us (14%)
  starting transfers between devices  21.5 us (8%)
  local copies, waits for them, and re-layouts  16.1 us (6%)
  between operations  13.7 us (5%)
  matrix products  12.2 us (4%)
    all_gather x1, blocking collectives, on_device(): lax.all_gather(payload.astype(f16), 'z', axis=0, tiled=True).astype(bf16)  44.4 us
    reduce_scatter x1, waiting for transfers between devices, on_device(): lax.psum_scatter(part.reshape(3, line_count, embed_width), 'z', scatter_d...  37.6 us
    all_to_all x1, blocking collectives, on_device(): lax.all_to_all(node_grads, ('x', 'y'), split_axis=0, concat_axis=0, tiled...  36.9 us
    all_to_all x1, waiting for transfers between devices, on_device(): lax.all_to_all(copies, 'z', split_axis=0, concat_axis=0, tiled=True)  17.7 us
    all_to_all x1, starting transfers between devices, on_device(): lax.all_to_all(copies, 'z', split_axis=0, concat_axis=0, tiled=True)  15.2 us
    all_gather x1, blocking collectives, on_device(): some_neg = lax.all_gather(line_neg, 'y', axis=0, tiled=True)  14.4 us
    all_gather x1, blocking collectives, on_device(): all_pre_grad = lax.all_gather(pre_grad, 'x', axis=0, tiled=True)  13.6 us
    dot_general x1, matrix products, dot_nn(): lax.dot_general(left, right, (((1,), (0,)), ((), ())), preferred_element_...  12.2 us
  transfers between devices with their start and end apart: 6, of which 3 were waited for; matrix products, arithmetic and copies ran while one was open for 4% of the time, Pallas kernels for 8%

profile of v7, /device:TPU:8, one launch (start us, length us, event | category | flops | bytes accessed | tf_op | source)
XLA Modules:
  0.0 273.5 jit_solution(10344745859986648396)
XLA Ops:
  6.5 0.0 all-gather.3.cloned.1.call-start
  6.5 0.0 copy-start
  6.5 1.6 copy-done
  8.1 0.0 copy-start.6
  8.1 1.0 copy-done.6
  9.2 0.0 copy-start.10
  9.2 0.7 copy-done.10
  9.8 3.7 %shard_map.64 = (f32[288,1024]{1,0:T(8,128)S(1)}, bf16[288,1024]{1,0:T(8,128)(2,1)}, bf16[8,1024]{1,0:T(8,128)(2,1)S(1)}) custom-call(s32[4]{0:T(128)S(1)} %copy-done.10, bf16[256,1024]{1,0:T(8,128)(2,1)S(1)} %copy-done.6, bf16[1024,1024]{1,0:T(8,128)(2,1)S(1)} %copy-done), custom_call_target="tpu_custom_call" | custom-call | flops 603979776 | bytes 5242880 | tf_op jit(solution)/shard_map/pallas_call | solution.py:249
  13.5 0.0 all-gather.3.cloned.1.call-update
  13.5 0.0 copy-done.14
  13.6 0.0 copy-done.15
  13.6 0.0 copy-done.16
  13.6 0.1 copy.26
  13.7 0.7 broadcast_in_dim.3
  14.5 15.2 %all-to-all-start = ((bf16[16,8,1024]{2,1,0:T(8,128)(2,1)}), bf16[16,8,1024]{2,1,0:T(8,128)(2,1)S(1)}, u32[]{:S(2)}, u32[]{:S(2)}) async-start(bf16[16,8,1024]{2,1,0:T(8,128)(2,1)} %broadcast_in_dim.3), calls=%async_computation | async-start | bytes 524288 | tf_op jit(solution)/shard_map/all_to_all | solution.py:271
  29.7 0.0 reduce-scatter.2.cloned.1.call-start
  29.7 0.6 pad_add_fusion.where_ref
  30.3 17.7 %all-to-all-done.received_ref = bf16[16,8,1024]{2,1,0:T(8,128)(2,1)S(1)} async-done(((bf16[16,8,1024]{2,1,0:T(8,128)(2,1)}), bf16[16,8,1024]{2,1,0:T(8,128)(2,1)S(1)}, u32[]{:S(2)}, u32[]{:S(2)}) %all-to-all-start) | async-done | bytes 262176 | tf_op jit(solution)/shard_map/all_to_all | solution.py:271
  48.1 0.6 copy-done.12
  48.7 12.2 %shard_map.65 = (bf16[3,512,2304]{2,1,0:T(8,128)(2,1)}, s32[512,16]{1,0:T(8,128)}) custom-call(s32[2]{0:T(128)} %pad_add_fusion.where_ref, bf16[16,8,1024]{2,1,0:T(8,128)(2,1)} %copy-done.12), custom_call_target="tpu_custom_call" | custom-call | flops 56623104 | bytes 7077888 | tf_op jit(solution)/shard_map/pallas_call | solution.py:273
  60.9 12.2 %convolution_convert_fusion = bf16[1536,1024]{1,0:T(8,128)(2,1)} fusion(bf16[1536,2304]{1,0:T(8,128)(2,1)} %bitcast.37, bf16[2304,1024]{1,0:T(8,128)(2,1)} %all-gather.3.cloned.1.call-done), kind=kOutput, calls=%fused_computation | convolution fusion | flops 7249330176 | bytes 14942208 | tf_op jit(solution)/shard_map/dot_general | solution.py:45
  73.1 0.0 reduce-scatter.2.cloned.1.call-update
  73.2 14.4 %all_gather.13.neg_a_ref = bf16[256,1024]{1,0:T(8,128)(2,1)} all-gather(bf16[64,1024]{1,0:T(8,128)(2,1)S(1)} %reshape.36), channel_id=1, replica_groups=mesh['y'=4,'z'=16,'c'=2,'x'=4] {'y'}, dimensions={0}, use_global_device_ids=true | all-gather | bytes 655360 | tf_op jit(solution)/shard_map/all_gather | solution.py:299
  87.6 1.9 collective-permute-start.1
  89.5 0.7 constant_dynamic-slice_fusion.pre_ref
  90.2 0.0 copy-done.13
  90.2 0.7 copy.22
  90.9 2.4 collective-permute-start
  93.3 2.0 constant_dynamic-slice_fusion.1
  95.3 1.8 copy.28
  97.2 0.0 copy-start.9
  97.2 2.7 copy.25
  99.9 0.6 reshape_squeeze.3.neg_ref
  100.5 0.0 copy-done.9
  100.5 4.8 %shard_map.66.own_w_ref = bf16[3,1152,512]{2,1,0:T(8,128)(2,1)S(1)} custom-call(s32[2]{0:T(128)S(1)} %copy-done.9, s32[16,512]{1,0:T(8,128)} %bitcast.9.line_ref), custom_call_target="tpu_custom_call" | custom-call | flops 28311552 | bytes 3538944 | tf_op jit(solution)/shard_map/pallas_call | solution.py:304
  105.3 0.0 collective-permute-done
  105.3 4.8 %shard_map.67.sib_w_ref = bf16[3,1152,512]{2,1,0:T(8,128)(2,1)S(1)} custom-call(s32[2]{0:T(128)S(1)} %copy-done.9, s32[16,512]{1,0:T(8,128)} %bitcast.10.line_ref), custom_call_target="tpu_custom_call" | custom-call | flops 28311552 | bytes 3538944 | tf_op jit(solution)/shard_map/pallas_call | solution.py:304
  110.2 0.0 copy-start.2
  110.2 1.7 copy-done.2
  111.9 0.0 collective-permute-done.1.neg_b_ref
  111.9 37.6 %reduce-scatter.2.cloned.1.call-done.got_ref = bf16[3,32,1024]{2,1,0:T(8,128)(2,1)} async-done(((bf16[3,512,1024]{2,1,0:T(8,128)(2,1)}), bf16[3,32,1024]{2,1,0:T(8,128)(2,1)}) %reduce-scatter.2.cloned.1.call-update) | async-done | bytes 196624 | tf_op jit(solution)/shard_map/reduce_scatter | solution.py:291
  149.5 0.9 copy-done.7
  150.5 2.0 shard_map.68
  152.5 0.0 copy-start.3
  152.5 0.0 copy-start.4
  152.5 0.0 copy-start.8
  152.6 44.4 %all-gather.4 = f16[1152,1024]{1,0:T(8,128)(2,1)S(1)} all-gather(f16[72,1024]{1,0:T(8,128)(2,1)S(1)} %convert_element_type.13), channel_id=1, replica_groups=mesh['y'=4,'z'=16,'c'=2,'x'=4] {'z'}, dimensions={0}, use_global_device_ids=true | all-gather | bytes 2506752 | tf_op jit(solution)/shard_map/all_gather | solution.py:330
  197.0 0.6 convert_element_type.14
  197.6 1.9 collective-permute-start.2
  199.6 4.5 %collective-permute-done.2.sib_ref = bf16[16,72,1024]{2,1,0:T(8,128)(2,1)S(1)} collective-permute-done((bf16[16,72,1024]{2,1,0:T(8,128)(2,1)S(1)}, bf16[16,72,1024]{2,1,0:T(8,128)(2,1)S(1)}, u32[]{:S(2)}, u32[]{:S(2)}) %collective-permute-start.2) | collective-permute-done | bytes 2359328 | tf_op jit(solution)/shard_map/ppermute | solution.py:332
  204.1 0.0 copy-done.3
  204.1 0.0 copy-done.4
  204.1 0.0 copy-done.8
  204.1 8.7 %shard_map.69 = bf16[1152,1024]{1,0:T(8,128)(2,1)S(1)} custom-call(bf16[3,1152,512]{2,1,0:T(8,128)(2,1)S(1)} %shard_map.66.own_w_ref, bf16[3,1152,512]{2,1,0:T(8,128)(2,1)S(1)} %copy-done.3, bf16[16,72,1024]{2,1,0:T(8,128)(2,1)S(1)} %bitcast.29, bf16[16,72,1024]{2,1,0:T(8,128)(2,1)S(1)} %collective-permute-done.2.sib_ref, bf16[1152,1024]{1,0:T(8,128)(2,1)S(1)} %bitcast.27, ...), custom_call_target="tpu_custom_call" | custom-call | flops 4831838208 | bytes 16777216 | tf_op jit(solution)/shard_map/pallas_call | solution.py:334
  212.8 0.0 copy-start.5
  212.8 0.0 copy-start.1
  212.8 0.0 copy-start.11
  212.8 36.9 %all_to_all.14.pieces_ref = bf16[16,72,1024]{2,1,0:T(8,128)(2,1)S(1)} all-to-all(bf16[16,72,1024]{2,1,0:T(8,128)(2,1)S(1)} %bitcast.30), channel_id=1, replica_groups=mesh['y'=4,'z'=16,'c'=2,'x'=4] {'x','y'}, dimensions={0} | all-to-all | bytes 4718592 | tf_op jit(solution)/shard_map/all_to_all | solution.py:353
  249.7 0.0 copy-done.5
  249.7 0.5 shard_map.70
  250.3 13.6 %all_gather.15.grad_ref = bf16[288,1024]{1,0:T(8,128)(2,1)S(1)} all-gather(bf16[72,1024]{1,0:T(8,128)(2,1)S(1)} %shard_map.70), channel_id=1, replica_groups=mesh['y'=4,'z'=16,'c'=2,'x'=4] {'x'}, dimensions={0}, use_global_device_ids=true | all-gather | bytes 737280 | tf_op jit(solution)/shard_map/all_gather | solution.py:363
  263.9 0.0 copy-done.1
  263.9 0.0 copy-done.11
  263.9 2.7 shard_map.71
  (18 shorter events, 0.2 us)
Async XLA Ops:
  6.5 54.4 %all-gather.3.cloned.1.call-start = ((), (), s32[]{:S(2)}) async-start(), calls=%async_computation.3 | async-start | bytes 5308416 | tf_op jit(solution)/shard_map/all_gather | solution.py:262
  6.5 1.6 copy-start
  8.1 1.0 copy-start.6
  9.2 0.7 copy-start.10
  9.8 3.7 %copy-start.14 = (s32[32,16]{0,1:T(8,128)S(1)}, s32[32,16]{0,1:T(8,128)}, u32[]{:S(2)}) copy-start(s32[32,16]{0,1:T(8,128)} %param.9) | copy-start | bytes 6148
  9.8 3.7 %copy-start.15 = (s32[32,13]{0,1:T(8,128)S(1)}, s32[32,13]{0,1:T(8,128)}, u32[]{:S(2)}) copy-start(s32[32,13]{0,1:T(8,128)} %param.10) | copy-start | bytes 4996
  9.8 3.7 %copy-start.16 = (s32[32,16,1]{0,2,1:T(1,128)S(1)}, s32[32,16,1]{0,2,1:T(1,128)}, u32[]{:S(2)}) copy-start(s32[32,16,1]{0,2,1:T(1,128)} %param.8) | copy-start | bytes 6148
  14.5 33.6 %all-to-all-start = ((bf16[16,8,1024]{2,1,0:T(8,128)(2,1)}), bf16[16,8,1024]{2,1,0:T(8,128)(2,1)S(1)}, u32[]{:S(2)}, u32[]{:S(2)}) async-start(bf16[16,8,1024]{2,1,0:T(8,128)(2,1)} %broadcast_in_dim.3), calls=%async_computation | async-start | bytes 524288 | tf_op jit(solution)/shard_map/all_to_all | solution.py:271
  29.7 119.9 %reduce-scatter.2.cloned.1.call-start = ((), (), s32[]{:S(2)}) async-start(), calls=%async_computation.4 | async-start | bytes 3342336 | tf_op jit(solution)/shard_map/reduce_scatter | solution.py:291
  48.1 0.7 copy-start.12
  73.1 17.1 %copy-start.13 = (s32[512,16]{1,0:T(8,128)S(1)}, s32[512,16]{1,0:T(8,128)}, u32[]{:S(2)}) copy-start(s32[512,16]{1,0:T(8,128)} %get-tuple-element.27) | copy-start | bytes 98308
  87.6 24.3 %collective-permute-start.1 = (bf16[256,1024]{1,0:T(8,128)(2,1)}, bf16[256,1024]{1,0:T(8,128)(2,1)}, u32[]{:S(2)}, u32[]{:S(2)}) collective-permute-start(bf16[256,1024]{1,0:T(8,128)(2,1)} %all_gather.13.neg_a_ref), channel_id=1, source_target_pairs={{0,4},{4,0},{1,5},{5,1},{2,6},{6,2},{3,7},{7,3},{8,12},{12,8},{9,1... | collective-permute-start | bytes 1572872 | tf_op jit(solution)/shard_map/ppermute | solution.py:300
  90.9 14.4 %collective-permute-start = (s32[512,16]{0,1:T(8,128)}, s32[512,16]{0,1:T(8,128)}, u32[]{:S(2)}, u32[]{:S(2)}) collective-permute-start(s32[512,16]{0,1:T(8,128)} %copy.22), channel_id=1, source_target_pairs={{0,4},{4,0},{1,5},{5,1},{2,6},{6,2},{3,7},{7,3},{8,12},{12,8},{9,1... | collective-permute-start | bytes 98312 | tf_op jit(solution)/shard_map/ppermute | solution.py:301
  97.2 3.3 %copy-start.9 = (s32[2]{0:T(128)S(1)}, s32[2]{0:T(128)}, u32[]{:S(2)}) copy-start(s32[2]{0:T(128)} %pad_add_fusion.where_ref) | copy-start | bytes 28
  110.2 1.7 copy-start.2
  149.5 0.9 copy-start.7
  152.5 51.5 %copy-start.3 = (bf16[3,1152,512]{2,1,0:T(8,128)(2,1)S(1)}, bf16[3,1152,512]{2,1,0:T(8,128)(2,1)}, u32[]{:S(2)}) copy-start(bf16[3,1152,512]{2,1,0:T(8,128)(2,1)} %copy-done.2) | copy-start | bytes 10616836
  152.5 51.5 %copy-start.4 = (bf16[4,4,72,1024]{3,2,1,0:T(8,128)(2,1)S(1)}, bf16[4,4,72,1024]{3,2,1,0:T(8,128)(2,1)}, u32[]{:S(2)}) copy-start(bf16[4,4,72,1024]{3,2,1,0:T(8,128)(2,1)} %copy.25) | copy-start | bytes 7077892
  152.5 51.5 %copy-start.8 = (bf16[16,1024]{1,0:T(8,128)(2,1)S(1)}, bf16[16,1024]{1,0:T(8,128)(2,1)}, u32[]{:S(2)}) copy-start(bf16[16,1024]{1,0:T(8,128)(2,1)} %reshape_squeeze.3.neg_ref) | copy-start | bytes 98308
  197.6 6.4 %collective-permute-start.2 = (bf16[16,72,1024]{2,1,0:T(8,128)(2,1)S(1)}, bf16[16,72,1024]{2,1,0:T(8,128)(2,1)S(1)}, u32[]{:S(2)}, u32[]{:S(2)}) collective-permute-start(bf16[16,72,1024]{2,1,0:T(8,128)(2,1)S(1)} %bitcast.28), channel_id=1, source_target_pairs={{0,4},{4,0},{1,5},{5,1},{2,6},{6,2},{3,7},{7,3},{8,12},{12,8},{9,1... | collective-permute-start | bytes 7077896 | tf_op jit(solution)/shard_map/ppermute | solution.py:332
  212.8 36.9 %copy-start.5 = (f32[72,1024]{1,0:T(8,128)S(1)}, f32[72,1024]{1,0:T(8,128)}, u32[]{:S(2)}) copy-start(f32[72,1024]{1,0:T(8,128)} %constant_dynamic-slice_fusion.pre_ref) | copy-start | bytes 884740
  212.8 51.1 %copy-start.1 = (bf16[1024,1024]{1,0:T(8,128)(2,1)S(1)}, bf16[1024,1024]{1,0:T(8,128)(2,1)}, u32[]{:S(2)}) copy-start(bf16[1024,1024]{1,0:T(8,128)(2,1)} %projection_ref.3) | copy-start | bytes 6291460
  212.8 51.1 %copy-start.11 = (s32[4]{0:T(128)S(1)}, s32[4]{0:T(128)}, u32[]{:S(2)}) copy-start(s32[4]{0:T(128)} %neg_row_ref.3) | copy-start | bytes 52
Sparse Core Ops, SparseCore 0:
  13.6 45.3 all-gather.2
  73.3 76.2 reduce-scatter.1

commit v8 on v7

--- a/solution.py
+++ b/solution.py
@@ -57,12 +57,20 @@
     return owner >> 5, owner & 1, (owner >> 1) & 15, row >> 6, row & 63, coefs
 
 
-def embed_kernel(neg_row_ref, table_ref, projection_ref, pre_ref, shared_ref, negs_ref):
+def embed_kernel(neg_row_ref, table_hbm, projection_hbm, pre_ref, shared_ref, negs_ref, table_ref, projection_ref, sems):
+    loads = (
+        pltpu.make_async_copy(table_hbm, table_ref, sems.at[0]),
+        pltpu.make_async_copy(projection_hbm, projection_ref, sems.at[1]),
+    )
+    for load in loads:
+        load.start()
     picks = lax.broadcasted_iota(jnp.int32, (X * 8, ROWS), 0)
     cols = lax.broadcasted_iota(jnp.int32, (X * 8, ROWS), 1)
     hot = jnp.zeros((X * 8, ROWS), f32)
     for i in range(X):
         hot = hot + jnp.where((picks == 8 * i) & (cols == neg_row_ref[i]), 1.0, 0.0)
+    for load in loads:
+        load.wait()
     neg_rows = dot_nn(hot.astype(bf16), table_ref[...]).astype(bf16)
     neg_pre = dot_nn(neg_rows, projection_ref[...])
     neg_act = neg_pre * jax.nn.sigmoid(neg_pre)
@@ -125,7 +133,7 @@
         out_ref[2, span, :] = jnp.where(nodes == column[2:3], 1.0, 0.0).astype(bf16)
 
 
-def query_kernel(where_ref, got_ref, neg_a_ref, neg_b_ref, out_ref):
+def query_kernel(got_ref, neg_a_ref, neg_b_ref, out_ref):
     count, width = got_ref.shape[1:]
     hood = got_ref[0].astype(f32)
     query_norm = row_norm(hood)
@@ -146,40 +154,32 @@
     grad = grad - query_unit * row_sum(query_unit * grad)
     power = jnp.exp(jnp.ceil(jnp.log(query_norm) * (1.0 / log_two)) * log_two).astype(bf16).astype(f32)
     inverse = (16.0 / power).astype(bf16).astype(f32)
-    out_ref[0:count] = grad * (power / query_norm)
-    out_ref[count : 2 * count] = query_float
+    out_ref[:, 0:width] = grad * (power / query_norm)
+    out_ref[:, width : 2 * width] = query_float
     lanes = lax.broadcasted_iota(jnp.int32, (count, 128), 1)
     scalars = jnp.where(lanes == 0, inverse, 0.0)
     for place, value in ((1, total), (3, hard), (5, first_norm), (7, second_norm), (9, positive)):
         high = value.astype(bf16).astype(f32)
         scalars = jnp.where(lanes == place, high, scalars)
         scalars = jnp.where(lanes == place + 1, value - high, scalars)
-    line_count = Z * count
-    spots = lax.broadcasted_iota(jnp.int32, (count, line_count), 0) + where_ref[0] * count
-    spots = jnp.where(spots == lax.broadcasted_iota(jnp.int32, (count, line_count), 1), 1.0, 0.0)
-    across = dot_nn(scalars.T[0:16].astype(bf16), spots.astype(bf16))
-    out_ref[2 * count : 2 * count + 8, 0:line_count] = across[0:8]
-    out_ref[2 * count : 2 * count + 8, line_count : 2 * line_count] = across[8:16]
+    out_ref[:, 2 * width :] = scalars
 
 
 def node_grad_kernel(own_w_ref, sib_w_ref, own_ref, sib_ref, plane_ref, neg_ref, out_ref, row_ref, neg_w_ref):
     step = pl.program_id(0)
     width = plane_ref.shape[1]
-    count = (own_ref.shape[1] - 8) // 2
-    line_count = Z * count
     received = (own_ref, sib_ref)
 
     @pl.when(step == 0)
     def _():
         for side, ref in enumerate(received):
-            spread = jnp.sum(ref[:, 2 * count : 2 * count + 8].astype(f32), axis=0)
-            scalars = jnp.concatenate([spread[:, :line_count], spread[:, line_count:]], axis=0)
+            scalars = ref[:, 2 * width :].astype(f32).T
             total = scalars[1:2] + scalars[2:3]
             hard = scalars[3:4] + scalars[4:5]
             row_ref[side, 0:1] = scalars[0:1] * 0.0625
             row_ref[side, 1:2] = -total / (scalars[5:6] + scalars[6:7])
             row_ref[side, 2:3] = hard / (scalars[7:8] + scalars[8:9])
-            scores = dot_nt(neg_ref[...], ref[:, count : 2 * count].reshape(line_count, width))
+            scores = dot_nt(neg_ref[...], ref[:, width : 2 * width])
             neg_w_ref[side] = weigh(scores, scalars[9:10] + scalars[10:11])
 
     negs = neg_ref.shape[0]
@@ -189,10 +189,10 @@
     query_part = jnp.zeros((OWN, width), f32)
     for side, (w_ref, ref) in enumerate(((own_w_ref, own_ref), (sib_w_ref, sib_ref))):
         w_hood = (w_ref[0].astype(f32) * row_ref[side, 0:1]).astype(bf16)
-        hood_part = hood_part + dot_nn(w_hood, ref[:, 0:count].reshape(line_count, width))
+        hood_part = hood_part + dot_nn(w_hood, ref[:, 0:width])
         w_query = w_ref[1].astype(f32) * row_ref[side, 1:2] + w_ref[2].astype(f32) * row_ref[side, 2:3]
         w_query = (w_query + dot_nn(spot, neg_w_ref[side])).astype(bf16)
-        query_part = query_part + dot_nn(w_query, ref[:, count : 2 * count].reshape(line_count, width))
+        query_part = query_part + dot_nn(w_query, ref[:, width : 2 * width])
     plane = plane_ref[...].astype(f32)
     place = lax.broadcasted_iota(jnp.int32, (OWN, 1), 0) % BLOCK
     inverse = jnp.where(place == PART, 0.0, 1.0 / (row_sum(plane * plane) + epsilon))
@@ -255,9 +255,14 @@
         ),
         2 * OWN * embed_width * feat_width,
         5 << 20,
-        16,
-        in_specs=[SMEM, VMEM, VMEM],
+        56,
+        in_specs=[SMEM, pl.BlockSpec(memory_space=pl.ANY), pl.BlockSpec(memory_space=pl.ANY)],
         out_specs=(VMEM, VMEM, VMEM),
+        scratch_shapes=[
+            pltpu.VMEM((ROWS, feat_width), bf16),
+            pltpu.VMEM((feat_width, embed_width), bf16),
+            pltpu.SemaphoreType.DMA((2,)),
+        ],
     )(neg_row, feature_table, projection)
     plane = lax.all_gather(shared, ("y", "c"), axis=0, tiled=True)
     my_pre = lax.dynamic_slice_in_dim(pre, x * BLOCK, BLOCK, axis=0)
@@ -317,18 +322,17 @@
         (got, own_w, sib_w, core_plane, core_neg, some_neg, other_neg, my_pre)
     )
 
-    payload_rows = 2 * query_count + 8
+    payload_width = 2 * embed_width + 128
     payload = call(
         query_kernel,
-        jax.ShapeDtypeStruct((payload_rows, embed_width), f32),
+        jax.ShapeDtypeStruct((query_count, payload_width), f32),
         4 * query_count * 512 * embed_width,
         1 << 20,
         10,
-        in_specs=[SMEM] + [VMEM] * 3,
+        in_specs=[VMEM] * 3,
         out_specs=VMEM,
-    )(here, got, some_neg, other_neg)
+    )(got, some_neg, other_neg)
     own = lax.all_gather(payload.astype(f16), "z", axis=0, tiled=True).astype(bf16)
-    own = own.reshape(Z, payload_rows, embed_width)
     sib = lax.ppermute(own, "c", SIBLING)
 
     node_grads = call(
@@ -341,8 +345,8 @@
         in_specs=[
             pl.BlockSpec((3, OWN, line_count), lambda i: (0, i, 0)),
             pl.BlockSpec((3, OWN, line_count), lambda i: (0, i, 0)),
-            pl.BlockSpec((Z, payload_rows, embed_width), lambda i: (0, 0, 0)),
-            pl.BlockSpec((Z, payload_rows, embed_width), lambda i: (0, 0, 0)),
+            pl.BlockSpec((line_count, payload_width), lambda i: (0, 0)),
+            pl.BlockSpec((line_count, payload_width), lambda i: (0, 0)),
             pl.BlockSpec((OWN, embed_width), lambda i: (i, 0)),
             pl.BlockSpec((X * Y, embed_width), lambda i: (0, 0)),
         ],

time: 275 us -> 273 us (level)
    unnamed x35 -> x29, local copies, waits for them, and re-layouts: 6.7 us -> 3.42 us
where the time goes in v8:
time: 273 us; the launch traced here: 271 us
  blocking collectives  107 us (39%)
  waiting for transfers between devices  58.8 us (22%)
  Pallas kernels  41.7 us (15%)
  starting transfers between devices  21.5 us (8%)
  local copies, waits for them, and re-layouts  14.5 us (5%)
  between operations  13.7 us (5%)
  matrix products  12.2 us (4%)
    all_gather x1, blocking collectives, on_device(): lax.all_gather(payload.astype(f16), 'z', axis=0, tiled=True).astype(bf16)  43 us
    all_to_all x1, blocking collectives, on_device(): lax.all_to_all(node_grads, ('x', 'y'), split_axis=0, concat_axis=0, tiled...  37 us
    reduce_scatter x1, waiting for transfers between devices, on_device(): lax.psum_scatter(part.reshape(3, line_count, embed_width), 'z', scatter_d...  36.7 us
    all_to_all x1, waiting for transfers between devices, on_device(): lax.all_to_all(copies, 'z', split_axis=0, concat_axis=0, tiled=True)  17.7 us
    all_to_all x1, starting transfers between devices, on_device(): lax.all_to_all(copies, 'z', split_axis=0, concat_axis=0, tiled=True)  15.2 us
    all_gather x1, blocking collectives, on_device(): some_neg = lax.all_gather(line_neg, 'y', axis=0, tiled=True)  13.9 us
    all_gather x1, blocking collectives, on_device(): all_pre_grad = lax.all_gather(pre_grad, 'x', axis=0, tiled=True)  13.6 us
    dot_general x1, matrix products, dot_nn(): lax.dot_general(left, right, (((1,), (0,)), ((), ())), preferred_element_...  12.2 us
  transfers between devices with their start and end apart: 6, of which 3 were waited for; matrix products, arithmetic and copies ran while one was open for 4% of the time, Pallas kernels for 8%

profile of v8, /device:TPU:8, one launch (start us, length us, event | category | flops | bytes accessed | tf_op | source)
XLA Modules:
  0.0 270.8 jit_solution(12961147535010124484)
XLA Ops:
  6.5 0.0 copy-start.11
  6.5 0.0 copy-start.13
  6.5 0.0 all-gather.3.cloned.1.call-start
  6.5 6.1 %shard_map.64 = (f32[288,1024]{1,0:T(8,128)}, bf16[288,1024]{1,0:T(8,128)(2,1)}, bf16[8,1024]{1,0:T(8,128)(2,1)}) custom-call(s32[4]{0:T(128)} %neg_row_ref.3, bf16[256,1024]{1,0:T(8,128)(2,1)} %table_hbm.1, bf16[1024,1024]{1,0:T(8,128)(2,1)} %projection_ref.1), custom_call_target="tpu_custom_call" | custom-call | flops 603979776 | bytes 5242880 | tf_op jit(solution)/shard_map/pallas_call | solution.py:249
  12.6 0.0 all-gather.3.cloned.1.call-update
  12.6 0.0 copy-done.11
  12.7 0.0 copy-done.12
  12.7 0.0 copy-done.13
  12.7 0.1 copy.26
  12.8 0.7 slice.9
  13.6 0.7 broadcast_in_dim.3
  14.3 15.2 %all-to-all-start = ((bf16[16,8,1024]{2,1,0:T(8,128)(2,1)}), bf16[16,8,1024]{2,1,0:T(8,128)(2,1)S(1)}, u32[]{:S(2)}, u32[]{:S(2)}) async-start(bf16[16,8,1024]{2,1,0:T(8,128)(2,1)} %broadcast_in_dim.3), calls=%async_computation | async-start | bytes 524288 | tf_op jit(solution)/shard_map/all_to_all | solution.py:276
  29.5 0.0 reduce-scatter.2.cloned.1.call-start
  29.5 0.6 pad_add_fusion.where_ref
  30.2 17.7 %all-to-all-done.received_ref = bf16[16,8,1024]{2,1,0:T(8,128)(2,1)S(1)} async-done(((bf16[16,8,1024]{2,1,0:T(8,128)(2,1)}), bf16[16,8,1024]{2,1,0:T(8,128)(2,1)S(1)}, u32[]{:S(2)}, u32[]{:S(2)}) %all-to-all-start) | async-done | bytes 262176 | tf_op jit(solution)/shard_map/all_to_all | solution.py:276
  47.9 0.0 copy-start.9
  48.0 0.6 copy-done.9
  48.6 12.1 %shard_map.65 = (bf16[3,512,2304]{2,1,0:T(8,128)(2,1)}, s32[512,16]{1,0:T(8,128)}) custom-call(s32[2]{0:T(128)} %pad_add_fusion.where_ref, bf16[16,8,1024]{2,1,0:T(8,128)(2,1)} %copy-done.9), custom_call_target="tpu_custom_call" | custom-call | flops 56623104 | bytes 7077888 | tf_op jit(solution)/shard_map/pallas_call | solution.py:278
  60.7 0.0 all-gather.3.cloned.1.call-done
  60.7 12.2 %convolution_convert_fusion = bf16[1536,1024]{1,0:T(8,128)(2,1)} fusion(bf16[1536,2304]{1,0:T(8,128)(2,1)} %bitcast.34, bf16[2304,1024]{1,0:T(8,128)(2,1)} %all-gather.3.cloned.1.call-done), kind=kOutput, calls=%fused_computation | convolution fusion | flops 7249330176 | bytes 14942208 | tf_op jit(solution)/shard_map/dot_general | solution.py:45
  72.9 0.0 copy-start.10
  72.9 0.0 reduce-scatter.2.cloned.1.call-update
  72.9 13.9 %all_gather.13.neg_a_ref = bf16[256,1024]{1,0:T(8,128)(2,1)} all-gather(bf16[64,1024]{1,0:T(8,128)(2,1)S(1)} %reshape.33), channel_id=1, replica_groups=mesh['y'=4,'z'=16,'c'=2,'x'=4] {'y'}, dimensions={0}, use_global_device_ids=true | all-gather | bytes 655360 | tf_op jit(solution)/shard_map/all_gather | solution.py:304
  86.8 1.9 collective-permute-start.1
  88.7 1.7 constant_dynamic-slice_fusion.pre_ref
  90.4 0.0 copy-done.10
  90.4 0.7 copy.22
  91.1 2.4 collective-permute-start
  93.5 2.0 constant_dynamic-slice_fusion.1
  95.6 1.8 copy.28
  97.4 0.0 copy-start.7
  97.4 2.7 copy.25
  100.1 0.6 reshape_squeeze.3.neg_ref
  100.7 0.0 copy-done.7
  100.7 4.8 %shard_map.66.own_w_ref = bf16[3,1152,512]{2,1,0:T(8,128)(2,1)S(1)} custom-call(s32[2]{0:T(128)S(1)} %copy-done.7, s32[16,512]{1,0:T(8,128)} %bitcast.9.line_ref), custom_call_target="tpu_custom_call" | custom-call | flops 28311552 | bytes 3538944 | tf_op jit(solution)/shard_map/pallas_call | solution.py:309
  105.6 0.0 collective-permute-done
  105.6 4.8 %shard_map.67.sib_w_ref = bf16[3,1152,512]{2,1,0:T(8,128)(2,1)S(1)} custom-call(s32[2]{0:T(128)S(1)} %copy-done.7, s32[16,512]{1,0:T(8,128)} %bitcast.10.line_ref), custom_call_target="tpu_custom_call" | custom-call | flops 28311552 | bytes 3538944 | tf_op jit(solution)/shard_map/pallas_call | solution.py:309
  110.4 0.0 copy-start.1
  110.4 1.7 copy-done.1
  112.2 0.0 collective-permute-done.1.neg_b_ref
  112.2 36.7 %reduce-scatter.2.cloned.1.call-done.got_ref = bf16[3,32,1024]{2,1,0:T(8,128)(2,1)} async-done(((bf16[3,512,1024]{2,1,0:T(8,128)(2,1)}), bf16[3,32,1024]{2,1,0:T(8,128)(2,1)}) %reduce-scatter.2.cloned.1.call-update) | async-done | bytes 196624 | tf_op jit(solution)/shard_map/reduce_scatter | solution.py:296
  148.9 0.9 copy-done.5
  149.8 2.0 shard_map.68
  151.9 0.0 copy-start.2
  151.9 0.0 copy-start.3
  151.9 0.0 copy-start.6
  151.9 43.0 %all-gather.4 = f16[512,2176]{1,0:T(8,128)(2,1)S(1)} all-gather(f16[32,2176]{1,0:T(8,128)(2,1)S(1)} %convert_element_type.13), channel_id=1, replica_groups=mesh['y'=4,'z'=16,'c'=2,'x'=4] {'z'}, dimensions={0}, use_global_device_ids=true | all-gather | bytes 2367488 | tf_op jit(solution)/shard_map/all_gather | solution.py:335
  194.9 0.3 convert_element_type.14.own_ref
  195.2 1.9 collective-permute-start.2
  197.2 4.3 %collective-permute-done.2.sib_ref = bf16[512,2176]{1,0:T(8,128)(2,1)S(1)} collective-permute-done((bf16[512,2176]{1,0:T(8,128)(2,1)S(1)}, bf16[512,2176]{1,0:T(8,128)(2,1)S(1)}, u32[]{:S(2)}, u32[]{:S(2)}) %collective-permute-start.2) | collective-permute-done | bytes 2228256 | tf_op jit(solution)/shard_map/ppermute | solution.py:336
  201.5 0.0 copy-done.2
  201.5 0.0 copy-done.3
  201.5 0.0 copy-done.6
  201.5 8.6 %shard_map.69 = bf16[1152,1024]{1,0:T(8,128)(2,1)S(1)} custom-call(bf16[3,1152,512]{2,1,0:T(8,128)(2,1)S(1)} %shard_map.66.own_w_ref, bf16[3,1152,512]{2,1,0:T(8,128)(2,1)S(1)} %copy-done.2, bf16[512,2176]{1,0:T(8,128)(2,1)S(1)} %convert_element_type.14.own_ref, bf16[512,2176]{1,0:T(8,128)(2,1)S(1)} %collective-permute-done.2.sib_ref, ...), custom_call_target="tpu_custom_call" | custom-call | flops 4831838208 | bytes 16777216 | tf_op jit(solution)/shard_map/pallas_call | solution.py:338
  210.1 0.0 copy-start.4
  210.1 0.0 copy-start
  210.1 0.0 copy-start.8
  210.2 37.0 %all_to_all.14.pieces_ref = bf16[16,72,1024]{2,1,0:T(8,128)(2,1)S(1)} all-to-all(bf16[16,72,1024]{2,1,0:T(8,128)(2,1)S(1)} %bitcast.27), channel_id=1, replica_groups=mesh['y'=4,'z'=16,'c'=2,'x'=4] {'x','y'}, dimensions={0} | all-to-all | bytes 4718592 | tf_op jit(solution)/shard_map/all_to_all | solution.py:357
  247.1 0.0 copy-done.4
  247.1 0.5 shard_map.70
  247.7 13.6 %all_gather.15.grad_ref = bf16[288,1024]{1,0:T(8,128)(2,1)S(1)} all-gather(bf16[72,1024]{1,0:T(8,128)(2,1)S(1)} %shard_map.70), channel_id=1, replica_groups=mesh['y'=4,'z'=16,'c'=2,'x'=4] {'x'}, dimensions={0}, use_global_device_ids=true | all-gather | bytes 737280 | tf_op jit(solution)/shard_map/all_gather | solution.py:367
  261.3 0.0 copy-done
  261.3 0.0 copy-done.8
  261.3 2.7 %shard_map.71 = f32[256,1024]{1,0:T(8,128)} custom-call(s32[4]{0:T(128)S(1)} %copy-done.8, bf16[288,1024]{1,0:T(8,128)(2,1)S(1)} %all_gather.15.grad_ref, bf16[1024,1024]{1,0:T(8,128)(2,1)S(1)} %copy-done), custom_call_target="tpu_custom_call" | custom-call | flops 603979776 | bytes 4194304 | tf_op jit(solution)/shard_map/pallas_call | solution.py:368
  (12 shorter events, 0.2 us)
Async XLA Ops:
  6.5 6.1 %copy-start.11 = (s32[32,16]{0,1:T(8,128)S(1)}, s32[32,16]{0,1:T(8,128)}, u32[]{:S(2)}) copy-start(s32[32,16]{0,1:T(8,128)} %param.9) | copy-start | bytes 6148
  6.5 6.1 %copy-start.12 = (s32[32,13]{0,1:T(8,128)S(1)}, s32[32,13]{0,1:T(8,128)}, u32[]{:S(2)}) copy-start(s32[32,13]{0,1:T(8,128)} %param.10) | copy-start | bytes 4996
  6.5 6.1 %copy-start.13 = (s32[32,16,1]{0,2,1:T(1,128)S(1)}, s32[32,16,1]{0,2,1:T(1,128)}, u32[]{:S(2)}) copy-start(s32[32,16,1]{0,2,1:T(1,128)} %param.8) | copy-start | bytes 6148
  6.5 54.1 %all-gather.3.cloned.1.call-start = ((), (), s32[]{:S(2)}) async-start(), calls=%async_computation.3 | async-start | bytes 5308416 | tf_op jit(solution)/shard_map/all_gather | solution.py:267
  14.3 33.6 %all-to-all-start = ((bf16[16,8,1024]{2,1,0:T(8,128)(2,1)}), bf16[16,8,1024]{2,1,0:T(8,128)(2,1)S(1)}, u32[]{:S(2)}, u32[]{:S(2)}) async-start(bf16[16,8,1024]{2,1,0:T(8,128)(2,1)} %broadcast_in_dim.3), calls=%async_computation | async-start | bytes 524288 | tf_op jit(solution)/shard_map/all_to_all | solution.py:276
  29.5 119.4 %reduce-scatter.2.cloned.1.call-start = ((), (), s32[]{:S(2)}) async-start(), calls=%async_computation.4 | async-start | bytes 3342336 | tf_op jit(solution)/shard_map/reduce_scatter | solution.py:296
  47.9 0.7 copy-start.9
  72.9 17.5 %copy-start.10 = (s32[512,16]{1,0:T(8,128)S(1)}, s32[512,16]{1,0:T(8,128)}, u32[]{:S(2)}) copy-start(s32[512,16]{1,0:T(8,128)} %get-tuple-element.27) | copy-start | bytes 98308
  86.8 25.4 %collective-permute-start.1 = (bf16[256,1024]{1,0:T(8,128)(2,1)}, bf16[256,1024]{1,0:T(8,128)(2,1)}, u32[]{:S(2)}, u32[]{:S(2)}) collective-permute-start(bf16[256,1024]{1,0:T(8,128)(2,1)} %all_gather.13.neg_a_ref), channel_id=1, source_target_pairs={{0,4},{4,0},{1,5},{5,1},{2,6},{6,2},{3,7},{7,3},{8,12},{12,8},{9,1... | collective-permute-start | bytes 1572872 | tf_op jit(solution)/shard_map/ppermute | solution.py:305
  91.1 14.4 %collective-permute-start = (s32[512,16]{0,1:T(8,128)}, s32[512,16]{0,1:T(8,128)}, u32[]{:S(2)}, u32[]{:S(2)}) collective-permute-start(s32[512,16]{0,1:T(8,128)} %copy.22), channel_id=1, source_target_pairs={{0,4},{4,0},{1,5},{5,1},{2,6},{6,2},{3,7},{7,3},{8,12},{12,8},{9,1... | collective-permute-start | bytes 98312 | tf_op jit(solution)/shard_map/ppermute | solution.py:306
  97.4 3.4 %copy-start.7 = (s32[2]{0:T(128)S(1)}, s32[2]{0:T(128)}, u32[]{:S(2)}) copy-start(s32[2]{0:T(128)} %pad_add_fusion.where_ref) | copy-start | bytes 28
  110.4 1.8 copy-start.1
  148.9 0.9 copy-start.5
  151.9 49.6 %copy-start.2 = (bf16[3,1152,512]{2,1,0:T(8,128)(2,1)S(1)}, bf16[3,1152,512]{2,1,0:T(8,128)(2,1)}, u32[]{:S(2)}) copy-start(bf16[3,1152,512]{2,1,0:T(8,128)(2,1)} %copy-done.1) | copy-start | bytes 10616836
  151.9 49.6 %copy-start.3 = (bf16[4,4,72,1024]{3,2,1,0:T(8,128)(2,1)S(1)}, bf16[4,4,72,1024]{3,2,1,0:T(8,128)(2,1)}, u32[]{:S(2)}) copy-start(bf16[4,4,72,1024]{3,2,1,0:T(8,128)(2,1)} %copy.25) | copy-start | bytes 7077892
  151.9 49.6 %copy-start.6 = (bf16[16,1024]{1,0:T(8,128)(2,1)S(1)}, bf16[16,1024]{1,0:T(8,128)(2,1)}, u32[]{:S(2)}) copy-start(bf16[16,1024]{1,0:T(8,128)(2,1)} %reshape_squeeze.3.neg_ref) | copy-start | bytes 98308
  195.2 6.2 %collective-permute-start.2 = (bf16[512,2176]{1,0:T(8,128)(2,1)S(1)}, bf16[512,2176]{1,0:T(8,128)(2,1)S(1)}, u32[]{:S(2)}, u32[]{:S(2)}) collective-permute-start(bf16[512,2176]{1,0:T(8,128)(2,1)S(1)} %convert_element_type.14.own_ref), channel_id=1, source_target_pairs={{0,4},{4,0},{1,5},{5,1},{2,6},{6,2},{3,7},{7,3},{8,12},{12,8},{9,1... | collective-permute-start | bytes 6684680 | tf_op jit(solution)/shard_map/ppermute | solution.py:336
  210.1 37.0 %copy-start.4 = (f32[72,1024]{1,0:T(8,128)S(1)}, f32[72,1024]{1,0:T(8,128)}, u32[]{:S(2)}) copy-start(f32[72,1024]{1,0:T(8,128)} %constant_dynamic-slice_fusion.pre_ref) | copy-start | bytes 884740
  210.1 51.2 %copy-start = (bf16[1024,1024]{1,0:T(8,128)(2,1)S(1)}, bf16[1024,1024]{1,0:T(8,128)(2,1)}, u32[]{:S(2)}) copy-start(bf16[1024,1024]{1,0:T(8,128)(2,1)} %projection_ref.1) | copy-start | bytes 6291460
  210.1 51.1 %copy-start.8 = (s32[4]{0:T(128)S(1)}, s32[4]{0:T(128)}, u32[]{:S(2)}) copy-start(s32[4]{0:T(128)} %neg_row_ref.3) | copy-start | bytes 52
Sparse Core Ops, SparseCore 0:
  12.8 45.3 all-gather.2
  73.0 75.8 reduce-scatter.1

commit v9 on v8

--- a/solution.py
+++ b/solution.py
@@ -165,39 +165,39 @@
     out_ref[:, 2 * width :] = scalars
 
 
-def node_grad_kernel(own_w_ref, sib_w_ref, own_ref, sib_ref, plane_ref, neg_ref, out_ref, row_ref, neg_w_ref):
+def node_grad_kernel(*refs):
+    weight_ref, ref, plane_ref, neg_ref = refs[:4]
+    out_ref, row_ref, neg_w_ref = refs[-3:]
     step = pl.program_id(0)
     width = plane_ref.shape[1]
-    received = (own_ref, sib_ref)
 
     @pl.when(step == 0)
     def _():
-        for side, ref in enumerate(received):
-            scalars = ref[:, 2 * width :].astype(f32).T
-            total = scalars[1:2] + scalars[2:3]
-            hard = scalars[3:4] + scalars[4:5]
-            row_ref[side, 0:1] = scalars[0:1] * 0.0625
-            row_ref[side, 1:2] = -total / (scalars[5:6] + scalars[6:7])
-            row_ref[side, 2:3] = hard / (scalars[7:8] + scalars[8:9])
-            scores = dot_nt(neg_ref[...], ref[:, width : 2 * width])
-            neg_w_ref[side] = weigh(scores, scalars[9:10] + scalars[10:11])
+        scalars = ref[:, 2 * width :].astype(f32).T
+        total = scalars[1:2] + scalars[2:3]
+        hard = scalars[3:4] + scalars[4:5]
+        row_ref[0:1] = scalars[0:1] * 0.0625
+        row_ref[1:2] = -total / (scalars[5:6] + scalars[6:7])
+        row_ref[2:3] = hard / (scalars[7:8] + scalars[8:9])
+        scores = dot_nt(neg_ref[...], ref[:, width : 2 * width])
+        neg_w_ref[...] = weigh(scores, scalars[9:10] + scalars[10:11])
 
     negs = neg_ref.shape[0]
     rows = lax.broadcasted_iota(jnp.int32, (OWN, negs), 0) + step * OWN
     spot = jnp.where(rows == lax.broadcasted_iota(jnp.int32, (OWN, negs), 1) * BLOCK + PART, 1.0, 0.0).astype(bf16)
-    hood_part = jnp.zeros((OWN, width), f32)
-    query_part = jnp.zeros((OWN, width), f32)
-    for side, (w_ref, ref) in enumerate(((own_w_ref, own_ref), (sib_w_ref, sib_ref))):
-        w_hood = (w_ref[0].astype(f32) * row_ref[side, 0:1]).astype(bf16)
-        hood_part = hood_part + dot_nn(w_hood, ref[:, 0:width])
-        w_query = w_ref[1].astype(f32) * row_ref[side, 1:2] + w_ref[2].astype(f32) * row_ref[side, 2:3]
-        w_query = (w_query + dot_nn(spot, neg_w_ref[side])).astype(bf16)
-        query_part = query_part + dot_nn(w_query, ref[:, width : 2 * width])
+    w_hood = (weight_ref[0].astype(f32) * row_ref[0:1]).astype(bf16)
+    hood_part = dot_nn(w_hood, ref[:, 0:width])
+    w_query = weight_ref[1].astype(f32) * row_ref[1:2] + weight_ref[2].astype(f32) * row_ref[2:3]
+    w_query = (w_query + dot_nn(spot, neg_w_ref[...])).astype(bf16)
+    query_part = dot_nn(w_query, ref[:, width : 2 * width])
     plane = plane_ref[...].astype(f32)
     place = lax.broadcasted_iota(jnp.int32, (OWN, 1), 0) % BLOCK
     inverse = jnp.where(place == PART, 0.0, 1.0 / (row_sum(plane * plane) + epsilon))
     query_part = query_part - plane * (inverse * row_sum(plane * query_part))
-    out_ref[...] = (hood_part + query_part).astype(bf16)
+    result = hood_part + query_part
+    if len(refs) > 7:
+        result = result + refs[4][...]
+    out_ref[...] = result.astype(out_ref.dtype)
 
 
 def owner_kernel(pieces_ref, pre_ref, out_ref):
@@ -335,24 +335,28 @@
     own = lax.all_gather(payload.astype(f16), "z", axis=0, tiled=True).astype(bf16)
     sib = lax.ppermute(own, "c", SIBLING)
 
-    node_grads = call(
-        node_grad_kernel,
-        jax.ShapeDtypeStruct((NARROW, embed_width), bf16),
-        8 * line_count * NARROW * embed_width,
-        16 << 20,
-        36,
-        grid=(X,),
-        in_specs=[
-            pl.BlockSpec((3, OWN, line_count), lambda i: (0, i, 0)),
-            pl.BlockSpec((3, OWN, line_count), lambda i: (0, i, 0)),
-            pl.BlockSpec((line_count, payload_width), lambda i: (0, 0)),
-            pl.BlockSpec((line_count, payload_width), lambda i: (0, 0)),
-            pl.BlockSpec((OWN, embed_width), lambda i: (i, 0)),
-            pl.BlockSpec((X * Y, embed_width), lambda i: (0, 0)),
-        ],
-        out_specs=pl.BlockSpec((OWN, embed_width), lambda i: (i, 0)),
-        scratch_shapes=[pltpu.VMEM((2, 8, line_count), f32), pltpu.VMEM((2, X * Y, line_count), bf16)],
-    )(own_w, sib_w, own, sib, core_plane, core_neg)
+    block = pl.BlockSpec((OWN, embed_width), lambda i: (i, 0))
+
+    def node_side(weights, vectors, kind, *before):
+        return call(
+            node_grad_kernel,
+            jax.ShapeDtypeStruct((NARROW, embed_width), kind),
+            4 * line_count * NARROW * embed_width,
+            10 << 20,
+            28,
+            grid=(X,),
+            in_specs=[
+                pl.BlockSpec((3, OWN, line_count), lambda i: (0, i, 0)),
+                pl.BlockSpec((line_count, payload_width), lambda i: (0, 0)),
+                block,
+                pl.BlockSpec((X * Y, embed_width), lambda i: (0, 0)),
+            ]
+            + [block] * len(before),
+            out_specs=block,
+            scratch_shapes=[pltpu.VMEM((8, line_count), f32), pltpu.VMEM((X * Y, line_count), bf16)],
+        )(weights, vectors, core_plane, core_neg, *before)
+
+    node_grads = node_side(sib_w, sib, bf16, node_side(own_w, own, f32))
 
     pieces = lax.all_to_all(node_grads, ("x", "y"), split_axis=0, concat_axis=0, tiled=True)
     pre_grad = call(

time: 273 us -> 269 us (0.985)
    ppermute x1, waiting for transfers between devices: 4.31 us -> 0.01 us  [on_device(): sib = lax.ppermute(own, 'c', SIBLING)]
    pallas_call x1 -> x2, Pallas kernels: 8.63 us -> 9.3 us  [node_side(): call(node_grad_kernel, jax.ShapeDtypeStruct((NARROW, embed_width), kind),...]
  transfers between devices with their start and end apart: 6 -> 6, of which waited for: 3 -> 2; matrix products, arithmetic and copies ran while one was open for 4% -> 3% of each run, Pallas kernels for 8% -> 10%
where the time goes in v9:
time: 269 us; the launch traced here: 268 us
  blocking collectives  108 us (40%)
  waiting for transfers between devices  56.7 us (21%)
  Pallas kernels  41.8 us (16%)
  starting transfers between devices  21.7 us (8%)
  between operations  13.7 us (5%)
  local copies, waits for them, and re-layouts  12.9 us (5%)
  matrix products  12.2 us (5%)
    all_gather x1, blocking collectives, on_device(): lax.all_gather(payload.astype(f16), 'z', axis=0, tiled=True).astype(bf16)  43.3 us
    reduce_scatter x1, waiting for transfers between devices, on_device(): lax.psum_scatter(part.reshape(3, line_count, embed_width), 'z', scatter_d...  39 us
    all_to_all x1, blocking collectives, on_device(): lax.all_to_all(node_grads, ('x', 'y'), split_axis=0, concat_axis=0, tiled...  37.3 us
    all_to_all x1, waiting for transfers between devices, on_device(): lax.all_to_all(copies, 'z', split_axis=0, concat_axis=0, tiled=True)  17.7 us
    all_to_all x1, starting transfers between devices, on_device(): lax.all_to_all(copies, 'z', split_axis=0, concat_axis=0, tiled=True)  15.2 us
    all_gather x1, blocking collectives, on_device(): all_pre_grad = lax.all_gather(pre_grad, 'x', axis=0, tiled=True)  13.6 us
    all_gather x1, blocking collectives, on_device(): some_neg = lax.all_gather(line_neg, 'y', axis=0, tiled=True)  13.3 us
    dot_general x1, matrix products, dot_nn(): lax.dot_general(left, right, (((1,), (0,)), ((), ())), preferred_element_...  12.2 us
  transfers between devices with their start and end apart: 6, of which 2 were waited for; matrix products, arithmetic and copies ran while one was open for 3% of the time, Pallas kernels for 10%

profile of v9, /device:TPU:8, one launch (start us, length us, event | category | flops | bytes accessed | tf_op | source)
XLA Modules:
  0.0 267.6 jit_solution(7449139709101074156)
XLA Ops:
  6.5 0.0 copy-start.10
  6.5 0.0 copy-start.11
  6.5 0.0 copy-start.12
  6.5 0.0 all-gather.3.cloned.1.call-start
  6.5 6.1 %shard_map.64 = (f32[288,1024]{1,0:T(8,128)}, bf16[288,1024]{1,0:T(8,128)(2,1)}, bf16[8,1024]{1,0:T(8,128)(2,1)}) custom-call(s32[4]{0:T(128)} %neg_row_ref.3, bf16[256,1024]{1,0:T(8,128)(2,1)} %table_hbm.1, bf16[1024,1024]{1,0:T(8,128)(2,1)} %projection_ref.1), custom_call_target="tpu_custom_call" | custom-call | flops 603979776 | bytes 5242880 | tf_op jit(solution)/shard_map/pallas_call | solution.py:249
  12.6 0.0 all-gather.3.cloned.1.call-update
  12.6 0.0 copy-done.10
  12.7 0.0 copy-done.11
  12.7 0.0 copy-done.12
  12.7 0.1 copy.26
  12.8 0.7 slice.9
  13.6 0.7 broadcast_in_dim.3
  14.3 15.2 %all-to-all-start = ((bf16[16,8,1024]{2,1,0:T(8,128)(2,1)}), bf16[16,8,1024]{2,1,0:T(8,128)(2,1)S(1)}, u32[]{:S(2)}, u32[]{:S(2)}) async-start(bf16[16,8,1024]{2,1,0:T(8,128)(2,1)} %broadcast_in_dim.3), calls=%async_computation | async-start | bytes 524288 | tf_op jit(solution)/shard_map/all_to_all | solution.py:276
  29.5 0.0 reduce-scatter.2.cloned.1.call-start
  29.5 0.6 pad_add_fusion.where_ref
  30.1 17.7 %all-to-all-done.received_ref = bf16[16,8,1024]{2,1,0:T(8,128)(2,1)S(1)} async-done(((bf16[16,8,1024]{2,1,0:T(8,128)(2,1)}), bf16[16,8,1024]{2,1,0:T(8,128)(2,1)S(1)}, u32[]{:S(2)}, u32[]{:S(2)}) %all-to-all-start) | async-done | bytes 262176 | tf_op jit(solution)/shard_map/all_to_all | solution.py:276
  47.9 0.0 copy-start.8
  48.0 0.6 copy-done.8
  48.6 12.1 %shard_map.65 = (bf16[3,512,2304]{2,1,0:T(8,128)(2,1)}, s32[512,16]{1,0:T(8,128)}) custom-call(s32[2]{0:T(128)} %pad_add_fusion.where_ref, bf16[16,8,1024]{2,1,0:T(8,128)(2,1)} %copy-done.8), custom_call_target="tpu_custom_call" | custom-call | flops 56623104 | bytes 7077888 | tf_op jit(solution)/shard_map/pallas_call | solution.py:278
  60.7 0.0 all-gather.3.cloned.1.call-done
  60.7 12.2 %convolution_convert_fusion = bf16[1536,1024]{1,0:T(8,128)(2,1)} fusion(bf16[1536,2304]{1,0:T(8,128)(2,1)} %bitcast.37, bf16[2304,1024]{1,0:T(8,128)(2,1)} %all-gather.3.cloned.1.call-done), kind=kOutput, calls=%fused_computation | convolution fusion | flops 7249330176 | bytes 14942208 | tf_op jit(solution)/shard_map/dot_general | solution.py:45
  72.9 0.0 copy-start.9
  72.9 0.0 reduce-scatter.2.cloned.1.call-update
  72.9 13.3 %all_gather.13.neg_a_ref = bf16[256,1024]{1,0:T(8,128)(2,1)S(1)} all-gather(bf16[64,1024]{1,0:T(8,128)(2,1)S(1)} %reshape.33), channel_id=1, replica_groups=mesh['y'=4,'z'=16,'c'=2,'x'=4] {'y'}, dimensions={0}, use_global_device_ids=true | all-gather | bytes 655360 | tf_op jit(solution)/shard_map/all_gather | solution.py:304
  86.3 1.9 collective-permute-start.1
  88.2 1.0 constant_dynamic-slice_fusion.pre_ref
  89.2 0.0 copy-done.9
  89.2 0.1 copy.22
  89.3 2.4 collective-permute-start
  91.7 1.9 constant_dynamic-slice_fusion.1
  93.6 1.8 copy.28
  95.5 0.0 copy-start.6
  95.5 1.3 copy.25
  96.8 0.0 copy-done.6
  96.8 4.6 %shard_map.66.refs_0_ = bf16[3,1152,512]{2,1,0:T(8,128)(2,1)S(1)} custom-call(s32[2]{0:T(128)S(1)} %copy-done.6, s32[16,512]{1,0:T(8,128)S(1)} %bitcast.29), custom_call_target="tpu_custom_call" | custom-call | flops 28311552 | bytes 3538944 | tf_op jit(solution)/shard_map/pallas_call | solution.py:309
  101.4 0.0 copy-start
  101.5 1.8 copy-done
  103.2 0.0 collective-permute-done
  103.2 4.6 %shard_map.67.refs_0_ = bf16[3,1152,512]{2,1,0:T(8,128)(2,1)S(1)} custom-call(s32[2]{0:T(128)S(1)} %copy-done.6, s32[16,512]{1,0:T(8,128)S(1)} %bitcast.30), custom_call_target="tpu_custom_call" | custom-call | flops 28311552 | bytes 3538944 | tf_op jit(solution)/shard_map/pallas_call | solution.py:309
  107.8 0.0 copy-start.2
  107.8 1.8 copy-done.2
  109.6 0.0 collective-permute-done.1.neg_b_ref
  109.6 39.0 %reduce-scatter.2.cloned.1.call-done.got_ref = bf16[3,32,1024]{2,1,0:T(8,128)(2,1)} async-done(((bf16[3,512,1024]{2,1,0:T(8,128)(2,1)}), bf16[3,32,1024]{2,1,0:T(8,128)(2,1)}) %reduce-scatter.2.cloned.1.call-update) | async-done | bytes 196624 | tf_op jit(solution)/shard_map/reduce_scatter | solution.py:296
  148.6 0.0 copy-start.5
  148.6 0.9 copy-done.5
  149.5 1.9 shard_map.68
  151.4 0.0 copy-start.1
  151.4 43.3 %all-gather.4 = f16[512,2176]{1,0:T(8,128)(2,1)S(1)} all-gather(f16[32,2176]{1,0:T(8,128)(2,1)S(1)} %convert_element_type.13), channel_id=1, replica_groups=mesh['y'=4,'z'=16,'c'=2,'x'=4] {'z'}, dimensions={0}, use_global_device_ids=true | all-gather | bytes 2367488 | tf_op jit(solution)/shard_map/all_gather | solution.py:335
  194.7 0.3 convert_element_type.14.refs_1_
  195.0 0.0 copy-start.3
  195.0 2.2 collective-permute-start.2
  197.2 0.0 copy-done.1
  197.2 4.6 %shard_map.69.refs_4_ = f32[1152,1024]{1,0:T(8,128)S(1)} custom-call(bf16[3,1152,512]{2,1,0:T(8,128)(2,1)S(1)} %copy-done.1, bf16[512,2176]{1,0:T(8,128)(2,1)S(1)} %convert_element_type.14.refs_1_, bf16[1152,1024]{1,0:T(8,128)(2,1)S(1)} %bitcast.26, bf16[16,1024]{1,0:T(8,128)(2,1)S(1)} %reshape_squeeze.3.refs_3_), custom_call_target="tpu_custom_call" | custom-call | flops 2415919104 | bytes 10485760 | tf_op jit(solution)/shard_map/pallas_call | solution.py:341
  201.7 0.0 collective-permute-done.2.refs_1_
  201.8 0.0 copy-done.3
  201.8 4.7 %shard_map.70 = bf16[1152,1024]{1,0:T(8,128)(2,1)S(1)} custom-call(bf16[3,1152,512]{2,1,0:T(8,128)(2,1)S(1)} %copy-done.3, bf16[512,2176]{1,0:T(8,128)(2,1)S(1)} %collective-permute-done.2.refs_1_, bf16[1152,1024]{1,0:T(8,128)(2,1)S(1)} %bitcast.27, bf16[16,1024]{1,0:T(8,128)(2,1)S(1)} %reshape_squeeze.3.refs_3_, f32[1152,1024]{1,0:T(8,128)S(1)} %shard_map.69.refs_4_), custom_call_target="tpu_custom_call" | custom-call | flops 2415919104 | bytes 10485760 | tf_op jit(solution)/shard_map/pallas_call | solution.py:341
  206.5 0.0 copy-start.4
  206.5 0.0 copy-start.7
  206.5 37.3 %all_to_all.14.pieces_ref = bf16[16,72,1024]{2,1,0:T(8,128)(2,1)S(1)} all-to-all(bf16[16,72,1024]{2,1,0:T(8,128)(2,1)S(1)} %bitcast.28), channel_id=1, replica_groups=mesh['y'=4,'z'=16,'c'=2,'x'=4] {'x','y'}, dimensions={0} | all-to-all | bytes 4718592 | tf_op jit(solution)/shard_map/all_to_all | solution.py:361
  243.9 0.5 shard_map.71
  244.4 13.6 %all_gather.15.grad_ref = bf16[288,1024]{1,0:T(8,128)(2,1)S(1)} all-gather(bf16[72,1024]{1,0:T(8,128)(2,1)S(1)} %shard_map.71), channel_id=1, replica_groups=mesh['y'=4,'z'=16,'c'=2,'x'=4] {'x'}, dimensions={0}, use_global_device_ids=true | all-gather | bytes 737280 | tf_op jit(solution)/shard_map/all_gather | solution.py:371
  258.1 0.0 copy-done.4
  258.1 0.0 copy-done.7
  258.1 2.7 %shard_map.72 = f32[256,1024]{1,0:T(8,128)} custom-call(s32[4]{0:T(128)S(1)} %copy-done.7, bf16[288,1024]{1,0:T(8,128)(2,1)S(1)} %all_gather.15.grad_ref, bf16[1024,1024]{1,0:T(8,128)(2,1)S(1)} %copy-done.4), custom_call_target="tpu_custom_call" | custom-call | flops 603979776 | bytes 4194304 | tf_op jit(solution)/shard_map/pallas_call | solution.py:372
  (11 shorter events, 0.2 us)
Async XLA Ops:
  6.5 6.1 %copy-start.10 = (s32[32,16]{0,1:T(8,128)S(1)}, s32[32,16]{0,1:T(8,128)}, u32[]{:S(2)}) copy-start(s32[32,16]{0,1:T(8,128)} %param.9) | copy-start | bytes 6148
  6.5 6.1 %copy-start.11 = (s32[32,13]{0,1:T(8,128)S(1)}, s32[32,13]{0,1:T(8,128)}, u32[]{:S(2)}) copy-start(s32[32,13]{0,1:T(8,128)} %param.10) | copy-start | bytes 4996
  6.5 6.1 %copy-start.12 = (s32[32,16,1]{0,2,1:T(1,128)S(1)}, s32[32,16,1]{0,2,1:T(1,128)}, u32[]{:S(2)}) copy-start(s32[32,16,1]{0,2,1:T(1,128)} %param.8) | copy-start | bytes 6148
  6.5 54.2 %all-gather.3.cloned.1.call-start = ((), (), s32[]{:S(2)}) async-start(), calls=%async_computation.3 | async-start | bytes 5308416 | tf_op jit(solution)/shard_map/all_gather | solution.py:267
  14.3 33.6 %all-to-all-start = ((bf16[16,8,1024]{2,1,0:T(8,128)(2,1)}), bf16[16,8,1024]{2,1,0:T(8,128)(2,1)S(1)}, u32[]{:S(2)}, u32[]{:S(2)}) async-start(bf16[16,8,1024]{2,1,0:T(8,128)(2,1)} %broadcast_in_dim.3), calls=%async_computation | async-start | bytes 524288 | tf_op jit(solution)/shard_map/all_to_all | solution.py:276
  29.5 119.1 %reduce-scatter.2.cloned.1.call-start = ((), (), s32[]{:S(2)}) async-start(), calls=%async_computation.4 | async-start | bytes 3342336 | tf_op jit(solution)/shard_map/reduce_scatter | solution.py:296
  47.9 0.7 copy-start.8
  72.9 16.3 %copy-start.9 = (s32[512,16]{1,0:T(8,128)S(1)}, s32[512,16]{1,0:T(8,128)}, u32[]{:S(2)}) copy-start(s32[512,16]{1,0:T(8,128)} %get-tuple-element.27) | copy-start | bytes 98308
  86.3 23.3 %collective-permute-start.1 = (bf16[256,1024]{1,0:T(8,128)(2,1)S(1)}, bf16[256,1024]{1,0:T(8,128)(2,1)}, u32[]{:S(2)}, u32[]{:S(2)}) collective-permute-start(bf16[256,1024]{1,0:T(8,128)(2,1)S(1)} %all_gather.13.neg_a_ref), channel_id=1, source_target_pairs={{0,4},{4,0},{1,5},{5,1},{2,6},{6,2},{3,7},{7,3},{8,12},{12,8},{9,1... | collective-permute-start | bytes 1572872 | tf_op jit(solution)/shard_map/ppermute | solution.py:305
  89.3 13.9 %collective-permute-start = (s32[512,16]{0,1:T(8,128)S(1)}, s32[512,16]{0,1:T(8,128)S(1)}, u32[]{:S(2)}, u32[]{:S(2)}) collective-permute-start(s32[512,16]{0,1:T(8,128)S(1)} %copy.22), channel_id=1, source_target_pairs={{0,4},{4,0},{1,5},{5,1},{2,6},{6,2},{3,7},{7,3},{8,12},{12,8},{9,1... | collective-permute-start | bytes 98312 | tf_op jit(solution)/shard_map/ppermute | solution.py:306
  95.5 1.4 copy-start.6
  101.4 1.8 copy-start
  107.8 1.8 copy-start.2
  148.6 0.9 copy-start.5
  151.4 45.8 %copy-start.1 = (bf16[3,1152,512]{2,1,0:T(8,128)(2,1)S(1)}, bf16[3,1152,512]{2,1,0:T(8,128)(2,1)}, u32[]{:S(2)}) copy-start(bf16[3,1152,512]{2,1,0:T(8,128)(2,1)} %copy-done) | copy-start | bytes 10616836
  195.0 6.8 %copy-start.3 = (bf16[3,1152,512]{2,1,0:T(8,128)(2,1)S(1)}, bf16[3,1152,512]{2,1,0:T(8,128)(2,1)}, u32[]{:S(2)}) copy-start(bf16[3,1152,512]{2,1,0:T(8,128)(2,1)} %copy-done.2) | copy-start | bytes 10616836
  195.0 6.8 %collective-permute-start.2 = (bf16[512,2176]{1,0:T(8,128)(2,1)S(1)}, bf16[512,2176]{1,0:T(8,128)(2,1)S(1)}, u32[]{:S(2)}, u32[]{:S(2)}) collective-permute-start(bf16[512,2176]{1,0:T(8,128)(2,1)S(1)} %convert_element_type.14.refs_1_), channel_id=1, source_target_pairs={{0,4},{4,0},{1,5},{5,1},{2,6},{6,2},{3,7},{7,3},{8,12},{12,8},{9,1... | collective-permute-start | bytes 6684680 | tf_op jit(solution)/shard_map/ppermute | solution.py:336
  206.5 51.5 %copy-start.4 = (bf16[1024,1024]{1,0:T(8,128)(2,1)S(1)}, bf16[1024,1024]{1,0:T(8,128)(2,1)}, u32[]{:S(2)}) copy-start(bf16[1024,1024]{1,0:T(8,128)(2,1)} %projection_ref.1) | copy-start | bytes 6291460
  206.5 51.5 %copy-start.7 = (s32[4]{0:T(128)S(1)}, s32[4]{0:T(128)}, u32[]{:S(2)}) copy-start(s32[4]{0:T(128)} %neg_row_ref.3) | copy-start | bytes 52
Sparse Core Ops, SparseCore 0:
  12.8 45.3 all-gather.2
  73.1 75.4 reduce-scatter.1

commit v10 on v9

--- a/solution.py
+++ b/solution.py
@@ -96,23 +96,25 @@
     line_ref[...] = packed
     ny, nc, nz, part, rest, coefs = decode(packed, 1)
     column = jnp.where(nz == where_ref[0], (ny * C + nc) * OWN + part * BLOCK + rest, -1)
-    high, low = column >> 8, column & 255
-    lanes = lax.broadcasted_iota(jnp.int32, (rows, 256), 1)
-    chunks = WIDE // 256
-    totals = [jnp.zeros((rows, 256), bf16) for _ in range(chunks)]
-    nothing = jnp.zeros((rows, 256), bf16)
-    for slot in range(slots):
-        weight = coefs[:, slot : slot + 1] if slot > 2 else 1.0
-        hot = jnp.where(lanes == low[:, slot : slot + 1], weight, 0.0).astype(bf16)
-        level = jnp.broadcast_to(high[:, slot : slot + 1].astype(f32), (rows, 256)).astype(bf16)
-        for k in range(chunks):
-            term = jnp.where(level == k, hot, nothing)
-            if slot == 1 or slot == 2:
-                out_ref[slot, :, k * 256 : (k + 1) * 256] = term
-            else:
-                totals[k] = totals[k] + term
-    for k in range(chunks):
-        out_ref[0, :, k * 256 : (k + 1) * 256] = totals[k]
+    filler = jnp.full((rows, 128 - slots), -1, jnp.int32)
+    names = jnp.concatenate([column, filler], axis=1)
+    place = lax.broadcasted_iota(jnp.int32, (rows, slots), 1)
+    weights = jnp.where(place == 0, 1.0, jnp.where(place > 2, coefs, 0.0))
+    weights = jnp.concatenate([weights, filler.astype(f32) * 0.0], axis=1)
+    merged = weights
+    for shift in range(1, slots):
+        same = pltpu.roll(names, shift, 1) == names
+        merged = merged + jnp.where(same, pltpu.roll(weights, shift, 1), 0.0)
+    chunk = WIDE // 3
+    for k in range(3):
+        lanes = lax.broadcasted_iota(jnp.int32, (rows, chunk), 1) + k * chunk
+        total = jnp.where(lanes == names[:, 0:1], merged[:, 0:1], 0.0)
+        for slot in range(3, slots):
+            total = jnp.where(lanes == names[:, slot : slot + 1], merged[:, slot : slot + 1], total)
+        span = pl.ds(k * chunk, chunk)
+        out_ref[0, :, span] = total.astype(bf16)
+        out_ref[1, :, span] = jnp.where(lanes == names[:, 1:2], 1.0, 0.0).astype(bf16)
+        out_ref[2, :, span] = jnp.where(lanes == names[:, 2:3], 1.0, 0.0).astype(bf16)
 
 
 def node_weights_kernel(where_ref, line_ref, out_ref):

time: 269 us -> 268 us (level)
  Pallas kernels: 41.8 us -> 45.2 us
  waiting for transfers between devices: 56.7 us -> 53.5 us
    pallas_call x1, Pallas kernels: 12.1 us -> 15.5 us  [on_device(): call(spread_kernel, (jax.ShapeDtypeStruct((3, line_count, WIDE), bf16), j...]
    reduce_scatter x1, waiting for transfers between devices: 39 us -> 35.7 us  [on_device(): lax.psum_scatter(part.reshape(3, line_count, embed_width), 'z', scatter_d...]
  transfers between devices with their start and end apart: 6 -> 6, of which waited for: 2 -> 2; matrix products, arithmetic and copies ran while one was open for 3% -> 3% of each run, Pallas kernels for 10% -> 11%
where the time goes in v10:
time: 268 us; the launch traced here: 267 us
  blocking collectives  107 us (40%)
  waiting for transfers between devices  53.5 us (20%)
  Pallas kernels  45.2 us (17%)
  starting transfers between devices  21.9 us (8%)
  between operations  13.7 us (5%)
  local copies, waits for them, and re-layouts  12.9 us (5%)
  matrix products  12.2 us (5%)
    all_gather x1, blocking collectives, on_device(): lax.all_gather(payload.astype(f16), 'z', axis=0, tiled=True).astype(bf16)  43 us
    all_to_all x1, blocking collectives, on_device(): lax.all_to_all(node_grads, ('x', 'y'), split_axis=0, concat_axis=0, tiled...  37.2 us
    reduce_scatter x1, waiting for transfers between devices, on_device(): lax.psum_scatter(part.reshape(3, line_count, embed_width), 'z', scatter_d...  35.7 us
    all_to_all x1, waiting for transfers between devices, on_device(): lax.all_to_all(copies, 'z', split_axis=0, concat_axis=0, tiled=True)  17.7 us
    pallas_call x1, Pallas kernels, on_device(): call(spread_kernel, (jax.ShapeDtypeStruct((3, line_count, WIDE), bf16), j...  15.5 us
    all_to_all x1, starting transfers between devices, on_device(): lax.all_to_all(copies, 'z', split_axis=0, concat_axis=0, tiled=True)  15.2 us
    all_gather x1, blocking collectives, on_device(): all_pre_grad = lax.all_gather(pre_grad, 'x', axis=0, tiled=True)  13.6 us
    all_gather x1, blocking collectives, on_device(): some_neg = lax.all_gather(line_neg, 'y', axis=0, tiled=True)  13.1 us
  transfers between devices with their start and end apart: 6, of which 2 were waited for; matrix products, arithmetic and copies ran while one was open for 3% of the time, Pallas kernels for 11%

profile of v10, /device:TPU:8, one launch (start us, length us, event | category | flops | bytes accessed | tf_op | source)
XLA Modules:
  0.0 267.3 jit_solution(14065062950840497409)
XLA Ops:
  6.5 0.0 copy-start.10
  6.5 0.0 copy-start.11
  6.5 0.0 copy-start.12
  6.5 0.0 all-gather.3.cloned.1.call-start
  6.5 6.1 %shard_map.64 = (f32[288,1024]{1,0:T(8,128)}, bf16[288,1024]{1,0:T(8,128)(2,1)}, bf16[8,1024]{1,0:T(8,128)(2,1)}) custom-call(s32[4]{0:T(128)} %neg_row_ref.3, bf16[256,1024]{1,0:T(8,128)(2,1)} %table_hbm.1, bf16[1024,1024]{1,0:T(8,128)(2,1)} %projection_ref.1), custom_call_target="tpu_custom_call" | custom-call | flops 603979776 | bytes 5242880 | tf_op jit(solution)/shard_map/pallas_call | solution.py:251
  12.6 0.0 all-gather.3.cloned.1.call-update
  12.6 0.0 copy-done.10
  12.7 0.0 copy-done.11
  12.7 0.0 copy-done.12
  12.7 0.1 copy.26
  12.8 0.7 slice.9
  13.6 0.7 broadcast_in_dim.3
  14.3 15.2 %all-to-all-start = ((bf16[16,8,1024]{2,1,0:T(8,128)(2,1)}), bf16[16,8,1024]{2,1,0:T(8,128)(2,1)S(1)}, u32[]{:S(2)}, u32[]{:S(2)}) async-start(bf16[16,8,1024]{2,1,0:T(8,128)(2,1)} %broadcast_in_dim.3), calls=%async_computation | async-start | bytes 524288 | tf_op jit(solution)/shard_map/all_to_all | solution.py:278
  29.5 0.0 reduce-scatter.2.cloned.1.call-start
  29.5 0.6 pad_add_fusion.where_ref
  30.1 17.7 %all-to-all-done.received_ref = bf16[16,8,1024]{2,1,0:T(8,128)(2,1)S(1)} async-done(((bf16[16,8,1024]{2,1,0:T(8,128)(2,1)}), bf16[16,8,1024]{2,1,0:T(8,128)(2,1)S(1)}, u32[]{:S(2)}, u32[]{:S(2)}) %all-to-all-start) | async-done | bytes 262176 | tf_op jit(solution)/shard_map/all_to_all | solution.py:278
  47.9 0.0 copy-start.8
  48.0 0.6 copy-done.8
  48.6 15.5 %shard_map.65 = (bf16[3,512,2304]{2,1,0:T(8,128)(2,1)}, s32[512,16]{1,0:T(8,128)}) custom-call(s32[2]{0:T(128)} %pad_add_fusion.where_ref, bf16[16,8,1024]{2,1,0:T(8,128)(2,1)} %copy-done.8), custom_call_target="tpu_custom_call" | custom-call | flops 56623104 | bytes 7077888 | tf_op jit(solution)/shard_map/pallas_call | solution.py:280
  64.1 0.0 all-gather.3.cloned.1.call-done
  64.1 12.2 %convolution_convert_fusion = bf16[1536,1024]{1,0:T(8,128)(2,1)} fusion(bf16[1536,2304]{1,0:T(8,128)(2,1)} %bitcast.37, bf16[2304,1024]{1,0:T(8,128)(2,1)} %all-gather.3.cloned.1.call-done), kind=kOutput, calls=%fused_computation | convolution fusion | flops 7249330176 | bytes 14942208 | tf_op jit(solution)/shard_map/dot_general | solution.py:45
  76.3 0.0 copy-start.9
  76.3 0.0 reduce-scatter.2.cloned.1.call-update
  76.4 13.1 %all_gather.13.neg_a_ref = bf16[256,1024]{1,0:T(8,128)(2,1)S(1)} all-gather(bf16[64,1024]{1,0:T(8,128)(2,1)S(1)} %reshape.33), channel_id=1, replica_groups=mesh['y'=4,'z'=16,'c'=2,'x'=4] {'y'}, dimensions={0}, use_global_device_ids=true | all-gather | bytes 655360 | tf_op jit(solution)/shard_map/all_gather | solution.py:306
  89.5 1.9 collective-permute-start.1
  91.4 1.0 constant_dynamic-slice_fusion.pre_ref
  92.4 0.0 copy-done.9
  92.4 0.1 copy.22
  92.5 2.6 collective-permute-start
  95.1 1.9 constant_dynamic-slice_fusion.1
  97.1 1.8 copy.28
  98.9 0.0 copy-start.6
  98.9 1.3 copy.25
  100.3 0.0 copy-done.6
  100.3 4.6 %shard_map.66.refs_0_ = bf16[3,1152,512]{2,1,0:T(8,128)(2,1)S(1)} custom-call(s32[2]{0:T(128)S(1)} %copy-done.6, s32[16,512]{1,0:T(8,128)S(1)} %bitcast.29), custom_call_target="tpu_custom_call" | custom-call | flops 28311552 | bytes 3538944 | tf_op jit(solution)/shard_map/pallas_call | solution.py:311
  104.9 0.0 copy-start
  104.9 1.8 copy-done
  106.7 0.0 collective-permute-done
  106.7 4.6 %shard_map.67.refs_0_ = bf16[3,1152,512]{2,1,0:T(8,128)(2,1)S(1)} custom-call(s32[2]{0:T(128)S(1)} %copy-done.6, s32[16,512]{1,0:T(8,128)S(1)} %bitcast.30), custom_call_target="tpu_custom_call" | custom-call | flops 28311552 | bytes 3538944 | tf_op jit(solution)/shard_map/pallas_call | solution.py:311
  111.3 0.0 copy-start.2
  111.3 1.8 copy-done.2
  113.0 0.0 collective-permute-done.1.neg_b_ref
  113.0 35.7 %reduce-scatter.2.cloned.1.call-done.got_ref = bf16[3,32,1024]{2,1,0:T(8,128)(2,1)} async-done(((bf16[3,512,1024]{2,1,0:T(8,128)(2,1)}), bf16[3,32,1024]{2,1,0:T(8,128)(2,1)}) %reduce-scatter.2.cloned.1.call-update) | async-done | bytes 196624 | tf_op jit(solution)/shard_map/reduce_scatter | solution.py:298
  148.8 0.0 copy-start.5
  148.8 0.9 copy-done.5
  149.7 1.9 shard_map.68
  151.6 0.0 copy-start.1
  151.6 43.0 %all-gather.4 = f16[512,2176]{1,0:T(8,128)(2,1)S(1)} all-gather(f16[32,2176]{1,0:T(8,128)(2,1)S(1)} %convert_element_type.13), channel_id=1, replica_groups=mesh['y'=4,'z'=16,'c'=2,'x'=4] {'z'}, dimensions={0}, use_global_device_ids=true | all-gather | bytes 2367488 | tf_op jit(solution)/shard_map/all_gather | solution.py:337
  194.6 0.3 convert_element_type.14.refs_1_
  194.8 0.0 copy-start.3
  194.8 2.2 collective-permute-start.2
  197.0 0.0 copy-done.1
  197.0 4.6 %shard_map.69.refs_4_ = f32[1152,1024]{1,0:T(8,128)S(1)} custom-call(bf16[3,1152,512]{2,1,0:T(8,128)(2,1)S(1)} %copy-done.1, bf16[512,2176]{1,0:T(8,128)(2,1)S(1)} %convert_element_type.14.refs_1_, bf16[1152,1024]{1,0:T(8,128)(2,1)S(1)} %bitcast.26, bf16[16,1024]{1,0:T(8,128)(2,1)S(1)} %reshape_squeeze.3.refs_3_), custom_call_target="tpu_custom_call" | custom-call | flops 2415919104 | bytes 10485760 | tf_op jit(solution)/shard_map/pallas_call | solution.py:343
  201.6 0.0 collective-permute-done.2.refs_1_
  201.6 0.0 copy-done.3
  201.6 4.7 %shard_map.70 = bf16[1152,1024]{1,0:T(8,128)(2,1)S(1)} custom-call(bf16[3,1152,512]{2,1,0:T(8,128)(2,1)S(1)} %copy-done.3, bf16[512,2176]{1,0:T(8,128)(2,1)S(1)} %collective-permute-done.2.refs_1_, bf16[1152,1024]{1,0:T(8,128)(2,1)S(1)} %bitcast.27, bf16[16,1024]{1,0:T(8,128)(2,1)S(1)} %reshape_squeeze.3.refs_3_, f32[1152,1024]{1,0:T(8,128)S(1)} %shard_map.69.refs_4_), custom_call_target="tpu_custom_call" | custom-call | flops 2415919104 | bytes 10485760 | tf_op jit(solution)/shard_map/pallas_call | solution.py:343
  206.4 0.0 copy-start.4
  206.4 0.0 copy-start.7
  206.4 37.2 %all_to_all.14.pieces_ref = bf16[16,72,1024]{2,1,0:T(8,128)(2,1)S(1)} all-to-all(bf16[16,72,1024]{2,1,0:T(8,128)(2,1)S(1)} %bitcast.28), channel_id=1, replica_groups=mesh['y'=4,'z'=16,'c'=2,'x'=4] {'x','y'}, dimensions={0} | all-to-all | bytes 4718592 | tf_op jit(solution)/shard_map/all_to_all | solution.py:363
  243.6 0.5 shard_map.71
  244.1 13.6 %all_gather.15.grad_ref = bf16[288,1024]{1,0:T(8,128)(2,1)S(1)} all-gather(bf16[72,1024]{1,0:T(8,128)(2,1)S(1)} %shard_map.71), channel_id=1, replica_groups=mesh['y'=4,'z'=16,'c'=2,'x'=4] {'x'}, dimensions={0}, use_global_device_ids=true | all-gather | bytes 737280 | tf_op jit(solution)/shard_map/all_gather | solution.py:373
  257.8 0.0 copy-done.4
  257.8 0.0 copy-done.7
  257.8 2.7 %shard_map.72 = f32[256,1024]{1,0:T(8,128)} custom-call(s32[4]{0:T(128)S(1)} %copy-done.7, bf16[288,1024]{1,0:T(8,128)(2,1)S(1)} %all_gather.15.grad_ref, bf16[1024,1024]{1,0:T(8,128)(2,1)S(1)} %copy-done.4), custom_call_target="tpu_custom_call" | custom-call | flops 603979776 | bytes 4194304 | tf_op jit(solution)/shard_map/pallas_call | solution.py:374
  (11 shorter events, 0.2 us)
Async XLA Ops:
  6.5 6.1 %copy-start.10 = (s32[32,16]{0,1:T(8,128)S(1)}, s32[32,16]{0,1:T(8,128)}, u32[]{:S(2)}) copy-start(s32[32,16]{0,1:T(8,128)} %param.9) | copy-start | bytes 6148
  6.5 6.1 %copy-start.11 = (s32[32,13]{0,1:T(8,128)S(1)}, s32[32,13]{0,1:T(8,128)}, u32[]{:S(2)}) copy-start(s32[32,13]{0,1:T(8,128)} %param.10) | copy-start | bytes 4996
  6.5 6.1 %copy-start.12 = (s32[32,16,1]{0,2,1:T(1,128)S(1)}, s32[32,16,1]{0,2,1:T(1,128)}, u32[]{:S(2)}) copy-start(s32[32,16,1]{0,2,1:T(1,128)} %param.8) | copy-start | bytes 6148
  6.5 57.6 %all-gather.3.cloned.1.call-start = ((), (), s32[]{:S(2)}) async-start(), calls=%async_computation.3 | async-start | bytes 5308416 | tf_op jit(solution)/shard_map/all_gather | solution.py:269
  14.3 33.6 %all-to-all-start = ((bf16[16,8,1024]{2,1,0:T(8,128)(2,1)}), bf16[16,8,1024]{2,1,0:T(8,128)(2,1)S(1)}, u32[]{:S(2)}, u32[]{:S(2)}) async-start(bf16[16,8,1024]{2,1,0:T(8,128)(2,1)} %broadcast_in_dim.3), calls=%async_computation | async-start | bytes 524288 | tf_op jit(solution)/shard_map/all_to_all | solution.py:278
  29.5 119.3 %reduce-scatter.2.cloned.1.call-start = ((), (), s32[]{:S(2)}) async-start(), calls=%async_computation.4 | async-start | bytes 3342336 | tf_op jit(solution)/shard_map/reduce_scatter | solution.py:298
  47.9 0.7 copy-start.8
  76.3 16.1 %copy-start.9 = (s32[512,16]{1,0:T(8,128)S(1)}, s32[512,16]{1,0:T(8,128)}, u32[]{:S(2)}) copy-start(s32[512,16]{1,0:T(8,128)} %get-tuple-element.27) | copy-start | bytes 98308
  89.5 23.5 %collective-permute-start.1 = (bf16[256,1024]{1,0:T(8,128)(2,1)S(1)}, bf16[256,1024]{1,0:T(8,128)(2,1)}, u32[]{:S(2)}, u32[]{:S(2)}) collective-permute-start(bf16[256,1024]{1,0:T(8,128)(2,1)S(1)} %all_gather.13.neg_a_ref), channel_id=1, source_target_pairs={{0,4},{4,0},{1,5},{5,1},{2,6},{6,2},{3,7},{7,3},{8,12},{12,8},{9,1... | collective-permute-start | bytes 1572872 | tf_op jit(solution)/shard_map/ppermute | solution.py:307
  92.5 14.1 %collective-permute-start = (s32[512,16]{0,1:T(8,128)S(1)}, s32[512,16]{0,1:T(8,128)S(1)}, u32[]{:S(2)}, u32[]{:S(2)}) collective-permute-start(s32[512,16]{0,1:T(8,128)S(1)} %copy.22), channel_id=1, source_target_pairs={{0,4},{4,0},{1,5},{5,1},{2,6},{6,2},{3,7},{7,3},{8,12},{12,8},{9,1... | collective-permute-start | bytes 98312 | tf_op jit(solution)/shard_map/ppermute | solution.py:308
  98.9 1.4 copy-start.6
  104.9 1.8 copy-start
  111.3 1.8 copy-start.2
  148.8 0.9 copy-start.5
  151.6 45.4 %copy-start.1 = (bf16[3,1152,512]{2,1,0:T(8,128)(2,1)S(1)}, bf16[3,1152,512]{2,1,0:T(8,128)(2,1)}, u32[]{:S(2)}) copy-start(bf16[3,1152,512]{2,1,0:T(8,128)(2,1)} %copy-done) | copy-start | bytes 10616836
  194.8 6.8 %copy-start.3 = (bf16[3,1152,512]{2,1,0:T(8,128)(2,1)S(1)}, bf16[3,1152,512]{2,1,0:T(8,128)(2,1)}, u32[]{:S(2)}) copy-start(bf16[3,1152,512]{2,1,0:T(8,128)(2,1)} %copy-done.2) | copy-start | bytes 10616836
  194.8 6.8 %collective-permute-start.2 = (bf16[512,2176]{1,0:T(8,128)(2,1)S(1)}, bf16[512,2176]{1,0:T(8,128)(2,1)S(1)}, u32[]{:S(2)}, u32[]{:S(2)}) collective-permute-start(bf16[512,2176]{1,0:T(8,128)(2,1)S(1)} %convert_element_type.14.refs_1_), channel_id=1, source_target_pairs={{0,4},{4,0},{1,5},{5,1},{2,6},{6,2},{3,7},{7,3},{8,12},{12,8},{9,1... | collective-permute-start | bytes 6684680 | tf_op jit(solution)/shard_map/ppermute | solution.py:338
  206.4 51.4 %copy-start.4 = (bf16[1024,1024]{1,0:T(8,128)(2,1)S(1)}, bf16[1024,1024]{1,0:T(8,128)(2,1)}, u32[]{:S(2)}) copy-start(bf16[1024,1024]{1,0:T(8,128)(2,1)} %projection_ref.1) | copy-start | bytes 6291460
  206.4 51.4 %copy-start.7 = (s32[4]{0:T(128)S(1)}, s32[4]{0:T(128)}, u32[]{:S(2)}) copy-start(s32[4]{0:T(128)} %neg_row_ref.3) | copy-start | bytes 52
Sparse Core Ops, SparseCore 0:
  12.8 45.3 all-gather.2
  76.5 72.2 reduce-scatter.1

commit v11 on v10

--- a/solution.py
+++ b/solution.py
@@ -96,25 +96,16 @@
     line_ref[...] = packed
     ny, nc, nz, part, rest, coefs = decode(packed, 1)
     column = jnp.where(nz == where_ref[0], (ny * C + nc) * OWN + part * BLOCK + rest, -1)
-    filler = jnp.full((rows, 128 - slots), -1, jnp.int32)
-    names = jnp.concatenate([column, filler], axis=1)
-    place = lax.broadcasted_iota(jnp.int32, (rows, slots), 1)
-    weights = jnp.where(place == 0, 1.0, jnp.where(place > 2, coefs, 0.0))
-    weights = jnp.concatenate([weights, filler.astype(f32) * 0.0], axis=1)
-    merged = weights
-    for shift in range(1, slots):
-        same = pltpu.roll(names, shift, 1) == names
-        merged = merged + jnp.where(same, pltpu.roll(weights, shift, 1), 0.0)
     chunk = WIDE // 3
     for k in range(3):
         lanes = lax.broadcasted_iota(jnp.int32, (rows, chunk), 1) + k * chunk
-        total = jnp.where(lanes == names[:, 0:1], merged[:, 0:1], 0.0)
+        total = jnp.where(lanes == column[:, 0:1], 1.0, 0.0)
         for slot in range(3, slots):
-            total = jnp.where(lanes == names[:, slot : slot + 1], merged[:, slot : slot + 1], total)
+            total = total + jnp.where(lanes == column[:, slot : slot + 1], coefs[:, slot : slot + 1], 0.0)
         span = pl.ds(k * chunk, chunk)
         out_ref[0, :, span] = total.astype(bf16)
-        out_ref[1, :, span] = jnp.where(lanes == names[:, 1:2], 1.0, 0.0).astype(bf16)
-        out_ref[2, :, span] = jnp.where(lanes == names[:, 2:3], 1.0, 0.0).astype(bf16)
+        out_ref[1, :, span] = jnp.where(lanes == column[:, 1:2], 1.0, 0.0).astype(bf16)
+        out_ref[2, :, span] = jnp.where(lanes == column[:, 2:3], 1.0, 0.0).astype(bf16)
 
 
 def node_weights_kernel(where_ref, line_ref, out_ref):

time: 268 us -> 268 us (level)
  the two profiles are of different devices: /device:TPU:8 before, /device:TPU:32 now
where the time goes in v11:
time: 268 us; the launch traced here: 267 us
  blocking collectives  108 us (40%)
  waiting for transfers between devices  53.2 us (20%)
  Pallas kernels  44.5 us (17%)
  starting transfers between devices  21.9 us (8%)
  between operations  13.7 us (5%)
  local copies, waits for them, and re-layouts  12.9 us (5%)
  matrix products  12.2 us (5%)
    all_gather x1, blocking collectives, on_device(): lax.all_gather(payload.astype(f16), 'z', axis=0, tiled=True).astype(bf16)  42.3 us
    all_to_all x1, blocking collectives, on_device(): lax.all_to_all(node_grads, ('x', 'y'), split_axis=0, concat_axis=0, tiled...  38.5 us
    reduce_scatter x1, waiting for transfers between devices, on_device(): lax.psum_scatter(part.reshape(3, line_count, embed_width), 'z', scatter_d...  35.9 us
    all_to_all x1, waiting for transfers between devices, on_device(): lax.all_to_all(copies, 'z', split_axis=0, concat_axis=0, tiled=True)  17.3 us
    all_to_all x1, starting transfers between devices, on_device(): lax.all_to_all(copies, 'z', split_axis=0, concat_axis=0, tiled=True)  15.2 us
    pallas_call x1, Pallas kernels, on_device(): call(spread_kernel, (jax.ShapeDtypeStruct((3, line_count, WIDE), bf16), j...  14.8 us
    all_gather x1, blocking collectives, on_device(): all_pre_grad = lax.all_gather(pre_grad, 'x', axis=0, tiled=True)  13.6 us
    all_gather x1, blocking collectives, on_device(): some_neg = lax.all_gather(line_neg, 'y', axis=0, tiled=True)  13.6 us
  transfers between devices with their start and end apart: 6, of which 2 were waited for; matrix products, arithmetic and copies ran while one was open for 3% of the time, Pallas kernels for 11%

profile of v11, /device:TPU:32, one launch (start us, length us, event | category | flops | bytes accessed | tf_op | source)
XLA Modules:
  0.0 267.4 jit_solution(18194109349749298272)
XLA Ops:
  6.5 0.0 copy-start.10
  6.5 0.0 copy-start.11
  6.5 0.0 copy-start.12
  6.5 0.0 all-gather.3.cloned.1.call-start
  6.5 6.1 %shard_map.64 = (f32[288,1024]{1,0:T(8,128)}, bf16[288,1024]{1,0:T(8,128)(2,1)}, bf16[8,1024]{1,0:T(8,128)(2,1)}) custom-call(s32[4]{0:T(128)} %neg_row_ref.3, bf16[256,1024]{1,0:T(8,128)(2,1)} %table_hbm.1, bf16[1024,1024]{1,0:T(8,128)(2,1)} %projection_ref.1), custom_call_target="tpu_custom_call" | custom-call | flops 603979776 | bytes 5242880 | tf_op jit(solution)/shard_map/pallas_call | solution.py:242
  12.6 0.0 all-gather.3.cloned.1.call-update
  12.6 0.0 copy-done.10
  12.7 0.0 copy-done.11
  12.7 0.0 copy-done.12
  12.7 0.1 copy.26
  12.8 0.7 slice.9
  13.6 0.7 broadcast_in_dim.3
  14.3 15.2 %all-to-all-start = ((bf16[16,8,1024]{2,1,0:T(8,128)(2,1)}), bf16[16,8,1024]{2,1,0:T(8,128)(2,1)S(1)}, u32[]{:S(2)}, u32[]{:S(2)}) async-start(bf16[16,8,1024]{2,1,0:T(8,128)(2,1)} %broadcast_in_dim.3), calls=%async_computation | async-start | bytes 524288 | tf_op jit(solution)/shard_map/all_to_all | solution.py:269
  29.5 0.0 reduce-scatter.2.cloned.1.call-start
  29.5 0.6 pad_add_fusion.where_ref
  30.1 17.3 %all-to-all-done.received_ref = bf16[16,8,1024]{2,1,0:T(8,128)(2,1)S(1)} async-done(((bf16[16,8,1024]{2,1,0:T(8,128)(2,1)}), bf16[16,8,1024]{2,1,0:T(8,128)(2,1)S(1)}, u32[]{:S(2)}, u32[]{:S(2)}) %all-to-all-start) | async-done | bytes 262176 | tf_op jit(solution)/shard_map/all_to_all | solution.py:269
  47.4 0.0 copy-start.8
  47.5 0.6 copy-done.8
  48.1 14.8 %shard_map.65 = (bf16[3,512,2304]{2,1,0:T(8,128)(2,1)}, s32[512,16]{1,0:T(8,128)}) custom-call(s32[2]{0:T(128)} %pad_add_fusion.where_ref, bf16[16,8,1024]{2,1,0:T(8,128)(2,1)} %copy-done.8), custom_call_target="tpu_custom_call" | custom-call | flops 56623104 | bytes 7077888 | tf_op jit(solution)/shard_map/pallas_call | solution.py:271
  63.0 0.0 all-gather.3.cloned.1.call-done
  63.0 12.2 %convolution_convert_fusion = bf16[1536,1024]{1,0:T(8,128)(2,1)} fusion(bf16[1536,2304]{1,0:T(8,128)(2,1)} %bitcast.37, bf16[2304,1024]{1,0:T(8,128)(2,1)} %all-gather.3.cloned.1.call-done), kind=kOutput, calls=%fused_computation | convolution fusion | flops 7249330176 | bytes 14942208 | tf_op jit(solution)/shard_map/dot_general | solution.py:45
  75.2 0.0 copy-start.9
  75.2 0.0 reduce-scatter.2.cloned.1.call-update
  75.2 13.6 %all_gather.13.neg_a_ref = bf16[256,1024]{1,0:T(8,128)(2,1)S(1)} all-gather(bf16[64,1024]{1,0:T(8,128)(2,1)S(1)} %reshape.33), channel_id=1, replica_groups=mesh['y'=4,'z'=16,'c'=2,'x'=4] {'y'}, dimensions={0}, use_global_device_ids=true | all-gather | bytes 655360 | tf_op jit(solution)/shard_map/all_gather | solution.py:297
  88.8 1.9 collective-permute-start.1
  90.7 1.0 constant_dynamic-slice_fusion.pre_ref
  91.7 0.0 copy-done.9
  91.7 0.1 copy.22
  91.8 2.6 collective-permute-start
  94.4 1.9 constant_dynamic-slice_fusion.1
  96.4 1.8 copy.28
  98.2 0.0 copy-start.6
  98.2 1.3 copy.25
  99.6 0.0 copy-done.6
  99.6 4.6 %shard_map.66.refs_0_ = bf16[3,1152,512]{2,1,0:T(8,128)(2,1)S(1)} custom-call(s32[2]{0:T(128)S(1)} %copy-done.6, s32[16,512]{1,0:T(8,128)S(1)} %bitcast.29), custom_call_target="tpu_custom_call" | custom-call | flops 28311552 | bytes 3538944 | tf_op jit(solution)/shard_map/pallas_call | solution.py:302
  104.2 0.0 copy-start
  104.2 1.8 copy-done
  106.0 0.0 collective-permute-done
  106.0 4.6 %shard_map.67.refs_0_ = bf16[3,1152,512]{2,1,0:T(8,128)(2,1)S(1)} custom-call(s32[2]{0:T(128)S(1)} %copy-done.6, s32[16,512]{1,0:T(8,128)S(1)} %bitcast.30), custom_call_target="tpu_custom_call" | custom-call | flops 28311552 | bytes 3538944 | tf_op jit(solution)/shard_map/pallas_call | solution.py:302
  110.6 0.0 copy-start.2
  110.6 1.8 copy-done.2
  112.3 0.0 collective-permute-done.1.neg_b_ref
  112.3 35.9 %reduce-scatter.2.cloned.1.call-done.got_ref = bf16[3,32,1024]{2,1,0:T(8,128)(2,1)} async-done(((bf16[3,512,1024]{2,1,0:T(8,128)(2,1)}), bf16[3,32,1024]{2,1,0:T(8,128)(2,1)}) %reduce-scatter.2.cloned.1.call-update) | async-done | bytes 196624 | tf_op jit(solution)/shard_map/reduce_scatter | solution.py:289
  148.2 0.0 copy-start.5
  148.2 0.9 copy-done.5
  149.1 1.9 shard_map.68
  151.0 0.0 copy-start.1
  151.0 42.3 %all-gather.4 = f16[512,2176]{1,0:T(8,128)(2,1)S(1)} all-gather(f16[32,2176]{1,0:T(8,128)(2,1)S(1)} %convert_element_type.13), channel_id=1, replica_groups=mesh['y'=4,'z'=16,'c'=2,'x'=4] {'z'}, dimensions={0}, use_global_device_ids=true | all-gather | bytes 2367488 | tf_op jit(solution)/shard_map/all_gather | solution.py:328
  193.3 0.3 convert_element_type.14.refs_1_
  193.6 0.0 copy-start.3
  193.6 2.2 collective-permute-start.2
  195.8 0.0 copy-done.1
  195.8 4.6 %shard_map.69.refs_4_ = f32[1152,1024]{1,0:T(8,128)S(1)} custom-call(bf16[3,1152,512]{2,1,0:T(8,128)(2,1)S(1)} %copy-done.1, bf16[512,2176]{1,0:T(8,128)(2,1)S(1)} %convert_element_type.14.refs_1_, bf16[1152,1024]{1,0:T(8,128)(2,1)S(1)} %bitcast.26, bf16[16,1024]{1,0:T(8,128)(2,1)S(1)} %reshape_squeeze.3.refs_3_), custom_call_target="tpu_custom_call" | custom-call | flops 2415919104 | bytes 10485760 | tf_op jit(solution)/shard_map/pallas_call | solution.py:334
  200.4 0.0 collective-permute-done.2.refs_1_
  200.4 0.0 copy-done.3
  200.4 4.7 %shard_map.70 = bf16[1152,1024]{1,0:T(8,128)(2,1)S(1)} custom-call(bf16[3,1152,512]{2,1,0:T(8,128)(2,1)S(1)} %copy-done.3, bf16[512,2176]{1,0:T(8,128)(2,1)S(1)} %collective-permute-done.2.refs_1_, bf16[1152,1024]{1,0:T(8,128)(2,1)S(1)} %bitcast.27, bf16[16,1024]{1,0:T(8,128)(2,1)S(1)} %reshape_squeeze.3.refs_3_, f32[1152,1024]{1,0:T(8,128)S(1)} %shard_map.69.refs_4_), custom_call_target="tpu_custom_call" | custom-call | flops 2415919104 | bytes 10485760 | tf_op jit(solution)/shard_map/pallas_call | solution.py:334
  205.1 0.0 copy-start.4
  205.1 0.0 copy-start.7
  205.1 38.5 %all_to_all.14.pieces_ref = bf16[16,72,1024]{2,1,0:T(8,128)(2,1)S(1)} all-to-all(bf16[16,72,1024]{2,1,0:T(8,128)(2,1)S(1)} %bitcast.28), channel_id=1, replica_groups=mesh['y'=4,'z'=16,'c'=2,'x'=4] {'x','y'}, dimensions={0} | all-to-all | bytes 4718592 | tf_op jit(solution)/shard_map/all_to_all | solution.py:354
  243.6 0.5 shard_map.71
  244.2 13.6 %all_gather.15.grad_ref = bf16[288,1024]{1,0:T(8,128)(2,1)S(1)} all-gather(bf16[72,1024]{1,0:T(8,128)(2,1)S(1)} %shard_map.71), channel_id=1, replica_groups=mesh['y'=4,'z'=16,'c'=2,'x'=4] {'x'}, dimensions={0}, use_global_device_ids=true | all-gather | bytes 737280 | tf_op jit(solution)/shard_map/all_gather | solution.py:364
  257.8 0.0 copy-done.4
  257.8 0.0 copy-done.7
  257.8 2.7 %shard_map.72 = f32[256,1024]{1,0:T(8,128)} custom-call(s32[4]{0:T(128)S(1)} %copy-done.7, bf16[288,1024]{1,0:T(8,128)(2,1)S(1)} %all_gather.15.grad_ref, bf16[1024,1024]{1,0:T(8,128)(2,1)S(1)} %copy-done.4), custom_call_target="tpu_custom_call" | custom-call | flops 603979776 | bytes 4194304 | tf_op jit(solution)/shard_map/pallas_call | solution.py:365
  (11 shorter events, 0.2 us)
Async XLA Ops:
  6.5 6.1 %copy-start.10 = (s32[32,16]{0,1:T(8,128)S(1)}, s32[32,16]{0,1:T(8,128)}, u32[]{:S(2)}) copy-start(s32[32,16]{0,1:T(8,128)} %param.9) | copy-start | bytes 6148
  6.5 6.1 %copy-start.11 = (s32[32,13]{0,1:T(8,128)S(1)}, s32[32,13]{0,1:T(8,128)}, u32[]{:S(2)}) copy-start(s32[32,13]{0,1:T(8,128)} %param.10) | copy-start | bytes 4996
  6.5 6.1 %copy-start.12 = (s32[32,16,1]{0,2,1:T(1,128)S(1)}, s32[32,16,1]{0,2,1:T(1,128)}, u32[]{:S(2)}) copy-start(s32[32,16,1]{0,2,1:T(1,128)} %param.8) | copy-start | bytes 6148
  6.5 56.4 %all-gather.3.cloned.1.call-start = ((), (), s32[]{:S(2)}) async-start(), calls=%async_computation.3 | async-start | bytes 5308416 | tf_op jit(solution)/shard_map/all_gather | solution.py:260
  14.3 33.1 %all-to-all-start = ((bf16[16,8,1024]{2,1,0:T(8,128)(2,1)}), bf16[16,8,1024]{2,1,0:T(8,128)(2,1)S(1)}, u32[]{:S(2)}, u32[]{:S(2)}) async-start(bf16[16,8,1024]{2,1,0:T(8,128)(2,1)} %broadcast_in_dim.3), calls=%async_computation | async-start | bytes 524288 | tf_op jit(solution)/shard_map/all_to_all | solution.py:269
  29.5 118.7 %reduce-scatter.2.cloned.1.call-start = ((), (), s32[]{:S(2)}) async-start(), calls=%async_computation.4 | async-start | bytes 3342336 | tf_op jit(solution)/shard_map/reduce_scatter | solution.py:289
  47.4 0.7 copy-start.8
  75.2 16.6 %copy-start.9 = (s32[512,16]{1,0:T(8,128)S(1)}, s32[512,16]{1,0:T(8,128)}, u32[]{:S(2)}) copy-start(s32[512,16]{1,0:T(8,128)} %get-tuple-element.27) | copy-start | bytes 98308
  88.8 23.5 %collective-permute-start.1 = (bf16[256,1024]{1,0:T(8,128)(2,1)S(1)}, bf16[256,1024]{1,0:T(8,128)(2,1)}, u32[]{:S(2)}, u32[]{:S(2)}) collective-permute-start(bf16[256,1024]{1,0:T(8,128)(2,1)S(1)} %all_gather.13.neg_a_ref), channel_id=1, source_target_pairs={{0,4},{4,0},{1,5},{5,1},{2,6},{6,2},{3,7},{7,3},{8,12},{12,8},{9,1... | collective-permute-start | bytes 1572872 | tf_op jit(solution)/shard_map/ppermute | solution.py:298
  91.8 14.1 %collective-permute-start = (s32[512,16]{0,1:T(8,128)S(1)}, s32[512,16]{0,1:T(8,128)S(1)}, u32[]{:S(2)}, u32[]{:S(2)}) collective-permute-start(s32[512,16]{0,1:T(8,128)S(1)} %copy.22), channel_id=1, source_target_pairs={{0,4},{4,0},{1,5},{5,1},{2,6},{6,2},{3,7},{7,3},{8,12},{12,8},{9,1... | collective-permute-start | bytes 98312 | tf_op jit(solution)/shard_map/ppermute | solution.py:299
  98.2 1.4 copy-start.6
  104.2 1.8 copy-start
  110.6 1.8 copy-start.2
  148.2 0.9 copy-start.5
  151.0 44.8 %copy-start.1 = (bf16[3,1152,512]{2,1,0:T(8,128)(2,1)S(1)}, bf16[3,1152,512]{2,1,0:T(8,128)(2,1)}, u32[]{:S(2)}) copy-start(bf16[3,1152,512]{2,1,0:T(8,128)(2,1)} %copy-done) | copy-start | bytes 10616836
  193.6 6.8 %copy-start.3 = (bf16[3,1152,512]{2,1,0:T(8,128)(2,1)S(1)}, bf16[3,1152,512]{2,1,0:T(8,128)(2,1)}, u32[]{:S(2)}) copy-start(bf16[3,1152,512]{2,1,0:T(8,128)(2,1)} %copy-done.2) | copy-start | bytes 10616836
  193.6 6.8 %collective-permute-start.2 = (bf16[512,2176]{1,0:T(8,128)(2,1)S(1)}, bf16[512,2176]{1,0:T(8,128)(2,1)S(1)}, u32[]{:S(2)}, u32[]{:S(2)}) collective-permute-start(bf16[512,2176]{1,0:T(8,128)(2,1)S(1)} %convert_element_type.14.refs_1_), channel_id=1, source_target_pairs={{0,4},{4,0},{1,5},{5,1},{2,6},{6,2},{3,7},{7,3},{8,12},{12,8},{9,1... | collective-permute-start | bytes 6684680 | tf_op jit(solution)/shard_map/ppermute | solution.py:329
  205.1 52.7 %copy-start.4 = (bf16[1024,1024]{1,0:T(8,128)(2,1)S(1)}, bf16[1024,1024]{1,0:T(8,128)(2,1)}, u32[]{:S(2)}) copy-start(bf16[1024,1024]{1,0:T(8,128)(2,1)} %projection_ref.1) | copy-start | bytes 6291460
  205.1 52.7 %copy-start.7 = (s32[4]{0:T(128)S(1)}, s32[4]{0:T(128)}, u32[]{:S(2)}) copy-start(s32[4]{0:T(128)} %neg_row_ref.3) | copy-start | bytes 52
Sparse Core Ops, SparseCore 0:
  12.8 46.0 all-gather.2
  75.3 72.7 reduce-scatter.1
